TPU v7x, 32 devices: a whole 2x2x4 slice. The times are simulated.
32 devices in a mesh: groups: 2 (over x), tp: 8 (over z, y), sp: 2 (over core).
Axes of the slice: x: 2, y: 2, z: 4, core: 2. Of those that a mesh axis runs over, the one named last changes fastest.
Arguments:
- tokens: bfloat16 [1536, 4608], P(('groups', 'tp', 'sp')), parts along dimension 0, may hold values from -48 to 48
- w_query: bfloat16 [4608, 1024], P(None, 'tp'), may hold values from -0.09375 to 0.09375
- w_key: bfloat16 [4608, 512], P(None, 'tp'), may hold values from -0.09375 to 0.09375
- w_value: bfloat16 [4608, 512], P(None, 'tp'), may hold values from -0.09375 to 0.09375
- w_out: bfloat16 [1024, 4608], P('tp'), may hold values from -0.5 to 0.5
- doc_lengths: int32 [16], P('groups'), parts along dimension 0, may hold values from 1 to 192, 768 in all
Outputs:
- attn_out: bfloat16 [1536, 4608], P(('groups', 'tp', 'sp')), parts along dimension 0
There are 2 independent parts, one for each index of `groups`. A program takes and returns all parts, laid end to end along the dimension named above; an argument that names none is the same for every part. Nothing has to cross between parts.
Inputs may be any that keep to these rules, and one draw needn't show every extreme that they name: `doc_lengths`: positive lengths that sum to 768; the largest is exactly a quarter of 768.
All inputs are finite; a program needn't handle non-finite values.
Results may differ from a plain program's by a relative error of at most 0.024.
Values may be sent and summed in bfloat16 or wider, within the bound.
No kernel may reach another device: no remote copies, remote signals or barrier semaphores. Data moves between devices by JAX's collectives and lax.ppermute only.
A program may use at most 128 MiB of HBM per device.

v0:
```python
import jax
import jax.numpy as jnp
import numpy as np
from jax import lax
from jax.experimental import pallas as pl
from jax.experimental.pallas import tpu as pltpu
from jax.sharding import PartitionSpec as P

PRE_SCALE = 144

masked_low = -1e30


def swap_tp(block, flip, only=None):
    count = lax.axis_size("tp")
    route = [(t, t ^ flip) for t in range(count) if only is None or only(t)]
    return lax.ppermute(block, "tp", route)


def swap_sp(block):
    count = lax.axis_size("sp")
    return lax.ppermute(block, "sp", [(s, s ^ 1) for s in range(count)])


def swap_by_core(block, flips, only=lambda t: True):
    count, cores = lax.axis_size("tp"), lax.axis_size("sp")
    route = [
        (t * cores + s, (t ^ flips[s]) * cores + s)
        for t in range(count)
        for s in range(cores)
        if only(t)
    ]
    return lax.ppermute(block, ("tp", "sp"), route)


def swap_in_slab(block, group_flip, tp_flip):
    groups = lax.axis_size("groups")
    count = lax.axis_size("tp")
    route = [
        (g * count + t, (g ^ group_flip) * count + (t ^ tp_flip))
        for g in range(groups)
        for t in range(count)
    ]
    return lax.ppermute(block, ("groups", "tp"), route)


def fence(*values):
    return lax.optimization_barrier(values)


def call(kernel, shapes, scalars, operands, scratch=(), outs=pltpu.VMEM, far=(), limit=16):
    size = sum(x.size * x.dtype.itemsize for x in operands)
    params = None
    if size < 8 << 20:
        operands = [pltpu.with_memory_space_constraint(x, pltpu.VMEM) for x in operands]
        params = pltpu.CompilerParams(vmem_limit_bytes=limit << 20)
    specs = [pl.BlockSpec(memory_space=pltpu.SMEM)] * len(scalars)
    specs += [pl.BlockSpec(memory_space=pltpu.VMEM)] * len(operands)
    specs += [pl.BlockSpec(memory_space=pl.ANY)] * len(far)
    return pl.pallas_call(
        kernel,
        in_specs=specs,
        out_specs=[pl.BlockSpec(memory_space=outs)] * len(shapes),
        out_shape=[jax.ShapeDtypeStruct(*shape) for shape in shapes],
        scratch_shapes=list(scratch),
        compiler_params=params,
    )(*scalars, *operands, *far)


def plain(a, w):
    return jnp.dot(a, w, preferred_element_type=jnp.float32)


def turned(a, w):
    return lax.dot_general(a, w, (((1,), (1,)), ((), ())), preferred_element_type=jnp.float32)


def rows_at(blocks, offset, size):
    parts = [block[:, pl.ds(pl.multiple_of(offset, 128), size)] for block in blocks]
    return jnp.concatenate(parts, axis=0) if len(parts) > 1 else parts[0]


def products(blocks, weights, sp, group):
    w_query, w_key, w_value, kv_came, kv_other, *quarters = weights
    rows = jnp.concatenate([block[...] for block in blocks], axis=0)
    own_query = plain(rows, w_query[...])
    own_kv = turned(rows, jnp.concatenate([w_key[...], w_value[...]], axis=0))
    size = quarters[0].shape[0]
    pair_query = None
    for i, weight in enumerate(quarters):
        at = (sp ^ (i >> 1)) * 2 + (group ^ (i & 1))
        term = plain(rows_at(blocks, at * size, size), weight[...])
        pair_query = term if pair_query is None else pair_query + term
    depth = kv_came.shape[1]
    pair_kv = turned(rows_at(blocks, sp * depth, depth), kv_came[...]) + turned(
        rows_at(blocks, (1 - sp) * depth, depth), kv_other[...]
    )
    return own_query, own_kv, pair_query, pair_kv


def early_kernel(flags, *refs):
    blocks, weights, out = refs[:-10], refs[-10:-1], refs[-1]
    head = weights[0].shape[1]
    for i, part in enumerate(products(blocks, weights, flags[0], flags[3])):
        out[:, i * head : (i + 1) * head] = part


def tail_kernel(flags, early, middle, relayed, cosine, sine_part, *refs):
    weights, (queries, key_value, last) = refs[:9], refs[9:]
    side, inner = flags[1], flags[2]
    head = weights[0].shape[1]
    half_head = head // 2
    last[...] = jnp.where(inner != 0, middle[...], relayed[...])
    late = products([last], weights, flags[0], flags[3])
    join = lambda i: jnp.concatenate([early[:, i * head : (i + 1) * head], late[i]], axis=0)
    own_query, own_kv, pair_query, pair_kv = [join(i) for i in range(4)]
    spin = lambda v: v * cosine[...] + pltpu.roll(v, half_head, 1) * sine_part[...]
    scale = PRE_SCALE ** (-0.5)
    count = own_query.shape[0]
    queries[:count] = (spin(own_query) * scale).astype(queries.dtype)
    queries[count:] = (spin(pair_query) * scale).astype(queries.dtype)
    lane = lax.broadcasted_iota(jnp.int32, own_kv.shape, 1)
    low = lane < half_head
    even = side == 0
    first = jnp.where(even, own_kv, pair_kv)
    second = jnp.where(even, pair_kv, own_kv)
    key_raw = jnp.where(low, first, pltpu.roll(second, half_head, 1))
    key_raw = key_raw.astype(jnp.bfloat16).astype(jnp.float32)
    key_value[:, :head] = spin(key_raw).astype(key_value.dtype)
    value = jnp.where(low, pltpu.roll(first, half_head, 1), second)
    key_value[:, head:] = value.astype(key_value.dtype)


def place_of(flags, index, flip_side, flip_core, slabs, rows, cores):
    block = jnp.zeros_like(index)
    for k in range(1, slabs):
        block = block + (index >= k * rows).astype(jnp.int32)
    at = (flags[5] ^ block) * 2 + (flags[1] ^ flip_side)
    return (at * cores + (flags[0] ^ flip_core)) * rows + index - block * rows


def tables_kernel(slabs, cores, flags, spread, cosine, sine_part):
    shape = cosine.shape
    index = lax.broadcasted_iota(jnp.int32, shape, 0)
    places = place_of(flags, index, 0, 0, slabs, shape[0] // slabs, cores)
    angles = places.astype(jnp.float32) * spread[...]
    cosine[...] = jnp.cos(angles)
    sines = jnp.sin(angles)
    low = lax.broadcasted_iota(jnp.int32, shape, 1) < shape[1] // 2
    sine_part[...] = jnp.where(low, -sines, sines)


def attend_kernel(slabs, cores, flags, lengths, queries, *refs):
    pieces, outs = refs[:4], refs[4:]
    count, head = pieces[0].shape[0], queries.shape[1]
    rows = count // slabs
    place = lambda shape, axis, a, b: place_of(
        flags, lax.broadcasted_iota(jnp.int32, shape, axis), a, b, slabs, rows, cores
    )
    end = 0
    ends = []
    for i in range(lengths.shape[0]):
        end = end + lengths[i]
        ends.append(end)
    step = min(count, 4 * rows)
    even = flags[1] == 0
    for at in range(0, count, step):
        index = at + lax.broadcasted_iota(jnp.int32, (step, 1), 0)
        query_places = place_of(flags, index, 0, 0, slabs, rows, cores)
        starts = jnp.zeros_like(query_places)
        for end in ends:
            starts = jnp.where(query_places >= end, end, starts)
        masks = []
        for c in range(4):
            key_places = place((1, count), 1, c % 2, c // 2)
            masks.append((key_places <= query_places) & (key_places >= starts))
        mixed = []
        for h in range(2):
            query = queries[h * count + at : h * count + at + step]
            scores = [
                jnp.where(mask, turned(query, piece[:, :head]), masked_low)
                for piece, mask in zip(pieces, masks)
            ]
            largest = scores[0]
            for part in scores[1:]:
                largest = jnp.maximum(largest, part)
            largest = jnp.max(largest, axis=1, keepdims=True)
            total, acc = 0.0, 0.0
            for part, piece, mask in zip(scores, pieces, masks):
                e = jnp.where(mask, jnp.exp(part - largest), 0.0)
                total = total + e
                acc = acc + plain(e.astype(jnp.bfloat16), piece[:, head:])
            total = jnp.sum(total, axis=1, keepdims=True)
            mixed.append((acc / total).astype(jnp.bfloat16))
        low = jnp.where(even, mixed[0], mixed[1])
        high = jnp.where(even, mixed[1], mixed[0])
        for k in range(step // rows):
            out = outs[at // rows + k]
            out[:, :head] = low[k * rows : (k + 1) * rows]
            out[:, head:] = high[k * rows : (k + 1) * rows]


def head_kernel(flags, came, other, w_out, out, sem):
    head, quarter = w_out.shape[0], out.shape[1]
    half_rows = came.shape[0]
    own = pl.ds(pl.multiple_of(flags[1] * head, head), head)
    columns = pl.ds(pl.multiple_of(flags[4] * quarter, 128), quarter)
    copy = pltpu.make_async_copy(w_out.at[:, columns], out.at[own], sem)
    copy.start()
    for i, piece in enumerate((came, other)):
        at = (1 - flags[1]) * head + (flags[0] ^ i) * half_rows
        out[pl.ds(pl.multiple_of(at, half_rows), half_rows)] = piece[...]
    copy.wait()


def project_kernel(peers, split, flags, *refs):
    stacked, pieces, outs = refs[:peers], list(refs[peers:-peers]), refs[-peers:]
    count, width = outs[0].shape
    rows = jnp.concatenate([m[...] for m in stacked], axis=0)
    step = 384 if width % 384 == 0 else width
    received = flags[2] != flags[0]
    for at in range(0, width, step):
        parts = [p[:, at : at + step] for p in pieces]
        if split:
            parts[-2:] = [jnp.where(received, parts[-2], parts[-1])]
        total = plain(rows, jnp.concatenate(parts, axis=0))
        for i, out in enumerate(outs):
            out[:, at : at + step] = total[i * count : (i + 1) * count].astype(out.dtype)


def assemble_kernel(flags, *refs):
    pieces, out, sems = refs[:-2], refs[-2], refs[-1]
    width = pieces[0].shape[1]
    copies = []
    for i, piece in enumerate(pieces):
        at = pl.multiple_of((flags[4] ^ i) * width, 128)
        copies.append(pltpu.make_async_copy(piece, out.at[:, pl.ds(at, width)], sems.at[i]))
        copies[-1].start()
    for copy in copies:
        copy.wait()


def local(tokens, w_query, w_key, w_value, w_out, doc_lengths):
    rows, width = tokens.shape
    tp_count = lax.axis_size("tp")
    sp_count = lax.axis_size("sp")
    sp_place = lax.axis_index("sp")
    tp_place = lax.axis_index("tp")
    group = lax.axis_index("groups") % 2
    slabs = tp_count // 2
    slab = tp_place // 2
    side = tp_place % 2
    head_dim = w_query.shape[1]
    short = slabs == 4
    is_inner = lambda t: (t >> 1) in (1, 2)

    if short:
        far = swap_tp(tokens, 4)
        near = swap_tp(tokens, 2)
        middle = swap_tp(tokens, 6, is_inner)
        relayed = swap_tp(far, 2, is_inner)
        firsts, last = [tokens, near, far], [middle, relayed]
    else:
        came = [swap_tp(tokens, 2 * k) for k in range(1, slabs)]
        firsts, last = [tokens] + came[:-1], [came[-1], came[-1]]

    depth = width // sp_count
    quarter = w_out.shape[1] // 4
    half_rows = head_dim // sp_count
    mine = group * 2 + side
    inner = ((slab == 1) | (slab == 2)).astype(jnp.int32)
    flags = jnp.stack([sp_place, side, inner, group, mine, slab]).astype(jnp.int32)
    turned_kv = [w_key.T, w_value.T]
    share_q = lax.dynamic_slice_in_dim(
        w_query, (sp_place * 2 + group) * (depth // 2), depth // 2, 0
    )
    share_kv = jnp.concatenate(
        [lax.dynamic_slice_in_dim(w, sp_place * depth, depth, 1) for w in turned_kv], axis=0
    )
    core_low = sp_place == 0
    sent_at = (sp_place * half_rows, (mine ^ 1) * quarter)
    share_q, share_kv, doc_lengths, w_out, flags, core_low, sent_at = fence(
        share_q, share_kv, doc_lengths, w_out, flags, core_low, sent_at
    )
    came_q = swap_tp(share_q, 1)
    cross_q = swap_in_slab(came_q, 1, 0)
    came_kv = swap_tp(share_kv, 1)
    out_sent = lax.dynamic_slice(w_out, sent_at, (half_rows, quarter))
    out_came = swap_tp(out_sent, 1)
    out_other = swap_sp(out_came)
    weights = [w_query, *turned_kv, came_kv, swap_sp(came_kv), came_q, cross_q]
    weights += [swap_sp(came_q), swap_sp(cross_q)]
    early = call(
        early_kernel, [((len(firsts) * rows, 4 * head_dim), jnp.float32)], [flags], firsts + weights
    )[0]

    in_order = lambda a, b, flag: [jnp.where(flag, a, b), jnp.where(flag, b, a)]
    out_own = call(
        head_kernel,
        [((2 * head_dim, quarter), jnp.bfloat16)],
        [flags],
        [out_came, out_other],
        [pltpu.SemaphoreType.DMA(())],
        far=[w_out],
    )[0]
    if short:
        out_first = swap_by_core(out_own, (2, 4))
        out_swapped = swap_sp(out_first)

    count = slabs * rows
    half_head = head_dim // 2
    powers = np.arange(head_dim, dtype=np.float32) % half_head * np.float32(2.0 / head_dim)
    spread = jnp.asarray(np.power(np.float32(10000.0), -powers)[None, :])
    tables = call(
        lambda *refs: tables_kernel(slabs, sp_count, *refs),
        [((count, head_dim), jnp.float32)] * 2,
        [flags],
        [spread],
    )
    queries, key_value = call(
        tail_kernel,
        [((2 * count, head_dim), jnp.bfloat16), ((count, 2 * head_dim), jnp.bfloat16)],
        [flags],
        [early, *last, *tables] + weights,
        [pltpu.VMEM((rows, width), jnp.bfloat16)],
    )

    beside = swap_tp(key_value, 1)
    every = [key_value, beside, swap_sp(key_value), swap_sp(beside)]
    mixed = call(
        lambda *refs: attend_kernel(slabs, sp_count, *refs),
        [((rows, 2 * head_dim), jnp.bfloat16)] * slabs,
        [flags, doc_lengths],
        [queries] + every,
        limit=16 if short else 56,
    )

    parts = [mixed[0]]
    for k in range(1, slabs):
        parts.append(swap_tp(mixed[k], 2 * k))
    if short:
        parts[1:3] = in_order(parts[1], parts[2], core_low)
    merged = jnp.concatenate(parts, axis=1)
    peers = ((0, 0), (0, 1), (1, 0), (1, 1))
    stacked = [merged] + [swap_in_slab(merged, g, t) for g, t in peers[1:]]
    if short:
        out_sent = jnp.where(core_low, out_own, out_first)
        out_last = swap_by_core(out_sent, (6, 2), is_inner)
        out_last, stacked[2] = fence(out_last, stacked[2])
        pieces = [out_own, out_first, out_swapped, out_last, swap_sp(out_last)]
    else:
        pieces = [out_own]
        mine_of = lax.dynamic_slice_in_dim(out_own, sp_place * head_dim, head_dim, 0)
        for k in range(1, slabs):
            piece = swap_tp(mine_of, 2 * k)
            both = in_order(piece, swap_sp(piece), core_low)
            pieces.append(jnp.concatenate(both, axis=0))
    outs = call(
        lambda *refs: project_kernel(len(peers), short, *refs),
        [((rows, quarter), jnp.bfloat16)] * len(peers),
        [flags],
        stacked + pieces,
    )
    outs = [outs[0]] + [swap_in_slab(o, g, t) for o, (g, t) in zip(outs[1:], peers[1:])]
    sems = [pltpu.SemaphoreType.DMA((len(outs),))]
    shape = ((rows, width), jnp.bfloat16)
    return call(assemble_kernel, [shape], [flags], outs, sems, pl.ANY)[0]


def solution(mesh):
    placed = (
        P(("groups", "tp", "sp"), None),
        P(None, "tp"),
        P(None, "tp"),
        P(None, "tp"),
        P("tp", None),
        P("groups"),
    )

    return jax.shard_map(
        local,
        mesh=mesh,
        in_specs=placed,
        out_specs=P(("groups", "tp", "sp"), None),
        check_vma=False,
    )
```

profile of v0, /device:TPU:0, one launch (start us, length us, event | category | flops | bytes accessed | tf_op | source)
XLA Modules:
  0.0 100.5 jit_solution(8771909214446426852)
XLA Ops:
  0.0 1.7 %constant_dynamic-slice_fusion = bf16[1152,128]{1,0:T(8,128)(2,1)} fusion(bf16[4608,128]{1,0:T(8,128)(2,1)} %refs_0_.3, s32[]{:T(128)S(6)} %select_n.49), kind=kLoop, calls=%fused_computation.7 | loop fusion | bytes 589828 | tf_op jit(solution)/shard_map/dynamic_slice | solution.py:274
  3.0 3.0 %collective-permute-start.2 = (bf16[128,2304]{1,0:T(8,128)(2,1)S(1)}, bf16[128,2304]{1,0:T(8,128)(2,1)S(1)}, u32[]{:S(2)}, u32[]{:S(2)}) collective-permute-start(bf16[128,2304]{1,0:T(8,128)(2,1)S(1)} %pad_maximum_fusion), channel_id=1, source_target_pairs={{0,2},{2,0},{4,6},{6,4},{8,10},{10,8},{12,14},{14,12},{1,3},{3,1},... | collective-permute-start | bytes 1769480 | tf_op jit(solution)/shard_map/ppermute | solution.py:17
  6.1 2.0 %collective-permute-start = (bf16[48,4608]{1,0:T(8,128)(2,1)S(1)}, bf16[48,4608]{1,0:T(8,128)(2,1)S(1)}, u32[]{:S(2)}, u32[]{:S(2)}) collective-permute-start(bf16[48,4608]{1,0:T(8,128)(2,1)S(1)} %copy-done.4), channel_id=1, source_target_pairs={{0,4},{2,6},{4,0},{6,2},{8,12},{10,14},{12,8},{14,10},{1,5},{3,7},... | collective-permute-start | bytes 1327112 | tf_op jit(solution)/shard_map/ppermute | solution.py:17
  8.3 1.6 %collective-permute-start.17 = (bf16[64,1152]{1,0:T(8,128)(2,1)S(1)}, bf16[64,1152]{1,0:T(8,128)(2,1)S(1)}, u32[]{:S(2)}, u32[]{:S(2)}) collective-permute-start(bf16[64,1152]{1,0:T(8,128)(2,1)S(1)} %dynamic_slice.15), channel_id=1, source_target_pairs={{0,2},{2,0},{4,6},{6,4},{8,10},{10,8},{12,14},{14,12},{1,3},{3,1},... | collective-permute-start | bytes 442376 | tf_op jit(solution)/shard_map/ppermute | solution.py:17
  9.9 2.6 %collective-permute-start.1 = (bf16[48,4608]{1,0:T(8,128)(2,1)S(1)}, bf16[48,4608]{1,0:T(8,128)(2,1)S(1)}, u32[]{:S(2)}, u32[]{:S(2)}) collective-permute-start(bf16[48,4608]{1,0:T(8,128)(2,1)S(1)} %copy-done.4), channel_id=1, source_target_pairs={{0,8},{2,10},{4,12},{6,14},{8,0},{10,2},{12,4},{14,6},{1,9},{3,11}... | collective-permute-start | bytes 1327112 | tf_op jit(solution)/shard_map/ppermute | solution.py:17
  12.5 16.4 %collective-permute-done.17.came = bf16[64,1152]{1,0:T(8,128)(2,1)S(1)} collective-permute-done((bf16[64,1152]{1,0:T(8,128)(2,1)S(1)}, bf16[64,1152]{1,0:T(8,128)(2,1)S(1)}, u32[]{:S(2)}, u32[]{:S(2)}) %collective-permute-start.17) | collective-permute-done | bytes 147488 | tf_op jit(solution)/shard_map/ppermute | solution.py:17
  28.9 1.7 %collective-permute-start.5 = (bf16[1152,128]{1,0:T(8,128)(2,1)S(1)}, bf16[1152,128]{1,0:T(8,128)(2,1)S(1)}, u32[]{:S(2)}, u32[]{:S(2)}) collective-permute-start(bf16[1152,128]{1,0:T(8,128)(2,1)S(1)} %collective-permute-done.4.refs_8_.refs_5_), channel_id=1, source_target_pairs={{0,16},{2,18},{4,20},{6,22},{8,24},{10,26},{12,28},{14,30},{16,0},... | collective-permute-start | bytes 884744 | tf_op jit(solution)/shard_map/ppermute | solution.py:44
  31.7 1.6 %collective-permute-start.19 = (bf16[256,1152]{1,0:T(8,128)(2,1)S(1)}, bf16[256,1152]{1,0:T(8,128)(2,1)S(1)}, u32[]{:S(2)}, u32[]{:S(2)}) collective-permute-start(bf16[256,1152]{1,0:T(8,128)(2,1)S(1)} %shard_map.77.refs_5_), channel_id=1, source_target_pairs={{0,4},{1,9},{2,6},{3,11},{4,0},{5,13},{6,2},{7,15},{8,12},{9,1},{1... | collective-permute-start | bytes 1769480 | tf_op jit(solution)/shard_map/ppermute | solution.py:33
  34.0 4.2 %collective-permute-done.5.refs_9_.refs_6_ = bf16[1152,128]{1,0:T(8,128)(2,1)S(1)} collective-permute-done((bf16[1152,128]{1,0:T(8,128)(2,1)S(1)}, bf16[1152,128]{1,0:T(8,128)(2,1)S(1)}, u32[]{:S(2)}, u32[]{:S(2)}) %collective-permute-start.5) | collective-permute-done | bytes 294944 | tf_op jit(solution)/shard_map/ppermute | solution.py:44
  41.2 2.2 %shard_map.73.early = f32[144,512]{1,0:T(8,128)S(1)} custom-call(s32[6]{0:T(128)S(1)} %stack.31.flags.refs_0_, bf16[48,4608]{1,0:T(8,128)(2,1)S(1)} %copy-done.4, bf16[48,4608]{1,0:T(8,128)(2,1)S(1)} %collective-permute-done.refs_1_, bf16[48,4608]{1,0:T(8,128)(2,1)S(1)} %collective-permute-done.1.refs_2_, bf16[4608,128]{1,0:T(8,128)(2,1)S(1)} %copy-done, ...), custom_call_target="tpu_custom_call" | custom-call | tf_op jit(solution)/shard_map/pallas_call | solution.py:60
  43.4 14.0 %collective-permute-done.9.relayed = bf16[48,4608]{1,0:T(8,128)(2,1)S(1)} collective-permute-done((bf16[48,4608]{1,0:T(8,128)(2,1)S(1)}, bf16[48,4608]{1,0:T(8,128)(2,1)S(1)}, u32[]{:S(2)}, u32[]{:S(2)}) %collective-permute-start.9) | collective-permute-done | bytes 442400 | tf_op jit(solution)/shard_map/ppermute | solution.py:17
  57.5 2.0 %shard_map.75 = (bf16[384,128]{1,0:T(8,128)(2,1)S(1)}, bf16[192,256]{1,0:T(8,128)(2,1)S(1)}) custom-call(s32[6]{0:T(128)S(1)} %stack.31.flags.refs_0_, f32[144,512]{1,0:T(8,128)S(1)} %shard_map.73.early, bf16[48,4608]{1,0:T(8,128)(2,1)S(1)} %collective-permute-done.8.middle, bf16[48,4608]{1,0:T(8,128)(2,1)S(1)} %collective-permute-done.9.relayed, ...), custom_call_target="tpu_custom_call" | custom-call | tf_op jit(solution)/shard_map/pallas_call | solution.py:60
  59.5 1.6 %collective-permute-start.10 = (bf16[192,256]{1,0:T(8,128)(2,1)S(1)}, bf16[192,256]{1,0:T(8,128)(2,1)S(1)}, u32[]{:S(2)}, u32[]{:S(2)}) collective-permute-start(bf16[192,256]{1,0:T(8,128)(2,1)S(1)} %get-tuple-element.34.refs_3_), channel_id=1, source_target_pairs={{0,2},{2,0},{4,6},{6,4},{8,10},{10,8},{12,14},{14,12},{1,3},{3,1},... | collective-permute-start | bytes 294920 | tf_op jit(solution)/shard_map/ppermute | solution.py:17
  61.9 2.2 %collective-permute-done.10.refs_4_ = bf16[192,256]{1,0:T(8,128)(2,1)S(1)} collective-permute-done((bf16[192,256]{1,0:T(8,128)(2,1)S(1)}, bf16[192,256]{1,0:T(8,128)(2,1)S(1)}, u32[]{:S(2)}, u32[]{:S(2)}) %collective-permute-start.10) | collective-permute-done | bytes 98336 | tf_op jit(solution)/shard_map/ppermute | solution.py:17
  65.5 1.8 %shard_map.76 = (bf16[48,256]{1,0:T(8,128)(2,1)S(1)}, bf16[48,256]{1,0:T(8,128)(2,1)S(1)}, bf16[48,256]{1,0:T(8,128)(2,1)S(1)}, bf16[48,256]{1,0:T(8,128)(2,1)S(1)}) custom-call(s32[6]{0:T(128)S(1)} %stack.31.flags.refs_0_, s32[8]{0:T(128)S(1)} %copy-done.5, bf16[384,128]{1,0:T(8,128)(2,1)S(1)} %get-tuple-element.33.refs_2_, ...), custom_call_target="tpu_custom_call" | custom-call | tf_op jit(solution)/shard_map/pallas_call | solution.py:60
  68.7 2.8 %collective-permute-start.14 = (bf16[48,256]{1,0:T(8,128)(2,1)S(1)}, bf16[48,256]{1,0:T(8,128)(2,1)S(1)}, u32[]{:S(2)}, u32[]{:S(2)}) collective-permute-start(bf16[48,256]{1,0:T(8,128)(2,1)S(1)} %get-tuple-element.38), channel_id=1, source_target_pairs={{0,8},{2,10},{4,12},{6,14},{8,0},{10,2},{12,4},{14,6},{1,9},{3,11}... | collective-permute-start | bytes 73736 | tf_op jit(solution)/shard_map/ppermute | solution.py:17
  71.7 2.0 %collective-permute-done.14 = bf16[48,256]{1,0:T(8,128)(2,1)S(1)} collective-permute-done((bf16[48,256]{1,0:T(8,128)(2,1)S(1)}, bf16[48,256]{1,0:T(8,128)(2,1)S(1)}, u32[]{:S(2)}, u32[]{:S(2)}) %collective-permute-start.14) | collective-permute-done | bytes 24608 | tf_op jit(solution)/shard_map/ppermute | solution.py:17
  73.7 3.4 %collective-permute-done.15 = bf16[48,256]{1,0:T(8,128)(2,1)S(1)} collective-permute-done((bf16[48,256]{1,0:T(8,128)(2,1)S(1)}, bf16[48,256]{1,0:T(8,128)(2,1)S(1)}, u32[]{:S(2)}, u32[]{:S(2)}) %collective-permute-start.15) | collective-permute-done | bytes 24608 | tf_op jit(solution)/shard_map/ppermute | solution.py:17
  78.6 3.2 %collective-permute-done.21.refs_3_ = bf16[48,1024]{1,0:T(8,128)(2,1)S(1)} collective-permute-done((bf16[48,1024]{1,0:T(8,128)(2,1)S(1)}, bf16[48,1024]{1,0:T(8,128)(2,1)S(1)}, u32[]{:S(2)}, u32[]{:S(2)}) %collective-permute-start.21) | collective-permute-done | bytes 98336 | tf_op jit(solution)/shard_map/ppermute | solution.py:44
  81.8 1.5 %collective-permute-start.16 = (bf16[48,1024]{1,0:T(8,128)(2,1)S(1)}, bf16[48,1024]{1,0:T(8,128)(2,1)S(1)}, u32[]{:S(2)}, u32[]{:S(2)}) collective-permute-start(bf16[48,1024]{1,0:T(8,128)(2,1)S(1)} %pad_maximum_fusion.1.refs_1_), channel_id=1, source_target_pairs={{0,2},{2,0},{4,6},{6,4},{8,10},{10,8},{12,14},{14,12},{16,18},{18,... | collective-permute-start | bytes 294920 | tf_op jit(solution)/shard_map/ppermute | solution.py:44
  84.7 3.5 %collective-permute-done.16.refs_2_ = bf16[48,1024]{1,0:T(8,128)(2,1)S(1)} collective-permute-done((bf16[48,1024]{1,0:T(8,128)(2,1)S(1)}, bf16[48,1024]{1,0:T(8,128)(2,1)S(1)}, u32[]{:S(2)}, u32[]{:S(2)}) %collective-permute-start.16) | collective-permute-done | bytes 98336 | tf_op jit(solution)/shard_map/ppermute | solution.py:44
  90.5 1.6 %collective-permute-start.25 = (bf16[48,1152]{1,0:T(8,128)(2,1)S(1)}, bf16[48,1152]{1,0:T(8,128)(2,1)S(1)}, u32[]{:S(2)}, u32[]{:S(2)}) collective-permute-start(bf16[48,1152]{1,0:T(8,128)(2,1)S(1)} %get-tuple-element.46), channel_id=1, source_target_pairs={{0,2},{2,0},{4,6},{6,4},{8,10},{10,8},{12,14},{14,12},{16,18},{18,... | collective-permute-start | bytes 331784 | tf_op jit(solution)/shard_map/ppermute | solution.py:44
  95.3 2.3 %collective-permute-done.26.refs_2_ = bf16[48,1152]{1,0:T(8,128)(2,1)S(1)} collective-permute-done((bf16[48,1152]{1,0:T(8,128)(2,1)S(1)}, bf16[48,1152]{1,0:T(8,128)(2,1)S(1)}, u32[]{:S(2)}, u32[]{:S(2)}) %collective-permute-start.26) | collective-permute-done | bytes 110624 | tf_op jit(solution)/shard_map/ppermute | solution.py:44
  97.6 1.6 %collective-permute-done.27.refs_3_ = bf16[48,1152]{1,0:T(8,128)(2,1)S(1)} collective-permute-done((bf16[48,1152]{1,0:T(8,128)(2,1)S(1)}, bf16[48,1152]{1,0:T(8,128)(2,1)S(1)}, u32[]{:S(2)}, u32[]{:S(2)}) %collective-permute-start.27) | collective-permute-done | bytes 110624 | tf_op jit(solution)/shard_map/ppermute | solution.py:44
  (61 shorter events, 19.8 us)
Async XLA Ops:
  3.0 27.8 %collective-permute-start.2 = (bf16[128,2304]{1,0:T(8,128)(2,1)S(1)}, bf16[128,2304]{1,0:T(8,128)(2,1)S(1)}, u32[]{:S(2)}, u32[]{:S(2)}) collective-permute-start(bf16[128,2304]{1,0:T(8,128)(2,1)S(1)} %pad_maximum_fusion), channel_id=1, source_target_pairs={{0,2},{2,0},{4,6},{6,4},{8,10},{10,8},{12,14},{14,12},{1,3},{3,1},... | collective-permute-start | bytes 1769480 | tf_op jit(solution)/shard_map/ppermute | solution.py:17
  6.0 22.8 %collective-permute-start.4 = (bf16[1152,128]{1,0:T(8,128)(2,1)}, bf16[1152,128]{1,0:T(8,128)(2,1)S(1)}, u32[]{:S(2)}, u32[]{:S(2)}) collective-permute-start(bf16[1152,128]{1,0:T(8,128)(2,1)} %constant_dynamic-slice_fusion), channel_id=1, source_target_pairs={{0,2},{2,0},{4,6},{6,4},{8,10},{10,8},{12,14},{14,12},{1,3},{3,1},... | collective-permute-start | bytes 884744 | tf_op jit(solution)/shard_map/ppermute | solution.py:17
  6.1 25.6 %collective-permute-start = (bf16[48,4608]{1,0:T(8,128)(2,1)S(1)}, bf16[48,4608]{1,0:T(8,128)(2,1)S(1)}, u32[]{:S(2)}, u32[]{:S(2)}) collective-permute-start(bf16[48,4608]{1,0:T(8,128)(2,1)S(1)} %copy-done.4), channel_id=1, source_target_pairs={{0,4},{2,6},{4,0},{6,2},{8,12},{10,14},{12,8},{14,10},{1,5},{3,7},... | collective-permute-start | bytes 1327112 | tf_op jit(solution)/shard_map/ppermute | solution.py:17
  8.3 20.6 %collective-permute-start.17 = (bf16[64,1152]{1,0:T(8,128)(2,1)S(1)}, bf16[64,1152]{1,0:T(8,128)(2,1)S(1)}, u32[]{:S(2)}, u32[]{:S(2)}) collective-permute-start(bf16[64,1152]{1,0:T(8,128)(2,1)S(1)} %dynamic_slice.15), channel_id=1, source_target_pairs={{0,2},{2,0},{4,6},{6,4},{8,10},{10,8},{12,14},{14,12},{1,3},{3,1},... | collective-permute-start | bytes 442376 | tf_op jit(solution)/shard_map/ppermute | solution.py:17
  9.9 23.5 %collective-permute-start.1 = (bf16[48,4608]{1,0:T(8,128)(2,1)S(1)}, bf16[48,4608]{1,0:T(8,128)(2,1)S(1)}, u32[]{:S(2)}, u32[]{:S(2)}) collective-permute-start(bf16[48,4608]{1,0:T(8,128)(2,1)S(1)} %copy-done.4), channel_id=1, source_target_pairs={{0,8},{2,10},{4,12},{6,14},{8,0},{10,2},{12,4},{14,6},{1,9},{3,11}... | collective-permute-start | bytes 1327112 | tf_op jit(solution)/shard_map/ppermute | solution.py:17
  28.9 9.4 %collective-permute-start.5 = (bf16[1152,128]{1,0:T(8,128)(2,1)S(1)}, bf16[1152,128]{1,0:T(8,128)(2,1)S(1)}, u32[]{:S(2)}, u32[]{:S(2)}) collective-permute-start(bf16[1152,128]{1,0:T(8,128)(2,1)S(1)} %collective-permute-done.4.refs_8_.refs_5_), channel_id=1, source_target_pairs={{0,16},{2,18},{4,20},{6,22},{8,24},{10,26},{12,28},{14,30},{16,0},... | collective-permute-start | bytes 884744 | tf_op jit(solution)/shard_map/ppermute | solution.py:44
  30.6 9.0 %collective-permute-start.6 = (bf16[1152,128]{1,0:T(8,128)(2,1)S(1)}, bf16[1152,128]{1,0:T(8,128)(2,1)S(1)}, u32[]{:S(2)}, u32[]{:S(2)}) collective-permute-start(bf16[1152,128]{1,0:T(8,128)(2,1)S(1)} %collective-permute-done.4.refs_8_.refs_5_), channel_id=1, source_target_pairs={{0,1},{1,0},{2,3},{3,2},{4,5},{5,4},{6,7},{7,6},{8,9},{9,8},{10,11... | collective-permute-start | bytes 884744 | tf_op jit(solution)/shard_map/ppermute | solution.py:22
  30.8 10.4 %collective-permute-start.3 = (bf16[128,2304]{1,0:T(8,128)(2,1)S(1)}, bf16[128,2304]{1,0:T(8,128)(2,1)S(1)}, u32[]{:S(2)}, u32[]{:S(2)}) collective-permute-start(bf16[128,2304]{1,0:T(8,128)(2,1)S(1)} %collective-permute-done.2.refs_6_.refs_3_), channel_id=1, source_target_pairs={{0,1},{1,0},{2,3},{3,2},{4,5},{5,4},{6,7},{7,6},{8,9},{9,8},{10,11... | collective-permute-start | bytes 1769480 | tf_op jit(solution)/shard_map/ppermute | solution.py:22
  31.7 29.3 %collective-permute-start.19 = (bf16[256,1152]{1,0:T(8,128)(2,1)S(1)}, bf16[256,1152]{1,0:T(8,128)(2,1)S(1)}, u32[]{:S(2)}, u32[]{:S(2)}) collective-permute-start(bf16[256,1152]{1,0:T(8,128)(2,1)S(1)} %shard_map.77.refs_5_), channel_id=1, source_target_pairs={{0,4},{1,9},{2,6},{3,11},{4,0},{5,13},{6,2},{7,15},{8,12},{9,1},{1... | collective-permute-start | bytes 1769480 | tf_op jit(solution)/shard_map/ppermute | solution.py:33
  33.4 10.0 %collective-permute-start.8 = (bf16[48,4608]{1,0:T(8,128)(2,1)S(1)}, bf16[48,4608]{1,0:T(8,128)(2,1)S(1)}, u32[]{:S(2)}, u32[]{:S(2)}) collective-permute-start(bf16[48,4608]{1,0:T(8,128)(2,1)S(1)} %copy-done.4), channel_id=1, source_target_pairs={{4,8},{6,10},{8,4},{10,6},{5,9},{7,11},{9,5},{11,7},{20,24},{22,26... | collective-permute-start | bytes 1327112 | tf_op jit(solution)/shard_map/ppermute | solution.py:17
  38.3 19.2 %collective-permute-start.9 = (bf16[48,4608]{1,0:T(8,128)(2,1)S(1)}, bf16[48,4608]{1,0:T(8,128)(2,1)S(1)}, u32[]{:S(2)}, u32[]{:S(2)}) collective-permute-start(bf16[48,4608]{1,0:T(8,128)(2,1)S(1)} %collective-permute-done.1.refs_2_), channel_id=1, source_target_pairs={{4,0},{6,2},{8,12},{10,14},{5,1},{7,3},{9,13},{11,15},{20,16},{22,... | collective-permute-start | bytes 1327112 | tf_op jit(solution)/shard_map/ppermute | solution.py:17
  59.5 4.7 %collective-permute-start.10 = (bf16[192,256]{1,0:T(8,128)(2,1)S(1)}, bf16[192,256]{1,0:T(8,128)(2,1)S(1)}, u32[]{:S(2)}, u32[]{:S(2)}) collective-permute-start(bf16[192,256]{1,0:T(8,128)(2,1)S(1)} %get-tuple-element.34.refs_3_), channel_id=1, source_target_pairs={{0,2},{2,0},{4,6},{6,4},{8,10},{10,8},{12,14},{14,12},{1,3},{3,1},... | collective-permute-start | bytes 294920 | tf_op jit(solution)/shard_map/ppermute | solution.py:17
  61.1 17.5 %collective-permute-start.20 = (bf16[256,1152]{1,0:T(8,128)(2,1)S(1)}, bf16[256,1152]{1,0:T(8,128)(2,1)S(1)}, u32[]{:S(2)}, u32[]{:S(2)}) collective-permute-start(bf16[256,1152]{1,0:T(8,128)(2,1)S(1)} %broadcast_select_fusion), channel_id=1, source_target_pairs={{4,8},{5,1},{6,10},{7,3},{8,4},{9,13},{10,6},{11,15},{20,24},{21,1... | collective-permute-start | bytes 1769480 | tf_op jit(solution)/shard_map/ppermute | solution.py:33
  67.3 4.5 %collective-permute-start.13 = (bf16[48,256]{1,0:T(8,128)(2,1)S(1)}, bf16[48,256]{1,0:T(8,128)(2,1)S(1)}, u32[]{:S(2)}, u32[]{:S(2)}) collective-permute-start(bf16[48,256]{1,0:T(8,128)(2,1)S(1)} %get-tuple-element.37), channel_id=1, source_target_pairs={{0,4},{2,6},{4,0},{6,2},{8,12},{10,14},{12,8},{14,10},{1,5},{3,7},... | collective-permute-start | bytes 73736 | tf_op jit(solution)/shard_map/ppermute | solution.py:17
  68.7 5.0 %collective-permute-start.14 = (bf16[48,256]{1,0:T(8,128)(2,1)S(1)}, bf16[48,256]{1,0:T(8,128)(2,1)S(1)}, u32[]{:S(2)}, u32[]{:S(2)}) collective-permute-start(bf16[48,256]{1,0:T(8,128)(2,1)S(1)} %get-tuple-element.38), channel_id=1, source_target_pairs={{0,8},{2,10},{4,12},{6,14},{8,0},{10,2},{12,4},{14,6},{1,9},{3,11}... | collective-permute-start | bytes 73736 | tf_op jit(solution)/shard_map/ppermute | solution.py:17
  71.5 5.6 %collective-permute-start.15 = (bf16[48,256]{1,0:T(8,128)(2,1)S(1)}, bf16[48,256]{1,0:T(8,128)(2,1)S(1)}, u32[]{:S(2)}, u32[]{:S(2)}) collective-permute-start(bf16[48,256]{1,0:T(8,128)(2,1)S(1)} %get-tuple-element.39), channel_id=1, source_target_pairs={{0,12},{2,14},{4,8},{6,10},{8,4},{10,6},{12,0},{14,2},{1,13},{3,15... | collective-permute-start | bytes 73736 | tf_op jit(solution)/shard_map/ppermute | solution.py:17
  77.1 4.7 %collective-permute-start.21 = (bf16[48,1024]{1,0:T(8,128)(2,1)S(1)}, bf16[48,1024]{1,0:T(8,128)(2,1)S(1)}, u32[]{:S(2)}, u32[]{:S(2)}) collective-permute-start(bf16[48,1024]{1,0:T(8,128)(2,1)S(1)} %pad_maximum_fusion.1.refs_1_), channel_id=1, source_target_pairs={{0,16},{2,18},{4,20},{6,22},{8,24},{10,26},{12,28},{14,30},{16,0},... | collective-permute-start | bytes 294920 | tf_op jit(solution)/shard_map/ppermute | solution.py:44
  78.6 6.1 %collective-permute-start.23 = (bf16[256,1152]{1,0:T(8,128)(2,1)S(1)}, bf16[256,1152]{1,0:T(8,128)(2,1)S(1)}, u32[]{:S(2)}, u32[]{:S(2)}) collective-permute-start(bf16[256,1152]{1,0:T(8,128)(2,1)S(1)} %collective-permute-done.19.refs_6_), channel_id=1, source_target_pairs={{0,1},{1,0},{2,3},{3,2},{4,5},{5,4},{6,7},{7,6},{8,9},{9,8},{10,11... | collective-permute-start | bytes 1769480 | tf_op jit(solution)/shard_map/ppermute | solution.py:22
  81.8 7.4 %collective-permute-start.24 = (bf16[256,1152]{1,0:T(8,128)(2,1)S(1)}, bf16[256,1152]{1,0:T(8,128)(2,1)S(1)}, u32[]{:S(2)}, u32[]{:S(2)}) collective-permute-start(bf16[256,1152]{1,0:T(8,128)(2,1)S(1)} %collective-permute-done.20.refs_8_), channel_id=1, source_target_pairs={{0,1},{1,0},{2,3},{3,2},{4,5},{5,4},{6,7},{7,6},{8,9},{9,8},{10,11... | collective-permute-start | bytes 1769480 | tf_op jit(solution)/shard_map/ppermute | solution.py:22
  81.8 6.4 %collective-permute-start.16 = (bf16[48,1024]{1,0:T(8,128)(2,1)S(1)}, bf16[48,1024]{1,0:T(8,128)(2,1)S(1)}, u32[]{:S(2)}, u32[]{:S(2)}) collective-permute-start(bf16[48,1024]{1,0:T(8,128)(2,1)S(1)} %pad_maximum_fusion.1.refs_1_), channel_id=1, source_target_pairs={{0,2},{2,0},{4,6},{6,4},{8,10},{10,8},{12,14},{14,12},{16,18},{18,... | collective-permute-start | bytes 294920 | tf_op jit(solution)/shard_map/ppermute | solution.py:44
  83.4 5.8 %collective-permute-start.22 = (bf16[48,1024]{1,0:T(8,128)(2,1)S(1)}, bf16[48,1024]{1,0:T(8,128)(2,1)S(1)}, u32[]{:S(2)}, u32[]{:S(2)}) collective-permute-start(bf16[48,1024]{1,0:T(8,128)(2,1)S(1)} %pad_maximum_fusion.1.refs_1_), channel_id=1, source_target_pairs={{0,18},{2,16},{4,22},{6,20},{8,26},{10,24},{12,30},{14,28},{16,2},... | collective-permute-start | bytes 294920 | tf_op jit(solution)/shard_map/ppermute | solution.py:44
  90.5 4.8 %collective-permute-start.25 = (bf16[48,1152]{1,0:T(8,128)(2,1)S(1)}, bf16[48,1152]{1,0:T(8,128)(2,1)S(1)}, u32[]{:S(2)}, u32[]{:S(2)}) collective-permute-start(bf16[48,1152]{1,0:T(8,128)(2,1)S(1)} %get-tuple-element.46), channel_id=1, source_target_pairs={{0,2},{2,0},{4,6},{6,4},{8,10},{10,8},{12,14},{14,12},{16,18},{18,... | collective-permute-start | bytes 331784 | tf_op jit(solution)/shard_map/ppermute | solution.py:44
  92.1 5.5 %collective-permute-start.26 = (bf16[48,1152]{1,0:T(8,128)(2,1)S(1)}, bf16[48,1152]{1,0:T(8,128)(2,1)S(1)}, u32[]{:S(2)}, u32[]{:S(2)}) collective-permute-start(bf16[48,1152]{1,0:T(8,128)(2,1)S(1)} %get-tuple-element.47), channel_id=1, source_target_pairs={{0,16},{2,18},{4,20},{6,22},{8,24},{10,26},{12,28},{14,30},{16,0},... | collective-permute-start | bytes 331784 | tf_op jit(solution)/shard_map/ppermute | solution.py:44
  93.4 5.7 %collective-permute-start.27 = (bf16[48,1152]{1,0:T(8,128)(2,1)S(1)}, bf16[48,1152]{1,0:T(8,128)(2,1)S(1)}, u32[]{:S(2)}, u32[]{:S(2)}) collective-permute-start(bf16[48,1152]{1,0:T(8,128)(2,1)S(1)} %get-tuple-element.48), channel_id=1, source_target_pairs={{0,18},{2,16},{4,22},{6,20},{8,26},{10,24},{12,30},{14,28},{16,2},... | collective-permute-start | bytes 331784 | tf_op jit(solution)/shard_map/ppermute | solution.py:44
  (11 other events, 154.7 us)
where the time goes:
time: 101 us; the launch traced here: 100 us
  waiting for transfers between devices  57.1 us (57%)
  starting transfers between devices  29.8 us (30%)
  Pallas kernels  10.1 us (10%)
  local copies, waits for them, and re-layouts  3.15 us (3%)
    ppermute x11, waiting for transfers between devices, swap_tp(): return lax.ppermute(block, 'tp', route)  38.1 us
    ppermute x11, starting transfers between devices, swap_tp(): return lax.ppermute(block, 'tp', route)  17.3 us
    ppermute x7, waiting for transfers between devices, swap_in_slab(): return lax.ppermute(block, ('groups', 'tp'), route)  17.1 us
    pallas_call x7, Pallas kernels, call(): pl.pallas_call(kernel, in_specs=specs, out_specs=[pl.BlockSpec(memory_spa...  10.1 us
    ppermute x7, starting transfers between devices, swap_in_slab(): return lax.ppermute(block, ('groups', 'tp'), route)  9.54 us
    ppermute x2, starting transfers between devices, swap_by_core(): return lax.ppermute(block, ('tp', 'sp'), route)  2.34 us
  transfers between devices with their start and end apart: 28, of which 14 were waited for; matrix products, arithmetic and copies ran while one was open for 0% of the time, Pallas kernels for 7%

commit v1 on v0

--- a/solution.py
+++ b/solution.py
@@ -22,7 +22,7 @@
     return lax.ppermute(block, "sp", [(s, s ^ 1) for s in range(count)])
 
 
-def swap_by_core(block, flips, only=lambda t: True):
+def swap_by_core(block, flips, only):
     count, cores = lax.axis_size("tp"), lax.axis_size("sp")
     route = [
         (t * cores + s, (t ^ flips[s]) * cores + s)
@@ -56,7 +56,8 @@
         params = pltpu.CompilerParams(vmem_limit_bytes=limit << 20)
     specs = [pl.BlockSpec(memory_space=pltpu.SMEM)] * len(scalars)
     specs += [pl.BlockSpec(memory_space=pltpu.VMEM)] * len(operands)
-    specs += [pl.BlockSpec(memory_space=pl.ANY)] * len(far)
+    specs += [pl.BlockSpec(memory_space=pltpu.HBM)] * len(far)
+    far = [pltpu.with_memory_space_constraint(x, pltpu.HBM) for x in far]
     return pl.pallas_call(
         kernel,
         in_specs=specs,
@@ -200,7 +201,29 @@
             out[:, head:] = high[k * rows : (k + 1) * rows]
 
 
-def head_kernel(flags, came, other, w_out, out, sem):
+def cut_kernel(flags, w_query, w_key, w_value, w_out, share_q, share_kv, out_sent, sems):
+    sp, group = flags[0], flags[3]
+    head = w_key.shape[0]
+    quarter_depth, depth = share_q.shape[0], share_kv.shape[1]
+    half_rows, quarter = out_sent.shape
+    rows = pl.ds(pl.multiple_of((sp * 2 + group) * quarter_depth, 128), quarter_depth)
+    deep = pl.ds(pl.multiple_of(sp * depth, 128), depth)
+    columns = pl.ds(pl.multiple_of((flags[4] ^ 1) * quarter, 128), quarter)
+    heads = pl.ds(pl.multiple_of(sp * half_rows, half_rows), half_rows)
+    moves = (
+        (w_query.at[rows], share_q),
+        (w_key.at[:, deep], share_kv.at[:head]),
+        (w_value.at[:, deep], share_kv.at[head:]),
+        (w_out.at[heads, columns], out_sent),
+    )
+    copies = [pltpu.make_async_copy(a, b, sems.at[i]) for i, (a, b) in enumerate(moves)]
+    for copy in copies:
+        copy.start()
+    for copy in copies:
+        copy.wait()
+
+
+def head_kernel(flags, came, other, w_out, out, out_head, sem):
     head, quarter = w_out.shape[0], out.shape[1]
     half_rows = came.shape[0]
     own = pl.ds(pl.multiple_of(flags[1] * head, head), head)
@@ -211,6 +234,7 @@
         at = (1 - flags[1]) * head + (flags[0] ^ i) * half_rows
         out[pl.ds(pl.multiple_of(at, half_rows), half_rows)] = piece[...]
     copy.wait()
+    out_head[...] = out[pl.ds(pl.multiple_of(flags[0] * head, head), head)]
 
 
 def project_kernel(peers, split, flags, *refs):
@@ -218,11 +242,19 @@
     count, width = outs[0].shape
     rows = jnp.concatenate([m[...] for m in stacked], axis=0)
     step = 384 if width % 384 == 0 else width
-    received = flags[2] != flags[0]
+    low, inner = flags[0] == 0, flags[2] != 0
     for at in range(0, width, step):
         parts = [p[:, at : at + step] for p in pieces]
         if split:
-            parts[-2:] = [jnp.where(received, parts[-2], parts[-1])]
+            own, outer, outer2, near, near2, far, far2, last, last2 = parts
+            pick = lambda flag, a, b: jnp.where(flag, a, b)
+            heads = lambda a, b: jnp.concatenate([pick(low, a, b), pick(low, b, a)], axis=0)
+            parts = [
+                own,
+                pick(inner, pick(low, outer2, outer), heads(near, near2)),
+                pick(inner, pick(low, outer, outer2), heads(far, far2)),
+                pick(low == inner, last2, last),
+            ]
         total = plain(rows, jnp.concatenate(parts, axis=0))
         for i, out in enumerate(outs):
             out[:, at : at + step] = total[i * count : (i + 1) * count].astype(out.dtype)
@@ -271,21 +303,24 @@
     inner = ((slab == 1) | (slab == 2)).astype(jnp.int32)
     flags = jnp.stack([sp_place, side, inner, group, mine, slab]).astype(jnp.int32)
     turned_kv = [w_key.T, w_value.T]
-    share_q = lax.dynamic_slice_in_dim(
-        w_query, (sp_place * 2 + group) * (depth // 2), depth // 2, 0
-    )
-    share_kv = jnp.concatenate(
-        [lax.dynamic_slice_in_dim(w, sp_place * depth, depth, 1) for w in turned_kv], axis=0
-    )
     core_low = sp_place == 0
-    sent_at = (sp_place * half_rows, (mine ^ 1) * quarter)
-    share_q, share_kv, doc_lengths, w_out, flags, core_low, sent_at = fence(
-        share_q, share_kv, doc_lengths, w_out, flags, core_low, sent_at
+    flags, doc_lengths, core_low = fence(flags, doc_lengths, core_low)
+    share_q, share_kv, out_sent = call(
+        cut_kernel,
+        [
+            ((depth // 2, head_dim), jnp.bfloat16),
+            ((head_dim, depth), jnp.bfloat16),
+            ((half_rows, quarter), jnp.bfloat16),
+        ],
+        [flags],
+        [],
+        [pltpu.SemaphoreType.DMA((4,))],
+        pltpu.VMEM if short else pl.ANY,
+        [w_query, *turned_kv, w_out],
     )
     came_q = swap_tp(share_q, 1)
     cross_q = swap_in_slab(came_q, 1, 0)
     came_kv = swap_tp(share_kv, 1)
-    out_sent = lax.dynamic_slice(w_out, sent_at, (half_rows, quarter))
     out_came = swap_tp(out_sent, 1)
     out_other = swap_sp(out_came)
     weights = [w_query, *turned_kv, came_kv, swap_sp(came_kv), came_q, cross_q]
@@ -295,17 +330,21 @@
     )[0]
 
     in_order = lambda a, b, flag: [jnp.where(flag, a, b), jnp.where(flag, b, a)]
-    out_own = call(
+    out_own, out_head = call(
         head_kernel,
-        [((2 * head_dim, quarter), jnp.bfloat16)],
+        [((2 * head_dim, quarter), jnp.bfloat16), ((head_dim, quarter), jnp.bfloat16)],
         [flags],
         [out_came, out_other],
         [pltpu.SemaphoreType.DMA(())],
         far=[w_out],
-    )[0]
+    )
     if short:
-        out_first = swap_by_core(out_own, (2, 4))
-        out_swapped = swap_sp(out_first)
+        is_outer = lambda t: not is_inner(t)
+        out_outer = swap_by_core(out_own, (4, 2), is_outer)
+        out_near = swap_by_core(out_head, (2, 2), is_inner)
+        out_far = swap_by_core(out_head, (4, 4), is_inner)
+        held = [out_outer, swap_sp(out_outer), out_near, swap_sp(out_near)]
+        held += [out_far, swap_sp(out_far)]
 
     count = slabs * rows
     half_head = head_dim // 2
@@ -334,25 +373,25 @@
         [queries] + every,
         limit=16 if short else 56,
     )
-
+    mixed = list(mixed)
+
+    if short:
+        out_outer, mixed[1] = fence(out_outer, mixed[1])
+        out_sent = jnp.where(core_low, out_outer, out_own)
     parts = [mixed[0]]
     for k in range(1, slabs):
         parts.append(swap_tp(mixed[k], 2 * k))
-    if short:
-        parts[1:3] = in_order(parts[1], parts[2], core_low)
     merged = jnp.concatenate(parts, axis=1)
     peers = ((0, 0), (0, 1), (1, 0), (1, 1))
     stacked = [merged] + [swap_in_slab(merged, g, t) for g, t in peers[1:]]
     if short:
-        out_sent = jnp.where(core_low, out_own, out_first)
-        out_last = swap_by_core(out_sent, (6, 2), is_inner)
+        out_last = swap_by_core(out_sent, (2, 6), is_inner)
         out_last, stacked[2] = fence(out_last, stacked[2])
-        pieces = [out_own, out_first, out_swapped, out_last, swap_sp(out_last)]
+        pieces = [out_own, *held, out_last, swap_sp(out_last)]
     else:
         pieces = [out_own]
-        mine_of = lax.dynamic_slice_in_dim(out_own, sp_place * head_dim, head_dim, 0)
         for k in range(1, slabs):
-            piece = swap_tp(mine_of, 2 * k)
+            piece = swap_tp(out_head, 2 * k)
             both = in_order(piece, swap_sp(piece), core_low)
             pieces.append(jnp.concatenate(both, axis=0))
     outs = call(

time: 101 us -> 105 us (1.040)
  starting transfers between devices: 29.8 us -> 37.2 us
  local copies, waits for them, and re-layouts: 3.15 us -> 0.12 us
  waiting for transfers between devices: 57.1 us -> 54.1 us
  Pallas kernels: 10.1 us -> 12.9 us
    ppermute x2 -> x4, waiting for transfers between devices: 0.01 us -> 12.1 us  [swap_by_core(): return lax.ppermute(block, ('tp', 'sp'), route)]
    ppermute x11, waiting for transfers between devices: 38.1 us -> 27.2 us  [swap_tp(): return lax.ppermute(block, 'tp', route)]
    ppermute x2 -> x4, starting transfers between devices: 2.34 us -> 8.6 us  [swap_by_core(): return lax.ppermute(block, ('tp', 'sp'), route)]
    ppermute x7, waiting for transfers between devices: 17.1 us -> 12.9 us  [swap_in_slab(): return lax.ppermute(block, ('groups', 'tp'), route)]
    dynamic_slice x3 -> x0, local copies, waits for them, and re-layouts: 3.04 us -> none  [the longest x1 1.69 us: local(): lax.dynamic_slice_in_dim(w_query, (sp_place * 2 + group) * (depth // 2),...]
    pallas_call x7 -> x8, Pallas kernels: 10.1 us -> 12.9 us  [call(): pl.pallas_call(kernel, in_specs=specs, out_specs=[pl.BlockSpec(memory_spa...]
  transfers between devices with their start and end apart: 28 -> 32, of which waited for: 14 -> 14; matrix products, arithmetic and copies ran while one was open for 0% -> 0% of each run, Pallas kernels for 7% -> 8%
where the time goes in v1:
time: 105 us
  waiting for transfers between devices  54.1 us (52%)
  starting transfers between devices  37.2 us (35%)
  Pallas kernels  12.9 us (12%)
    ppermute x11, waiting for transfers between devices, swap_tp(): return lax.ppermute(block, 'tp', route)  27.2 us
    ppermute x11, starting transfers between devices, swap_tp(): return lax.ppermute(block, 'tp', route)  18 us
    ppermute x7, waiting for transfers between devices, swap_in_slab(): return lax.ppermute(block, ('groups', 'tp'), route)  12.9 us
    pallas_call x8, Pallas kernels, call(): pl.pallas_call(kernel, in_specs=specs, out_specs=[pl.BlockSpec(memory_spa...  12.9 us
    ppermute x4, waiting for transfers between devices, swap_by_core(): return lax.ppermute(block, ('tp', 'sp'), route)  12.1 us
    ppermute x7, starting transfers between devices, swap_in_slab(): return lax.ppermute(block, ('groups', 'tp'), route)  9.39 us
    ppermute x4, starting transfers between devices, swap_by_core(): return lax.ppermute(block, ('tp', 'sp'), route)  8.6 us
  transfers between devices with their start and end apart: 32, of which 14 were waited for; matrix products, arithmetic and copies ran while one was open for 0% of the time, Pallas kernels for 8%

profile of v1, /device:TPU:0, one launch (start us, length us, event | category | flops | bytes accessed | tf_op | source)
XLA Modules:
  0.0 104.6 jit_solution(5779597820809038029)
XLA Ops:
  0.1 1.8 %shard_map.73 = (bf16[1152,128]{1,0:T(8,128)(2,1)S(1)}, bf16[128,2304]{1,0:T(8,128)(2,1)S(1)}, bf16[64,1152]{1,0:T(8,128)(2,1)S(1)}) custom-call(s32[6]{0:T(128)S(1)} %stack.31.flags.refs_0_, bf16[4608,128]{1,0:T(8,128)(2,1)} %refs_0_.3, bf16[64,4608]{1,0:T(8,128)(2,1)} %bitcast.8, bf16[64,4608]{1,0:T(8,128)(2,1)} %bitcast.11, bf16[128,4608]{1,0:T(8,128)(2,1)} %w_out.3), custom_call_target="tpu_custom_call" | custom-call | tf_op jit(solution)/shard_map/pallas_call | solution.py:61
  1.9 3.1 %collective-permute-start.2 = (bf16[128,2304]{1,0:T(8,128)(2,1)S(1)}, bf16[128,2304]{1,0:T(8,128)(2,1)S(1)}, u32[]{:S(2)}, u32[]{:S(2)}) collective-permute-start(bf16[128,2304]{1,0:T(8,128)(2,1)S(1)} %get-tuple-element.31), channel_id=1, source_target_pairs={{0,2},{2,0},{4,6},{6,4},{8,10},{10,8},{12,14},{14,12},{1,3},{3,1},... | collective-permute-start | bytes 1769480 | tf_op jit(solution)/shard_map/ppermute | solution.py:17
  5.0 1.9 %collective-permute-start.13 = (bf16[64,1152]{1,0:T(8,128)(2,1)S(1)}, bf16[64,1152]{1,0:T(8,128)(2,1)S(1)}, u32[]{:S(2)}, u32[]{:S(2)}) collective-permute-start(bf16[64,1152]{1,0:T(8,128)(2,1)S(1)} %get-tuple-element.38), channel_id=1, source_target_pairs={{0,2},{2,0},{4,6},{6,4},{8,10},{10,8},{12,14},{14,12},{1,3},{3,1},... | collective-permute-start | bytes 442376 | tf_op jit(solution)/shard_map/ppermute | solution.py:17
  7.0 2.6 %collective-permute-start.1 = (bf16[48,4608]{1,0:T(8,128)(2,1)S(1)}, bf16[48,4608]{1,0:T(8,128)(2,1)S(1)}, u32[]{:S(2)}, u32[]{:S(2)}) collective-permute-start(bf16[48,4608]{1,0:T(8,128)(2,1)S(1)} %copy-done.3), channel_id=1, source_target_pairs={{0,8},{2,10},{4,12},{6,14},{8,0},{10,2},{12,4},{14,6},{1,9},{3,11}... | collective-permute-start | bytes 1327112 | tf_op jit(solution)/shard_map/ppermute | solution.py:17
  9.6 1.6 %collective-permute-start = (bf16[48,4608]{1,0:T(8,128)(2,1)S(1)}, bf16[48,4608]{1,0:T(8,128)(2,1)S(1)}, u32[]{:S(2)}, u32[]{:S(2)}) collective-permute-start(bf16[48,4608]{1,0:T(8,128)(2,1)S(1)} %copy-done.3), channel_id=1, source_target_pairs={{0,4},{2,6},{4,0},{6,2},{8,12},{10,14},{12,8},{14,10},{1,5},{3,7},... | collective-permute-start | bytes 1327112 | tf_op jit(solution)/shard_map/ppermute | solution.py:17
  11.1 16.6 %collective-permute-done.13.came = bf16[64,1152]{1,0:T(8,128)(2,1)S(1)} collective-permute-done((bf16[64,1152]{1,0:T(8,128)(2,1)S(1)}, bf16[64,1152]{1,0:T(8,128)(2,1)S(1)}, u32[]{:S(2)}, u32[]{:S(2)}) %collective-permute-start.13) | collective-permute-done | bytes 147488 | tf_op jit(solution)/shard_map/ppermute | solution.py:17
  27.8 1.7 %collective-permute-start.5 = (bf16[1152,128]{1,0:T(8,128)(2,1)S(1)}, bf16[1152,128]{1,0:T(8,128)(2,1)S(1)}, u32[]{:S(2)}, u32[]{:S(2)}) collective-permute-start(bf16[1152,128]{1,0:T(8,128)(2,1)S(1)} %collective-permute-done.4.refs_8_.refs_5_), channel_id=1, source_target_pairs={{0,16},{2,18},{4,20},{6,22},{8,24},{10,26},{12,28},{14,30},{16,0},... | collective-permute-start | bytes 884744 | tf_op jit(solution)/shard_map/ppermute | solution.py:44
  32.0 1.5 %shard_map.78 = (bf16[256,1152]{1,0:T(8,128)(2,1)S(1)}, bf16[128,1152]{1,0:T(8,128)(2,1)S(1)}) custom-call(s32[6]{0:T(128)S(1)} %stack.31.flags.refs_0_, bf16[64,1152]{1,0:T(8,128)(2,1)S(1)} %collective-permute-done.13.came, bf16[64,1152]{1,0:T(8,128)(2,1)S(1)} %collective-permute-done.14.other, bf16[128,4608]{1,0:T(8,128)(2,1)} %w_out.3), custom_call_target="tpu_custom_call" | custom-call | tf_op jit(solution)/shard_map/pallas_call | solution.py:61
  33.5 3.6 %collective-permute-done.5.refs_9_.refs_6_ = bf16[1152,128]{1,0:T(8,128)(2,1)S(1)} collective-permute-done((bf16[1152,128]{1,0:T(8,128)(2,1)S(1)}, bf16[1152,128]{1,0:T(8,128)(2,1)S(1)}, u32[]{:S(2)}, u32[]{:S(2)}) %collective-permute-start.5) | collective-permute-done | bytes 294944 | tf_op jit(solution)/shard_map/ppermute | solution.py:44
  37.2 4.7 %collective-permute-start.15 = (bf16[256,1152]{1,0:T(8,128)(2,1)S(1)}, bf16[256,1152]{1,0:T(8,128)(2,1)S(1)}, u32[]{:S(2)}, u32[]{:S(2)}) collective-permute-start(bf16[256,1152]{1,0:T(8,128)(2,1)S(1)} %get-tuple-element.39.refs_5_), channel_id=1, source_target_pairs={{0,8},{1,5},{2,10},{3,7},{12,4},{13,9},{14,6},{15,11},{16,24},{17,... | collective-permute-start | bytes 1769480 | tf_op jit(solution)/shard_map/ppermute | solution.py:33
  43.6 2.1 %shard_map.74.early = f32[144,512]{1,0:T(8,128)S(1)} custom-call(s32[6]{0:T(128)S(1)} %stack.31.flags.refs_0_, bf16[48,4608]{1,0:T(8,128)(2,1)S(1)} %copy-done.3, bf16[48,4608]{1,0:T(8,128)(2,1)S(1)} %collective-permute-done.refs_1_, bf16[48,4608]{1,0:T(8,128)(2,1)S(1)} %collective-permute-done.1.refs_2_, bf16[4608,128]{1,0:T(8,128)(2,1)S(1)} %copy-done, ...), custom_call_target="tpu_custom_call" | custom-call | tf_op jit(solution)/shard_map/pallas_call | solution.py:61
  46.6 2.0 %shard_map.76 = (bf16[384,128]{1,0:T(8,128)(2,1)S(1)}, bf16[192,256]{1,0:T(8,128)(2,1)S(1)}) custom-call(s32[6]{0:T(128)S(1)} %stack.31.flags.refs_0_, f32[144,512]{1,0:T(8,128)S(1)} %shard_map.74.early, bf16[48,4608]{1,0:T(8,128)(2,1)S(1)} %collective-permute-done.8.middle, bf16[48,4608]{1,0:T(8,128)(2,1)S(1)} %collective-permute-done.9.relayed, ...), custom_call_target="tpu_custom_call" | custom-call | tf_op jit(solution)/shard_map/pallas_call | solution.py:61
  48.6 1.6 %collective-permute-start.10 = (bf16[192,256]{1,0:T(8,128)(2,1)S(1)}, bf16[192,256]{1,0:T(8,128)(2,1)S(1)}, u32[]{:S(2)}, u32[]{:S(2)}) collective-permute-start(bf16[192,256]{1,0:T(8,128)(2,1)S(1)} %get-tuple-element.36.refs_3_), channel_id=1, source_target_pairs={{0,2},{2,0},{4,6},{6,4},{8,10},{10,8},{12,14},{14,12},{1,3},{3,1},... | collective-permute-start | bytes 294920 | tf_op jit(solution)/shard_map/ppermute | solution.py:17
  50.2 3.1 %collective-permute-done.10.refs_4_ = bf16[192,256]{1,0:T(8,128)(2,1)S(1)} collective-permute-done((bf16[192,256]{1,0:T(8,128)(2,1)S(1)}, bf16[192,256]{1,0:T(8,128)(2,1)S(1)}, u32[]{:S(2)}, u32[]{:S(2)}) %collective-permute-start.10) | collective-permute-done | bytes 98336 | tf_op jit(solution)/shard_map/ppermute | solution.py:17
  54.6 1.8 %shard_map.77 = (bf16[48,256]{1,0:T(8,128)(2,1)S(1)}, bf16[48,256]{1,0:T(8,128)(2,1)S(1)}, bf16[48,256]{1,0:T(8,128)(2,1)S(1)}, bf16[48,256]{1,0:T(8,128)(2,1)S(1)}) custom-call(s32[6]{0:T(128)S(1)} %stack.31.flags.refs_0_, s32[8]{0:T(128)S(1)} %copy-done.4, bf16[384,128]{1,0:T(8,128)(2,1)S(1)} %get-tuple-element.35.refs_2_, ...), custom_call_target="tpu_custom_call" | custom-call | tf_op jit(solution)/shard_map/pallas_call | solution.py:61
  57.8 2.7 %collective-permute-start.16 = (bf16[48,256]{1,0:T(8,128)(2,1)S(1)}, bf16[48,256]{1,0:T(8,128)(2,1)S(1)}, u32[]{:S(2)}, u32[]{:S(2)}) collective-permute-start(bf16[48,256]{1,0:T(8,128)(2,1)S(1)} %get-tuple-element.41), channel_id=1, source_target_pairs={{0,4},{2,6},{4,0},{6,2},{8,12},{10,14},{12,8},{14,10},{1,5},{3,7},... | collective-permute-start | bytes 73736 | tf_op jit(solution)/shard_map/ppermute | solution.py:17
  61.0 2.0 %collective-permute-start.18 = (bf16[48,256]{1,0:T(8,128)(2,1)S(1)}, bf16[48,256]{1,0:T(8,128)(2,1)S(1)}, u32[]{:S(2)}, u32[]{:S(2)}) collective-permute-start(bf16[48,256]{1,0:T(8,128)(2,1)S(1)} %get-tuple-element.43), channel_id=1, source_target_pairs={{0,12},{2,14},{4,8},{6,10},{8,4},{10,6},{12,0},{14,2},{1,13},{3,15... | collective-permute-start | bytes 73736 | tf_op jit(solution)/shard_map/ppermute | solution.py:17
  63.0 6.6 %collective-permute-done.16 = bf16[48,256]{1,0:T(8,128)(2,1)S(1)} collective-permute-done((bf16[48,256]{1,0:T(8,128)(2,1)S(1)}, bf16[48,256]{1,0:T(8,128)(2,1)S(1)}, u32[]{:S(2)}, u32[]{:S(2)}) %collective-permute-start.16) | collective-permute-done | bytes 24608 | tf_op jit(solution)/shard_map/ppermute | solution.py:17
  74.3 12.1 %collective-permute-done.24.refs_8_ = bf16[128,1152]{1,0:T(8,128)(2,1)S(1)} collective-permute-done((bf16[128,1152]{1,0:T(8,128)(2,1)S(1)}, bf16[128,1152]{1,0:T(8,128)(2,1)S(1)}, u32[]{:S(2)}, u32[]{:S(2)}) %collective-permute-start.24) | collective-permute-done | bytes 294944 | tf_op jit(solution)/shard_map/ppermute | solution.py:33
  86.9 1.5 %collective-permute-start.19 = (bf16[48,1024]{1,0:T(8,128)(2,1)S(1)}, bf16[48,1024]{1,0:T(8,128)(2,1)S(1)}, u32[]{:S(2)}, u32[]{:S(2)}) collective-permute-start(bf16[48,1024]{1,0:T(8,128)(2,1)S(1)} %constant_dynamic-update-slice_fusion.refs_1_), channel_id=1, source_target_pairs={{0,2},{2,0},{4,6},{6,4},{8,10},{10,8},{12,14},{14,12},{16,18},{18,... | collective-permute-start | bytes 294920 | tf_op jit(solution)/shard_map/ppermute | solution.py:44
  89.7 1.9 %collective-permute-done.19.refs_2_ = bf16[48,1024]{1,0:T(8,128)(2,1)S(1)} collective-permute-done((bf16[48,1024]{1,0:T(8,128)(2,1)S(1)}, bf16[48,1024]{1,0:T(8,128)(2,1)S(1)}, u32[]{:S(2)}, u32[]{:S(2)}) %collective-permute-start.19) | collective-permute-done | bytes 98336 | tf_op jit(solution)/shard_map/ppermute | solution.py:44
  91.6 2.3 %collective-permute-done.22.refs_4_ = bf16[48,1024]{1,0:T(8,128)(2,1)S(1)} collective-permute-done((bf16[48,1024]{1,0:T(8,128)(2,1)S(1)}, bf16[48,1024]{1,0:T(8,128)(2,1)S(1)}, u32[]{:S(2)}, u32[]{:S(2)}) %collective-permute-start.22) | collective-permute-done | bytes 98336 | tf_op jit(solution)/shard_map/ppermute | solution.py:44
  97.5 1.4 %collective-permute-start.31 = (bf16[48,1152]{1,0:T(8,128)(2,1)S(1)}, bf16[48,1152]{1,0:T(8,128)(2,1)S(1)}, u32[]{:S(2)}, u32[]{:S(2)}) collective-permute-start(bf16[48,1152]{1,0:T(8,128)(2,1)S(1)} %get-tuple-element.52), channel_id=1, source_target_pairs={{0,18},{2,16},{4,22},{6,20},{8,26},{10,24},{12,30},{14,28},{16,2},... | collective-permute-start | bytes 331784 | tf_op jit(solution)/shard_map/ppermute | solution.py:44
  98.9 2.4 %collective-permute-done.29.refs_1_ = bf16[48,1152]{1,0:T(8,128)(2,1)S(1)} collective-permute-done((bf16[48,1152]{1,0:T(8,128)(2,1)S(1)}, bf16[48,1152]{1,0:T(8,128)(2,1)S(1)}, u32[]{:S(2)}, u32[]{:S(2)}) %collective-permute-start.29) | collective-permute-done | bytes 110624 | tf_op jit(solution)/shard_map/ppermute | solution.py:44
  (66 shorter events, 21.5 us)
Async XLA Ops:
  1.9 27.8 %collective-permute-start.2 = (bf16[128,2304]{1,0:T(8,128)(2,1)S(1)}, bf16[128,2304]{1,0:T(8,128)(2,1)S(1)}, u32[]{:S(2)}, u32[]{:S(2)}) collective-permute-start(bf16[128,2304]{1,0:T(8,128)(2,1)S(1)} %get-tuple-element.31), channel_id=1, source_target_pairs={{0,2},{2,0},{4,6},{6,4},{8,10},{10,8},{12,14},{14,12},{1,3},{3,1},... | collective-permute-start | bytes 1769480 | tf_op jit(solution)/shard_map/ppermute | solution.py:17
  4.9 22.8 %collective-permute-start.4 = (bf16[1152,128]{1,0:T(8,128)(2,1)S(1)}, bf16[1152,128]{1,0:T(8,128)(2,1)S(1)}, u32[]{:S(2)}, u32[]{:S(2)}) collective-permute-start(bf16[1152,128]{1,0:T(8,128)(2,1)S(1)} %get-tuple-element.32), channel_id=1, source_target_pairs={{0,2},{2,0},{4,6},{6,4},{8,10},{10,8},{12,14},{14,12},{1,3},{3,1},... | collective-permute-start | bytes 884744 | tf_op jit(solution)/shard_map/ppermute | solution.py:17
  5.0 22.7 %collective-permute-start.13 = (bf16[64,1152]{1,0:T(8,128)(2,1)S(1)}, bf16[64,1152]{1,0:T(8,128)(2,1)S(1)}, u32[]{:S(2)}, u32[]{:S(2)}) collective-permute-start(bf16[64,1152]{1,0:T(8,128)(2,1)S(1)} %get-tuple-element.38), channel_id=1, source_target_pairs={{0,2},{2,0},{4,6},{6,4},{8,10},{10,8},{12,14},{14,12},{1,3},{3,1},... | collective-permute-start | bytes 442376 | tf_op jit(solution)/shard_map/ppermute | solution.py:17
  7.0 23.0 %collective-permute-start.1 = (bf16[48,4608]{1,0:T(8,128)(2,1)S(1)}, bf16[48,4608]{1,0:T(8,128)(2,1)S(1)}, u32[]{:S(2)}, u32[]{:S(2)}) collective-permute-start(bf16[48,4608]{1,0:T(8,128)(2,1)S(1)} %copy-done.3), channel_id=1, source_target_pairs={{0,8},{2,10},{4,12},{6,14},{8,0},{10,2},{12,4},{14,6},{1,9},{3,11}... | collective-permute-start | bytes 1327112 | tf_op jit(solution)/shard_map/ppermute | solution.py:17
  9.6 21.1 %collective-permute-start = (bf16[48,4608]{1,0:T(8,128)(2,1)S(1)}, bf16[48,4608]{1,0:T(8,128)(2,1)S(1)}, u32[]{:S(2)}, u32[]{:S(2)}) collective-permute-start(bf16[48,4608]{1,0:T(8,128)(2,1)S(1)} %copy-done.3), channel_id=1, source_target_pairs={{0,4},{2,6},{4,0},{6,2},{8,12},{10,14},{12,8},{14,10},{1,5},{3,7},... | collective-permute-start | bytes 1327112 | tf_op jit(solution)/shard_map/ppermute | solution.py:17
  27.8 9.4 %collective-permute-start.5 = (bf16[1152,128]{1,0:T(8,128)(2,1)S(1)}, bf16[1152,128]{1,0:T(8,128)(2,1)S(1)}, u32[]{:S(2)}, u32[]{:S(2)}) collective-permute-start(bf16[1152,128]{1,0:T(8,128)(2,1)S(1)} %collective-permute-done.4.refs_8_.refs_5_), channel_id=1, source_target_pairs={{0,16},{2,18},{4,20},{6,22},{8,24},{10,26},{12,28},{14,30},{16,0},... | collective-permute-start | bytes 884744 | tf_op jit(solution)/shard_map/ppermute | solution.py:44
  29.5 12.5 %collective-permute-start.6 = (bf16[1152,128]{1,0:T(8,128)(2,1)S(1)}, bf16[1152,128]{1,0:T(8,128)(2,1)S(1)}, u32[]{:S(2)}, u32[]{:S(2)}) collective-permute-start(bf16[1152,128]{1,0:T(8,128)(2,1)S(1)} %collective-permute-done.4.refs_8_.refs_5_), channel_id=1, source_target_pairs={{0,1},{1,0},{2,3},{3,2},{4,5},{5,4},{6,7},{7,6},{8,9},{9,8},{10,11... | collective-permute-start | bytes 884744 | tf_op jit(solution)/shard_map/ppermute | solution.py:22
  29.7 13.9 %collective-permute-start.3 = (bf16[128,2304]{1,0:T(8,128)(2,1)S(1)}, bf16[128,2304]{1,0:T(8,128)(2,1)S(1)}, u32[]{:S(2)}, u32[]{:S(2)}) collective-permute-start(bf16[128,2304]{1,0:T(8,128)(2,1)S(1)} %collective-permute-done.2.refs_6_.refs_3_), channel_id=1, source_target_pairs={{0,1},{1,0},{2,3},{3,2},{4,5},{5,4},{6,7},{7,6},{8,9},{9,8},{10,11... | collective-permute-start | bytes 1769480 | tf_op jit(solution)/shard_map/ppermute | solution.py:22
  30.0 15.8 %collective-permute-start.8 = (bf16[48,4608]{1,0:T(8,128)(2,1)S(1)}, bf16[48,4608]{1,0:T(8,128)(2,1)S(1)}, u32[]{:S(2)}, u32[]{:S(2)}) collective-permute-start(bf16[48,4608]{1,0:T(8,128)(2,1)S(1)} %copy-done.3), channel_id=1, source_target_pairs={{4,8},{6,10},{8,4},{10,6},{5,9},{7,11},{9,5},{11,7},{20,24},{22,26... | collective-permute-start | bytes 1327112 | tf_op jit(solution)/shard_map/ppermute | solution.py:17
  30.7 15.9 %collective-permute-start.9 = (bf16[48,4608]{1,0:T(8,128)(2,1)S(1)}, bf16[48,4608]{1,0:T(8,128)(2,1)S(1)}, u32[]{:S(2)}, u32[]{:S(2)}) collective-permute-start(bf16[48,4608]{1,0:T(8,128)(2,1)S(1)} %collective-permute-done.1.refs_2_), channel_id=1, source_target_pairs={{4,0},{6,2},{8,12},{10,14},{5,1},{7,3},{9,13},{11,15},{20,16},{22,... | collective-permute-start | bytes 1327112 | tf_op jit(solution)/shard_map/ppermute | solution.py:17
  37.2 19.2 %collective-permute-start.15 = (bf16[256,1152]{1,0:T(8,128)(2,1)S(1)}, bf16[256,1152]{1,0:T(8,128)(2,1)S(1)}, u32[]{:S(2)}, u32[]{:S(2)}) collective-permute-start(bf16[256,1152]{1,0:T(8,128)(2,1)S(1)} %get-tuple-element.39.refs_5_), channel_id=1, source_target_pairs={{0,8},{1,5},{2,10},{3,7},{12,4},{13,9},{14,6},{15,11},{16,24},{17,... | collective-permute-start | bytes 1769480 | tf_op jit(solution)/shard_map/ppermute | solution.py:33
  56.5 17.8 %collective-permute-start.20 = (bf16[256,1152]{1,0:T(8,128)(2,1)S(1)}, bf16[256,1152]{1,0:T(8,128)(2,1)S(1)}, u32[]{:S(2)}, u32[]{:S(2)}) collective-permute-start(bf16[256,1152]{1,0:T(8,128)(2,1)S(1)} %broadcast_select_fusion), channel_id=1, source_target_pairs={{4,0},{5,9},{6,2},{7,11},{8,12},{9,5},{10,14},{11,7},{20,16},{21,2... | collective-permute-start | bytes 1769480 | tf_op jit(solution)/shard_map/ppermute | solution.py:33
  57.8 11.8 %collective-permute-start.16 = (bf16[48,256]{1,0:T(8,128)(2,1)S(1)}, bf16[48,256]{1,0:T(8,128)(2,1)S(1)}, u32[]{:S(2)}, u32[]{:S(2)}) collective-permute-start(bf16[48,256]{1,0:T(8,128)(2,1)S(1)} %get-tuple-element.41), channel_id=1, source_target_pairs={{0,4},{2,6},{4,0},{6,2},{8,12},{10,14},{12,8},{14,10},{1,5},{3,7},... | collective-permute-start | bytes 73736 | tf_op jit(solution)/shard_map/ppermute | solution.py:17
  60.5 9.1 %collective-permute-start.17 = (bf16[48,256]{1,0:T(8,128)(2,1)S(1)}, bf16[48,256]{1,0:T(8,128)(2,1)S(1)}, u32[]{:S(2)}, u32[]{:S(2)}) collective-permute-start(bf16[48,256]{1,0:T(8,128)(2,1)S(1)} %get-tuple-element.42), channel_id=1, source_target_pairs={{0,8},{2,10},{4,12},{6,14},{8,0},{10,2},{12,4},{14,6},{1,9},{3,11}... | collective-permute-start | bytes 73736 | tf_op jit(solution)/shard_map/ppermute | solution.py:17
  61.0 8.6 %collective-permute-start.18 = (bf16[48,256]{1,0:T(8,128)(2,1)S(1)}, bf16[48,256]{1,0:T(8,128)(2,1)S(1)}, u32[]{:S(2)}, u32[]{:S(2)}) collective-permute-start(bf16[48,256]{1,0:T(8,128)(2,1)S(1)} %get-tuple-element.43), channel_id=1, source_target_pairs={{0,12},{2,14},{4,8},{6,10},{8,4},{10,6},{12,0},{14,2},{1,13},{3,15... | collective-permute-start | bytes 73736 | tf_op jit(solution)/shard_map/ppermute | solution.py:17
  71.0 15.4 %collective-permute-start.24 = (bf16[128,1152]{1,0:T(8,128)(2,1)S(1)}, bf16[128,1152]{1,0:T(8,128)(2,1)S(1)}, u32[]{:S(2)}, u32[]{:S(2)}) collective-permute-start(bf16[128,1152]{1,0:T(8,128)(2,1)S(1)} %get-tuple-element.47), channel_id=1, source_target_pairs={{4,0},{5,1},{6,2},{7,3},{8,12},{9,13},{10,14},{11,15},{20,16},{21,... | collective-permute-start | bytes 884744 | tf_op jit(solution)/shard_map/ppermute | solution.py:33
  72.3 14.1 %collective-permute-start.26 = (bf16[128,1152]{1,0:T(8,128)(2,1)S(1)}, bf16[128,1152]{1,0:T(8,128)(2,1)S(1)}, u32[]{:S(2)}, u32[]{:S(2)}) collective-permute-start(bf16[128,1152]{1,0:T(8,128)(2,1)S(1)} %get-tuple-element.47), channel_id=1, source_target_pairs={{4,12},{5,13},{6,14},{7,15},{8,0},{9,1},{10,2},{11,3},{20,28},{21,... | collective-permute-start | bytes 884744 | tf_op jit(solution)/shard_map/ppermute | solution.py:33
  73.6 16.1 %collective-permute-start.23 = (bf16[256,1152]{1,0:T(8,128)(2,1)S(1)}, bf16[256,1152]{1,0:T(8,128)(2,1)S(1)}, u32[]{:S(2)}, u32[]{:S(2)}) collective-permute-start(bf16[256,1152]{1,0:T(8,128)(2,1)S(1)} %collective-permute-done.15.refs_6_), channel_id=1, source_target_pairs={{0,1},{1,0},{2,3},{3,2},{4,5},{5,4},{6,7},{7,6},{8,9},{9,8},{10,11... | collective-permute-start | bytes 1769480 | tf_op jit(solution)/shard_map/ppermute | solution.py:22
  74.3 19.6 %collective-permute-start.28 = (bf16[256,1152]{1,0:T(8,128)(2,1)S(1)}, bf16[256,1152]{1,0:T(8,128)(2,1)S(1)}, u32[]{:S(2)}, u32[]{:S(2)}) collective-permute-start(bf16[256,1152]{1,0:T(8,128)(2,1)S(1)} %collective-permute-done.20.refs_12_), channel_id=1, source_target_pairs={{0,1},{1,0},{2,3},{3,2},{4,5},{5,4},{6,7},{7,6},{8,9},{9,8},{10,11... | collective-permute-start | bytes 1769480 | tf_op jit(solution)/shard_map/ppermute | solution.py:22
  86.9 4.7 %collective-permute-start.19 = (bf16[48,1024]{1,0:T(8,128)(2,1)S(1)}, bf16[48,1024]{1,0:T(8,128)(2,1)S(1)}, u32[]{:S(2)}, u32[]{:S(2)}) collective-permute-start(bf16[48,1024]{1,0:T(8,128)(2,1)S(1)} %constant_dynamic-update-slice_fusion.refs_1_), channel_id=1, source_target_pairs={{0,2},{2,0},{4,6},{6,4},{8,10},{10,8},{12,14},{14,12},{16,18},{18,... | collective-permute-start | bytes 294920 | tf_op jit(solution)/shard_map/ppermute | solution.py:44
  88.4 5.5 %collective-permute-start.22 = (bf16[48,1024]{1,0:T(8,128)(2,1)S(1)}, bf16[48,1024]{1,0:T(8,128)(2,1)S(1)}, u32[]{:S(2)}, u32[]{:S(2)}) collective-permute-start(bf16[48,1024]{1,0:T(8,128)(2,1)S(1)} %constant_dynamic-update-slice_fusion.refs_1_), channel_id=1, source_target_pairs={{0,18},{2,16},{4,22},{6,20},{8,26},{10,24},{12,30},{14,28},{16,2},... | collective-permute-start | bytes 294920 | tf_op jit(solution)/shard_map/ppermute | solution.py:44
  95.4 6.0 %collective-permute-start.29 = (bf16[48,1152]{1,0:T(8,128)(2,1)S(1)}, bf16[48,1152]{1,0:T(8,128)(2,1)S(1)}, u32[]{:S(2)}, u32[]{:S(2)}) collective-permute-start(bf16[48,1152]{1,0:T(8,128)(2,1)S(1)} %get-tuple-element.50), channel_id=1, source_target_pairs={{0,2},{2,0},{4,6},{6,4},{8,10},{10,8},{12,14},{14,12},{16,18},{18,... | collective-permute-start | bytes 331784 | tf_op jit(solution)/shard_map/ppermute | solution.py:44
  96.7 5.1 %collective-permute-start.30 = (bf16[48,1152]{1,0:T(8,128)(2,1)S(1)}, bf16[48,1152]{1,0:T(8,128)(2,1)S(1)}, u32[]{:S(2)}, u32[]{:S(2)}) collective-permute-start(bf16[48,1152]{1,0:T(8,128)(2,1)S(1)} %get-tuple-element.51), channel_id=1, source_target_pairs={{0,16},{2,18},{4,20},{6,22},{8,24},{10,26},{12,28},{14,30},{16,0},... | collective-permute-start | bytes 331784 | tf_op jit(solution)/shard_map/ppermute | solution.py:44
  97.5 5.8 %collective-permute-start.31 = (bf16[48,1152]{1,0:T(8,128)(2,1)S(1)}, bf16[48,1152]{1,0:T(8,128)(2,1)S(1)}, u32[]{:S(2)}, u32[]{:S(2)}) collective-permute-start(bf16[48,1152]{1,0:T(8,128)(2,1)S(1)} %get-tuple-element.52), channel_id=1, source_target_pairs={{0,18},{2,16},{4,22},{6,20},{8,26},{10,24},{12,30},{14,28},{16,2},... | collective-permute-start | bytes 331784 | tf_op jit(solution)/shard_map/ppermute | solution.py:44
  (14 other events, 206.2 us)

commit v2 on v1

--- a/solution.py
+++ b/solution.py
@@ -56,8 +56,7 @@
         params = pltpu.CompilerParams(vmem_limit_bytes=limit << 20)
     specs = [pl.BlockSpec(memory_space=pltpu.SMEM)] * len(scalars)
     specs += [pl.BlockSpec(memory_space=pltpu.VMEM)] * len(operands)
-    specs += [pl.BlockSpec(memory_space=pltpu.HBM)] * len(far)
-    far = [pltpu.with_memory_space_constraint(x, pltpu.HBM) for x in far]
+    specs += [pl.BlockSpec(memory_space=pl.ANY)] * len(far)
     return pl.pallas_call(
         kernel,
         in_specs=specs,
@@ -223,7 +222,7 @@
         copy.wait()
 
 
-def head_kernel(flags, came, other, w_out, out, out_head, sem):
+def head_kernel(flags, came, other, w_out, out, sem):
     head, quarter = w_out.shape[0], out.shape[1]
     half_rows = came.shape[0]
     own = pl.ds(pl.multiple_of(flags[1] * head, head), head)
@@ -234,7 +233,6 @@
         at = (1 - flags[1]) * head + (flags[0] ^ i) * half_rows
         out[pl.ds(pl.multiple_of(at, half_rows), half_rows)] = piece[...]
     copy.wait()
-    out_head[...] = out[pl.ds(pl.multiple_of(flags[0] * head, head), head)]
 
 
 def project_kernel(peers, split, flags, *refs):
@@ -246,13 +244,12 @@
     for at in range(0, width, step):
         parts = [p[:, at : at + step] for p in pieces]
         if split:
-            own, outer, outer2, near, near2, far, far2, last, last2 = parts
+            own, outer, outer2, inside, inside2, last, last2 = parts
             pick = lambda flag, a, b: jnp.where(flag, a, b)
-            heads = lambda a, b: jnp.concatenate([pick(low, a, b), pick(low, b, a)], axis=0)
             parts = [
                 own,
-                pick(inner, pick(low, outer2, outer), heads(near, near2)),
-                pick(inner, pick(low, outer, outer2), heads(far, far2)),
+                pick(inner, pick(low, outer2, outer), pick(low, inside, inside2)),
+                pick(inner, pick(low, outer, outer2), pick(low, inside2, inside)),
                 pick(low == inner, last2, last),
             ]
         total = plain(rows, jnp.concatenate(parts, axis=0))
@@ -316,7 +313,7 @@
         [],
         [pltpu.SemaphoreType.DMA((4,))],
         pltpu.VMEM if short else pl.ANY,
-        [w_query, *turned_kv, w_out],
+        [pltpu.with_memory_space_constraint(x, pltpu.HBM) for x in (w_query, *turned_kv, w_out)],
     )
     came_q = swap_tp(share_q, 1)
     cross_q = swap_in_slab(came_q, 1, 0)
@@ -330,21 +327,20 @@
     )[0]
 
     in_order = lambda a, b, flag: [jnp.where(flag, a, b), jnp.where(flag, b, a)]
-    out_own, out_head = call(
+    out_own = call(
         head_kernel,
-        [((2 * head_dim, quarter), jnp.bfloat16), ((head_dim, quarter), jnp.bfloat16)],
+        [((2 * head_dim, quarter), jnp.bfloat16)],
         [flags],
         [out_came, out_other],
         [pltpu.SemaphoreType.DMA(())],
         far=[w_out],
-    )
+    )[0]
     if short:
         is_outer = lambda t: not is_inner(t)
         out_outer = swap_by_core(out_own, (4, 2), is_outer)
-        out_near = swap_by_core(out_head, (2, 2), is_inner)
-        out_far = swap_by_core(out_head, (4, 4), is_inner)
-        held = [out_outer, swap_sp(out_outer), out_near, swap_sp(out_near)]
-        held += [out_far, swap_sp(out_far)]
+        out_inner = swap_by_core(out_own, (2, 4), is_inner)
+        held = [out_outer, swap_sp(out_outer)]
+        held += [out_inner, swap_sp(out_inner)]
 
     count = slabs * rows
     half_head = head_dim // 2
@@ -373,8 +369,8 @@
         [queries] + every,
         limit=16 if short else 56,
     )
+
     mixed = list(mixed)
-
     if short:
         out_outer, mixed[1] = fence(out_outer, mixed[1])
         out_sent = jnp.where(core_low, out_outer, out_own)
@@ -390,8 +386,9 @@
         pieces = [out_own, *held, out_last, swap_sp(out_last)]
     else:
         pieces = [out_own]
+        mine_of = lax.dynamic_slice_in_dim(out_own, sp_place * head_dim, head_dim, 0)
         for k in range(1, slabs):
-            piece = swap_tp(out_head, 2 * k)
+            piece = swap_tp(mine_of, 2 * k)
             both = in_order(piece, swap_sp(piece), core_low)
             pieces.append(jnp.concatenate(both, axis=0))
     outs = call(

time: 105 us -> 103 us (0.981)
  starting transfers between devices: 37.2 us -> 35.8 us
    ppermute x4 -> x3, waiting for transfers between devices: 12.1 us -> 0.01 us  [swap_by_core(): return lax.ppermute(block, ('tp', 'sp'), route)]
    ppermute x11, waiting for transfers between devices: 27.2 us -> 36.8 us  [swap_tp(): return lax.ppermute(block, 'tp', route)]
    ppermute x7, waiting for transfers between devices: 12.9 us -> 17 us  [swap_in_slab(): return lax.ppermute(block, ('groups', 'tp'), route)]
    ppermute x10 -> x9, waiting for transfers between devices: 1.95 us -> 0.65 us  [swap_sp(): return lax.ppermute(block, 'sp', [(s, s ^ 1) for s in range(count)])]
    ppermute x4 -> x3, starting transfers between devices: 8.6 us -> 7.31 us  [swap_by_core(): return lax.ppermute(block, ('tp', 'sp'), route)]
  transfers between devices with their start and end apart: 32 -> 30, of which waited for: 14 -> 12; matrix products, arithmetic and copies ran while one was open for 0% -> 0% of each run, Pallas kernels for 8% -> 7%
where the time goes in v2:
time: 103 us
  waiting for transfers between devices  54.5 us (53%)
  starting transfers between devices  35.8 us (35%)
  Pallas kernels  12.1 us (12%)
    ppermute x11, waiting for transfers between devices, swap_tp(): return lax.ppermute(block, 'tp', route)  36.8 us
    ppermute x11, starting transfers between devices, swap_tp(): return lax.ppermute(block, 'tp', route)  18 us
    ppermute x7, waiting for transfers between devices, swap_in_slab(): return lax.ppermute(block, ('groups', 'tp'), route)  17 us
    pallas_call x8, Pallas kernels, call(): pl.pallas_call(kernel, in_specs=specs, out_specs=[pl.BlockSpec(memory_spa...  12.1 us
    ppermute x7, starting transfers between devices, swap_in_slab(): return lax.ppermute(block, ('groups', 'tp'), route)  9.39 us
    ppermute x3, starting transfers between devices, swap_by_core(): return lax.ppermute(block, ('tp', 'sp'), route)  7.31 us
  transfers between devices with their start and end apart: 30, of which 12 were waited for; matrix products, arithmetic and copies ran while one was open for 0% of the time, Pallas kernels for 7%

profile of v2, /device:TPU:0, one launch (start us, length us, event | category | flops | bytes accessed | tf_op | source)
XLA Modules:
  0.0 102.9 jit_solution(12562932593663690366)
XLA Ops:
  0.1 1.9 %shard_map.73 = (bf16[1152,128]{1,0:T(8,128)(2,1)S(1)}, bf16[128,2304]{1,0:T(8,128)(2,1)S(1)}, bf16[64,1152]{1,0:T(8,128)(2,1)S(1)}) custom-call(s32[6]{0:T(128)S(1)} %stack.31.flags.refs_0_, bf16[4608,128]{1,0:T(8,128)(2,1)} %refs_0_.3, bf16[64,4608]{1,0:T(8,128)(2,1)} %bitcast.8, bf16[64,4608]{1,0:T(8,128)(2,1)} %bitcast.11, bf16[128,4608]{1,0:T(8,128)(2,1)} %w_out.3), custom_call_target="tpu_custom_call" | custom-call | tf_op jit(solution)/shard_map/pallas_call | solution.py:60
  2.0 3.1 %collective-permute-start.2 = (bf16[128,2304]{1,0:T(8,128)(2,1)S(1)}, bf16[128,2304]{1,0:T(8,128)(2,1)S(1)}, u32[]{:S(2)}, u32[]{:S(2)}) collective-permute-start(bf16[128,2304]{1,0:T(8,128)(2,1)S(1)} %get-tuple-element.29), channel_id=1, source_target_pairs={{0,2},{2,0},{4,6},{6,4},{8,10},{10,8},{12,14},{14,12},{1,3},{3,1},... | collective-permute-start | bytes 1769480 | tf_op jit(solution)/shard_map/ppermute | solution.py:17
  5.1 1.9 %collective-permute-start.13 = (bf16[64,1152]{1,0:T(8,128)(2,1)S(1)}, bf16[64,1152]{1,0:T(8,128)(2,1)S(1)}, u32[]{:S(2)}, u32[]{:S(2)}) collective-permute-start(bf16[64,1152]{1,0:T(8,128)(2,1)S(1)} %get-tuple-element.36), channel_id=1, source_target_pairs={{0,2},{2,0},{4,6},{6,4},{8,10},{10,8},{12,14},{14,12},{1,3},{3,1},... | collective-permute-start | bytes 442376 | tf_op jit(solution)/shard_map/ppermute | solution.py:17
  7.1 2.6 %collective-permute-start.1 = (bf16[48,4608]{1,0:T(8,128)(2,1)S(1)}, bf16[48,4608]{1,0:T(8,128)(2,1)S(1)}, u32[]{:S(2)}, u32[]{:S(2)}) collective-permute-start(bf16[48,4608]{1,0:T(8,128)(2,1)S(1)} %copy-done.4), channel_id=1, source_target_pairs={{0,8},{2,10},{4,12},{6,14},{8,0},{10,2},{12,4},{14,6},{1,9},{3,11}... | collective-permute-start | bytes 1327112 | tf_op jit(solution)/shard_map/ppermute | solution.py:17
  9.7 1.6 %collective-permute-start = (bf16[48,4608]{1,0:T(8,128)(2,1)S(1)}, bf16[48,4608]{1,0:T(8,128)(2,1)S(1)}, u32[]{:S(2)}, u32[]{:S(2)}) collective-permute-start(bf16[48,4608]{1,0:T(8,128)(2,1)S(1)} %copy-done.4), channel_id=1, source_target_pairs={{0,4},{2,6},{4,0},{6,2},{8,12},{10,14},{12,8},{14,10},{1,5},{3,7},... | collective-permute-start | bytes 1327112 | tf_op jit(solution)/shard_map/ppermute | solution.py:17
  11.3 16.6 %collective-permute-done.13.came = bf16[64,1152]{1,0:T(8,128)(2,1)S(1)} collective-permute-done((bf16[64,1152]{1,0:T(8,128)(2,1)S(1)}, bf16[64,1152]{1,0:T(8,128)(2,1)S(1)}, u32[]{:S(2)}, u32[]{:S(2)}) %collective-permute-start.13) | collective-permute-done | bytes 147488 | tf_op jit(solution)/shard_map/ppermute | solution.py:17
  27.9 1.7 %collective-permute-start.5 = (bf16[1152,128]{1,0:T(8,128)(2,1)S(1)}, bf16[1152,128]{1,0:T(8,128)(2,1)S(1)}, u32[]{:S(2)}, u32[]{:S(2)}) collective-permute-start(bf16[1152,128]{1,0:T(8,128)(2,1)S(1)} %collective-permute-done.4.refs_8_.refs_5_), channel_id=1, source_target_pairs={{0,16},{2,18},{4,20},{6,22},{8,24},{10,26},{12,28},{14,30},{16,0},... | collective-permute-start | bytes 884744 | tf_op jit(solution)/shard_map/ppermute | solution.py:44
  32.7 4.6 %collective-permute-done.5.refs_9_.refs_6_ = bf16[1152,128]{1,0:T(8,128)(2,1)S(1)} collective-permute-done((bf16[1152,128]{1,0:T(8,128)(2,1)S(1)}, bf16[1152,128]{1,0:T(8,128)(2,1)S(1)}, u32[]{:S(2)}, u32[]{:S(2)}) %collective-permute-start.5) | collective-permute-done | bytes 294944 | tf_op jit(solution)/shard_map/ppermute | solution.py:44
  37.3 4.7 %collective-permute-start.15 = (bf16[256,1152]{1,0:T(8,128)(2,1)S(1)}, bf16[256,1152]{1,0:T(8,128)(2,1)S(1)}, u32[]{:S(2)}, u32[]{:S(2)}) collective-permute-start(bf16[256,1152]{1,0:T(8,128)(2,1)S(1)} %shard_map.78.refs_5_), channel_id=1, source_target_pairs={{0,8},{1,5},{2,10},{3,7},{12,4},{13,9},{14,6},{15,11},{16,24},{17,... | collective-permute-start | bytes 1769480 | tf_op jit(solution)/shard_map/ppermute | solution.py:33
  43.7 2.1 %shard_map.74.early = f32[144,512]{1,0:T(8,128)S(1)} custom-call(s32[6]{0:T(128)S(1)} %stack.31.flags.refs_0_, bf16[48,4608]{1,0:T(8,128)(2,1)S(1)} %copy-done.4, bf16[48,4608]{1,0:T(8,128)(2,1)S(1)} %collective-permute-done.refs_1_, bf16[48,4608]{1,0:T(8,128)(2,1)S(1)} %collective-permute-done.1.refs_2_, bf16[4608,128]{1,0:T(8,128)(2,1)S(1)} %copy-done, ...), custom_call_target="tpu_custom_call" | custom-call | tf_op jit(solution)/shard_map/pallas_call | solution.py:60
  46.7 2.0 %shard_map.76 = (bf16[384,128]{1,0:T(8,128)(2,1)S(1)}, bf16[192,256]{1,0:T(8,128)(2,1)S(1)}) custom-call(s32[6]{0:T(128)S(1)} %stack.31.flags.refs_0_, f32[144,512]{1,0:T(8,128)S(1)} %shard_map.74.early, bf16[48,4608]{1,0:T(8,128)(2,1)S(1)} %collective-permute-done.8.middle, bf16[48,4608]{1,0:T(8,128)(2,1)S(1)} %collective-permute-done.9.relayed, ...), custom_call_target="tpu_custom_call" | custom-call | tf_op jit(solution)/shard_map/pallas_call | solution.py:60
  48.7 1.6 %collective-permute-start.10 = (bf16[192,256]{1,0:T(8,128)(2,1)S(1)}, bf16[192,256]{1,0:T(8,128)(2,1)S(1)}, u32[]{:S(2)}, u32[]{:S(2)}) collective-permute-start(bf16[192,256]{1,0:T(8,128)(2,1)S(1)} %get-tuple-element.34.refs_3_), channel_id=1, source_target_pairs={{0,2},{2,0},{4,6},{6,4},{8,10},{10,8},{12,14},{14,12},{1,3},{3,1},... | collective-permute-start | bytes 294920 | tf_op jit(solution)/shard_map/ppermute | solution.py:17
  50.3 3.1 %collective-permute-done.10.refs_4_ = bf16[192,256]{1,0:T(8,128)(2,1)S(1)} collective-permute-done((bf16[192,256]{1,0:T(8,128)(2,1)S(1)}, bf16[192,256]{1,0:T(8,128)(2,1)S(1)}, u32[]{:S(2)}, u32[]{:S(2)}) %collective-permute-start.10) | collective-permute-done | bytes 98336 | tf_op jit(solution)/shard_map/ppermute | solution.py:17
  54.7 1.8 %shard_map.77 = (bf16[48,256]{1,0:T(8,128)(2,1)S(1)}, bf16[48,256]{1,0:T(8,128)(2,1)S(1)}, bf16[48,256]{1,0:T(8,128)(2,1)S(1)}, bf16[48,256]{1,0:T(8,128)(2,1)S(1)}) custom-call(s32[6]{0:T(128)S(1)} %stack.31.flags.refs_0_, s32[8]{0:T(128)S(1)} %copy-done.5, bf16[384,128]{1,0:T(8,128)(2,1)S(1)} %get-tuple-element.33.refs_2_, ...), custom_call_target="tpu_custom_call" | custom-call | tf_op jit(solution)/shard_map/pallas_call | solution.py:60
  58.0 2.8 %collective-permute-start.16 = (bf16[48,256]{1,0:T(8,128)(2,1)S(1)}, bf16[48,256]{1,0:T(8,128)(2,1)S(1)}, u32[]{:S(2)}, u32[]{:S(2)}) collective-permute-start(bf16[48,256]{1,0:T(8,128)(2,1)S(1)} %get-tuple-element.38), channel_id=1, source_target_pairs={{0,4},{2,6},{4,0},{6,2},{8,12},{10,14},{12,8},{14,10},{1,5},{3,7},... | collective-permute-start | bytes 73736 | tf_op jit(solution)/shard_map/ppermute | solution.py:17
  61.2 2.0 %collective-permute-start.18 = (bf16[48,256]{1,0:T(8,128)(2,1)S(1)}, bf16[48,256]{1,0:T(8,128)(2,1)S(1)}, u32[]{:S(2)}, u32[]{:S(2)}) collective-permute-start(bf16[48,256]{1,0:T(8,128)(2,1)S(1)} %get-tuple-element.40), channel_id=1, source_target_pairs={{0,12},{2,14},{4,8},{6,10},{8,4},{10,6},{12,0},{14,2},{1,13},{3,15... | collective-permute-start | bytes 73736 | tf_op jit(solution)/shard_map/ppermute | solution.py:17
  63.2 16.2 %collective-permute-done.16 = bf16[48,256]{1,0:T(8,128)(2,1)S(1)} collective-permute-done((bf16[48,256]{1,0:T(8,128)(2,1)S(1)}, bf16[48,256]{1,0:T(8,128)(2,1)S(1)}, u32[]{:S(2)}, u32[]{:S(2)}) %collective-permute-start.16) | collective-permute-done | bytes 24608 | tf_op jit(solution)/shard_map/ppermute | solution.py:17
  81.3 2.8 %collective-permute-done.21.refs_3_ = bf16[48,1024]{1,0:T(8,128)(2,1)S(1)} collective-permute-done((bf16[48,1024]{1,0:T(8,128)(2,1)S(1)}, bf16[48,1024]{1,0:T(8,128)(2,1)S(1)}, u32[]{:S(2)}, u32[]{:S(2)}) %collective-permute-start.21) | collective-permute-done | bytes 98336 | tf_op jit(solution)/shard_map/ppermute | solution.py:44
  84.1 1.5 %collective-permute-start.19 = (bf16[48,1024]{1,0:T(8,128)(2,1)S(1)}, bf16[48,1024]{1,0:T(8,128)(2,1)S(1)}, u32[]{:S(2)}, u32[]{:S(2)}) collective-permute-start(bf16[48,1024]{1,0:T(8,128)(2,1)S(1)} %constant_dynamic-update-slice_fusion.refs_1_), channel_id=1, source_target_pairs={{0,2},{2,0},{4,6},{6,4},{8,10},{10,8},{12,14},{14,12},{16,18},{18,... | collective-permute-start | bytes 294920 | tf_op jit(solution)/shard_map/ppermute | solution.py:44
  86.9 3.6 %collective-permute-done.19.refs_2_ = bf16[48,1024]{1,0:T(8,128)(2,1)S(1)} collective-permute-done((bf16[48,1024]{1,0:T(8,128)(2,1)S(1)}, bf16[48,1024]{1,0:T(8,128)(2,1)S(1)}, u32[]{:S(2)}, u32[]{:S(2)}) %collective-permute-start.19) | collective-permute-done | bytes 98336 | tf_op jit(solution)/shard_map/ppermute | solution.py:44
  91.5 1.4 %shard_map.79 = (bf16[48,1152]{1,0:T(8,128)(2,1)S(1)}, bf16[48,1152]{1,0:T(8,128)(2,1)S(1)}, bf16[48,1152]{1,0:T(8,128)(2,1)S(1)}, bf16[48,1152]{1,0:T(8,128)(2,1)S(1)}) custom-call(s32[6]{0:T(128)S(1)} %stack.31.flags.refs_0_, bf16[48,1024]{1,0:T(8,128)(2,1)S(1)} %constant_dynamic-update-slice_fusion.refs_1_, ...), custom_call_target="tpu_custom_call" | custom-call | tf_op jit(solution)/shard_map/pallas_call | solution.py:60
  92.9 1.6 %collective-permute-start.27 = (bf16[48,1152]{1,0:T(8,128)(2,1)S(1)}, bf16[48,1152]{1,0:T(8,128)(2,1)S(1)}, u32[]{:S(2)}, u32[]{:S(2)}) collective-permute-start(bf16[48,1152]{1,0:T(8,128)(2,1)S(1)} %get-tuple-element.46), channel_id=1, source_target_pairs={{0,2},{2,0},{4,6},{6,4},{8,10},{10,8},{12,14},{14,12},{16,18},{18,... | collective-permute-start | bytes 331784 | tf_op jit(solution)/shard_map/ppermute | solution.py:44
  97.7 2.3 %collective-permute-done.28.refs_2_ = bf16[48,1152]{1,0:T(8,128)(2,1)S(1)} collective-permute-done((bf16[48,1152]{1,0:T(8,128)(2,1)S(1)}, bf16[48,1152]{1,0:T(8,128)(2,1)S(1)}, u32[]{:S(2)}, u32[]{:S(2)}) %collective-permute-start.28) | collective-permute-done | bytes 110624 | tf_op jit(solution)/shard_map/ppermute | solution.py:44
  100.0 1.6 %collective-permute-done.29.refs_3_ = bf16[48,1152]{1,0:T(8,128)(2,1)S(1)} collective-permute-done((bf16[48,1152]{1,0:T(8,128)(2,1)S(1)}, bf16[48,1152]{1,0:T(8,128)(2,1)S(1)}, u32[]{:S(2)}, u32[]{:S(2)}) %collective-permute-start.29) | collective-permute-done | bytes 110624 | tf_op jit(solution)/shard_map/ppermute | solution.py:44
  (64 shorter events, 17.7 us)
Async XLA Ops:
  2.0 27.8 %collective-permute-start.2 = (bf16[128,2304]{1,0:T(8,128)(2,1)S(1)}, bf16[128,2304]{1,0:T(8,128)(2,1)S(1)}, u32[]{:S(2)}, u32[]{:S(2)}) collective-permute-start(bf16[128,2304]{1,0:T(8,128)(2,1)S(1)} %get-tuple-element.29), channel_id=1, source_target_pairs={{0,2},{2,0},{4,6},{6,4},{8,10},{10,8},{12,14},{14,12},{1,3},{3,1},... | collective-permute-start | bytes 1769480 | tf_op jit(solution)/shard_map/ppermute | solution.py:17
  5.1 22.8 %collective-permute-start.4 = (bf16[1152,128]{1,0:T(8,128)(2,1)S(1)}, bf16[1152,128]{1,0:T(8,128)(2,1)S(1)}, u32[]{:S(2)}, u32[]{:S(2)}) collective-permute-start(bf16[1152,128]{1,0:T(8,128)(2,1)S(1)} %get-tuple-element.30), channel_id=1, source_target_pairs={{0,2},{2,0},{4,6},{6,4},{8,10},{10,8},{12,14},{14,12},{1,3},{3,1},... | collective-permute-start | bytes 884744 | tf_op jit(solution)/shard_map/ppermute | solution.py:17
  5.1 22.7 %collective-permute-start.13 = (bf16[64,1152]{1,0:T(8,128)(2,1)S(1)}, bf16[64,1152]{1,0:T(8,128)(2,1)S(1)}, u32[]{:S(2)}, u32[]{:S(2)}) collective-permute-start(bf16[64,1152]{1,0:T(8,128)(2,1)S(1)} %get-tuple-element.36), channel_id=1, source_target_pairs={{0,2},{2,0},{4,6},{6,4},{8,10},{10,8},{12,14},{14,12},{1,3},{3,1},... | collective-permute-start | bytes 442376 | tf_op jit(solution)/shard_map/ppermute | solution.py:17
  7.1 23.0 %collective-permute-start.1 = (bf16[48,4608]{1,0:T(8,128)(2,1)S(1)}, bf16[48,4608]{1,0:T(8,128)(2,1)S(1)}, u32[]{:S(2)}, u32[]{:S(2)}) collective-permute-start(bf16[48,4608]{1,0:T(8,128)(2,1)S(1)} %copy-done.4), channel_id=1, source_target_pairs={{0,8},{2,10},{4,12},{6,14},{8,0},{10,2},{12,4},{14,6},{1,9},{3,11}... | collective-permute-start | bytes 1327112 | tf_op jit(solution)/shard_map/ppermute | solution.py:17
  9.7 21.1 %collective-permute-start = (bf16[48,4608]{1,0:T(8,128)(2,1)S(1)}, bf16[48,4608]{1,0:T(8,128)(2,1)S(1)}, u32[]{:S(2)}, u32[]{:S(2)}) collective-permute-start(bf16[48,4608]{1,0:T(8,128)(2,1)S(1)} %copy-done.4), channel_id=1, source_target_pairs={{0,4},{2,6},{4,0},{6,2},{8,12},{10,14},{12,8},{14,10},{1,5},{3,7},... | collective-permute-start | bytes 1327112 | tf_op jit(solution)/shard_map/ppermute | solution.py:17
  27.9 9.4 %collective-permute-start.5 = (bf16[1152,128]{1,0:T(8,128)(2,1)S(1)}, bf16[1152,128]{1,0:T(8,128)(2,1)S(1)}, u32[]{:S(2)}, u32[]{:S(2)}) collective-permute-start(bf16[1152,128]{1,0:T(8,128)(2,1)S(1)} %collective-permute-done.4.refs_8_.refs_5_), channel_id=1, source_target_pairs={{0,16},{2,18},{4,20},{6,22},{8,24},{10,26},{12,28},{14,30},{16,0},... | collective-permute-start | bytes 884744 | tf_op jit(solution)/shard_map/ppermute | solution.py:44
  29.6 12.5 %collective-permute-start.6 = (bf16[1152,128]{1,0:T(8,128)(2,1)S(1)}, bf16[1152,128]{1,0:T(8,128)(2,1)S(1)}, u32[]{:S(2)}, u32[]{:S(2)}) collective-permute-start(bf16[1152,128]{1,0:T(8,128)(2,1)S(1)} %collective-permute-done.4.refs_8_.refs_5_), channel_id=1, source_target_pairs={{0,1},{1,0},{2,3},{3,2},{4,5},{5,4},{6,7},{7,6},{8,9},{9,8},{10,11... | collective-permute-start | bytes 884744 | tf_op jit(solution)/shard_map/ppermute | solution.py:22
  29.8 13.9 %collective-permute-start.3 = (bf16[128,2304]{1,0:T(8,128)(2,1)S(1)}, bf16[128,2304]{1,0:T(8,128)(2,1)S(1)}, u32[]{:S(2)}, u32[]{:S(2)}) collective-permute-start(bf16[128,2304]{1,0:T(8,128)(2,1)S(1)} %collective-permute-done.2.refs_6_.refs_3_), channel_id=1, source_target_pairs={{0,1},{1,0},{2,3},{3,2},{4,5},{5,4},{6,7},{7,6},{8,9},{9,8},{10,11... | collective-permute-start | bytes 1769480 | tf_op jit(solution)/shard_map/ppermute | solution.py:22
  30.1 15.8 %collective-permute-start.8 = (bf16[48,4608]{1,0:T(8,128)(2,1)S(1)}, bf16[48,4608]{1,0:T(8,128)(2,1)S(1)}, u32[]{:S(2)}, u32[]{:S(2)}) collective-permute-start(bf16[48,4608]{1,0:T(8,128)(2,1)S(1)} %copy-done.4), channel_id=1, source_target_pairs={{4,8},{6,10},{8,4},{10,6},{5,9},{7,11},{9,5},{11,7},{20,24},{22,26... | collective-permute-start | bytes 1327112 | tf_op jit(solution)/shard_map/ppermute | solution.py:17
  30.8 15.9 %collective-permute-start.9 = (bf16[48,4608]{1,0:T(8,128)(2,1)S(1)}, bf16[48,4608]{1,0:T(8,128)(2,1)S(1)}, u32[]{:S(2)}, u32[]{:S(2)}) collective-permute-start(bf16[48,4608]{1,0:T(8,128)(2,1)S(1)} %collective-permute-done.1.refs_2_), channel_id=1, source_target_pairs={{4,0},{6,2},{8,12},{10,14},{5,1},{7,3},{9,13},{11,15},{20,16},{22,... | collective-permute-start | bytes 1327112 | tf_op jit(solution)/shard_map/ppermute | solution.py:17
  37.3 19.3 %collective-permute-start.15 = (bf16[256,1152]{1,0:T(8,128)(2,1)S(1)}, bf16[256,1152]{1,0:T(8,128)(2,1)S(1)}, u32[]{:S(2)}, u32[]{:S(2)}) collective-permute-start(bf16[256,1152]{1,0:T(8,128)(2,1)S(1)} %shard_map.78.refs_5_), channel_id=1, source_target_pairs={{0,8},{1,5},{2,10},{3,7},{12,4},{13,9},{14,6},{15,11},{16,24},{17,... | collective-permute-start | bytes 1769480 | tf_op jit(solution)/shard_map/ppermute | solution.py:33
  53.4 27.4 %collective-permute-start.24 = (bf16[256,1152]{1,0:T(8,128)(2,1)S(1)}, bf16[256,1152]{1,0:T(8,128)(2,1)S(1)}, u32[]{:S(2)}, u32[]{:S(2)}) collective-permute-start(bf16[256,1152]{1,0:T(8,128)(2,1)S(1)} %shard_map.78.refs_5_), channel_id=1, source_target_pairs={{4,0},{5,13},{6,2},{7,15},{8,12},{9,1},{10,14},{11,3},{20,16},{21,... | collective-permute-start | bytes 1769480 | tf_op jit(solution)/shard_map/ppermute | solution.py:33
  56.7 27.5 %collective-permute-start.20 = (bf16[256,1152]{1,0:T(8,128)(2,1)S(1)}, bf16[256,1152]{1,0:T(8,128)(2,1)S(1)}, u32[]{:S(2)}, u32[]{:S(2)}) collective-permute-start(bf16[256,1152]{1,0:T(8,128)(2,1)S(1)} %broadcast_select_fusion), channel_id=1, source_target_pairs={{4,0},{5,9},{6,2},{7,11},{8,12},{9,5},{10,14},{11,7},{20,16},{21,2... | collective-permute-start | bytes 1769480 | tf_op jit(solution)/shard_map/ppermute | solution.py:33
  58.0 21.4 %collective-permute-start.16 = (bf16[48,256]{1,0:T(8,128)(2,1)S(1)}, bf16[48,256]{1,0:T(8,128)(2,1)S(1)}, u32[]{:S(2)}, u32[]{:S(2)}) collective-permute-start(bf16[48,256]{1,0:T(8,128)(2,1)S(1)} %get-tuple-element.38), channel_id=1, source_target_pairs={{0,4},{2,6},{4,0},{6,2},{8,12},{10,14},{12,8},{14,10},{1,5},{3,7},... | collective-permute-start | bytes 73736 | tf_op jit(solution)/shard_map/ppermute | solution.py:17
  60.7 18.7 %collective-permute-start.17 = (bf16[48,256]{1,0:T(8,128)(2,1)S(1)}, bf16[48,256]{1,0:T(8,128)(2,1)S(1)}, u32[]{:S(2)}, u32[]{:S(2)}) collective-permute-start(bf16[48,256]{1,0:T(8,128)(2,1)S(1)} %get-tuple-element.39), channel_id=1, source_target_pairs={{0,8},{2,10},{4,12},{6,14},{8,0},{10,2},{12,4},{14,6},{1,9},{3,11}... | collective-permute-start | bytes 73736 | tf_op jit(solution)/shard_map/ppermute | solution.py:17
  61.2 18.2 %collective-permute-start.18 = (bf16[48,256]{1,0:T(8,128)(2,1)S(1)}, bf16[48,256]{1,0:T(8,128)(2,1)S(1)}, u32[]{:S(2)}, u32[]{:S(2)}) collective-permute-start(bf16[48,256]{1,0:T(8,128)(2,1)S(1)} %get-tuple-element.40), channel_id=1, source_target_pairs={{0,12},{2,14},{4,8},{6,10},{8,4},{10,6},{12,0},{14,2},{1,13},{3,15... | collective-permute-start | bytes 73736 | tf_op jit(solution)/shard_map/ppermute | solution.py:17
  80.8 6.1 %collective-permute-start.23 = (bf16[256,1152]{1,0:T(8,128)(2,1)S(1)}, bf16[256,1152]{1,0:T(8,128)(2,1)S(1)}, u32[]{:S(2)}, u32[]{:S(2)}) collective-permute-start(bf16[256,1152]{1,0:T(8,128)(2,1)S(1)} %collective-permute-done.15.refs_6_), channel_id=1, source_target_pairs={{0,1},{1,0},{2,3},{3,2},{4,5},{5,4},{6,7},{7,6},{8,9},{9,8},{10,11... | collective-permute-start | bytes 1769480 | tf_op jit(solution)/shard_map/ppermute | solution.py:22
  80.8 6.1 %collective-permute-start.25 = (bf16[256,1152]{1,0:T(8,128)(2,1)S(1)}, bf16[256,1152]{1,0:T(8,128)(2,1)S(1)}, u32[]{:S(2)}, u32[]{:S(2)}) collective-permute-start(bf16[256,1152]{1,0:T(8,128)(2,1)S(1)} %collective-permute-done.24.refs_8_), channel_id=1, source_target_pairs={{0,1},{1,0},{2,3},{3,2},{4,5},{5,4},{6,7},{7,6},{8,9},{9,8},{10,11... | collective-permute-start | bytes 1769480 | tf_op jit(solution)/shard_map/ppermute | solution.py:22
  84.1 7.4 %collective-permute-start.26 = (bf16[256,1152]{1,0:T(8,128)(2,1)S(1)}, bf16[256,1152]{1,0:T(8,128)(2,1)S(1)}, u32[]{:S(2)}, u32[]{:S(2)}) collective-permute-start(bf16[256,1152]{1,0:T(8,128)(2,1)S(1)} %collective-permute-done.20.refs_10_), channel_id=1, source_target_pairs={{0,1},{1,0},{2,3},{3,2},{4,5},{5,4},{6,7},{7,6},{8,9},{9,8},{10,11... | collective-permute-start | bytes 1769480 | tf_op jit(solution)/shard_map/ppermute | solution.py:22
  84.1 6.4 %collective-permute-start.19 = (bf16[48,1024]{1,0:T(8,128)(2,1)S(1)}, bf16[48,1024]{1,0:T(8,128)(2,1)S(1)}, u32[]{:S(2)}, u32[]{:S(2)}) collective-permute-start(bf16[48,1024]{1,0:T(8,128)(2,1)S(1)} %constant_dynamic-update-slice_fusion.refs_1_), channel_id=1, source_target_pairs={{0,2},{2,0},{4,6},{6,4},{8,10},{10,8},{12,14},{14,12},{16,18},{18,... | collective-permute-start | bytes 294920 | tf_op jit(solution)/shard_map/ppermute | solution.py:44
  85.6 5.8 %collective-permute-start.22 = (bf16[48,1024]{1,0:T(8,128)(2,1)S(1)}, bf16[48,1024]{1,0:T(8,128)(2,1)S(1)}, u32[]{:S(2)}, u32[]{:S(2)}) collective-permute-start(bf16[48,1024]{1,0:T(8,128)(2,1)S(1)} %constant_dynamic-update-slice_fusion.refs_1_), channel_id=1, source_target_pairs={{0,18},{2,16},{4,22},{6,20},{8,26},{10,24},{12,30},{14,28},{16,2},... | collective-permute-start | bytes 294920 | tf_op jit(solution)/shard_map/ppermute | solution.py:44
  92.9 4.8 %collective-permute-start.27 = (bf16[48,1152]{1,0:T(8,128)(2,1)S(1)}, bf16[48,1152]{1,0:T(8,128)(2,1)S(1)}, u32[]{:S(2)}, u32[]{:S(2)}) collective-permute-start(bf16[48,1152]{1,0:T(8,128)(2,1)S(1)} %get-tuple-element.46), channel_id=1, source_target_pairs={{0,2},{2,0},{4,6},{6,4},{8,10},{10,8},{12,14},{14,12},{16,18},{18,... | collective-permute-start | bytes 331784 | tf_op jit(solution)/shard_map/ppermute | solution.py:44
  94.5 5.5 %collective-permute-start.28 = (bf16[48,1152]{1,0:T(8,128)(2,1)S(1)}, bf16[48,1152]{1,0:T(8,128)(2,1)S(1)}, u32[]{:S(2)}, u32[]{:S(2)}) collective-permute-start(bf16[48,1152]{1,0:T(8,128)(2,1)S(1)} %get-tuple-element.47), channel_id=1, source_target_pairs={{0,16},{2,18},{4,20},{6,22},{8,24},{10,26},{12,28},{14,30},{16,0},... | collective-permute-start | bytes 331784 | tf_op jit(solution)/shard_map/ppermute | solution.py:44
  95.8 5.8 %collective-permute-start.29 = (bf16[48,1152]{1,0:T(8,128)(2,1)S(1)}, bf16[48,1152]{1,0:T(8,128)(2,1)S(1)}, u32[]{:S(2)}, u32[]{:S(2)}) collective-permute-start(bf16[48,1152]{1,0:T(8,128)(2,1)S(1)} %get-tuple-element.48), channel_id=1, source_target_pairs={{0,18},{2,16},{4,22},{6,20},{8,26},{10,24},{12,30},{14,28},{16,2},... | collective-permute-start | bytes 331784 | tf_op jit(solution)/shard_map/ppermute | solution.py:44
  (13 other events, 232.7 us)

commit v3 on v2

--- a/solution.py
+++ b/solution.py
@@ -22,7 +22,7 @@
     return lax.ppermute(block, "sp", [(s, s ^ 1) for s in range(count)])
 
 
-def swap_by_core(block, flips, only):
+def swap_by_core(block, flips, only=lambda t: True):
     count, cores = lax.axis_size("tp"), lax.axis_size("sp")
     route = [
         (t * cores + s, (t ^ flips[s]) * cores + s)
@@ -98,8 +98,11 @@
     return own_query, own_kv, pair_query, pair_kv
 
 
-def early_kernel(flags, *refs):
-    blocks, weights, out = refs[:-10], refs[-10:-1], refs[-1]
+def early_kernel(short, flags, *refs):
+    blocks, weights, (out, near) = list(refs[:-11]), refs[-11:-2], refs[-2:]
+    if short:
+        near[...] = jnp.where(flags[2] != 0, blocks[1][...], blocks[2][...])
+        blocks[1:3] = [near]
     head = weights[0].shape[1]
     for i, part in enumerate(products(blocks, weights, flags[0], flags[3])):
         out[:, i * head : (i + 1) * head] = part
@@ -240,18 +243,11 @@
     count, width = outs[0].shape
     rows = jnp.concatenate([m[...] for m in stacked], axis=0)
     step = 384 if width % 384 == 0 else width
-    low, inner = flags[0] == 0, flags[2] != 0
+    received = flags[2] != flags[0]
     for at in range(0, width, step):
         parts = [p[:, at : at + step] for p in pieces]
         if split:
-            own, outer, outer2, inside, inside2, last, last2 = parts
-            pick = lambda flag, a, b: jnp.where(flag, a, b)
-            parts = [
-                own,
-                pick(inner, pick(low, outer2, outer), pick(low, inside, inside2)),
-                pick(inner, pick(low, outer, outer2), pick(low, inside2, inside)),
-                pick(low == inner, last2, last),
-            ]
+            parts[-2:] = [jnp.where(received, parts[-2], parts[-1])]
         total = plain(rows, jnp.concatenate(parts, axis=0))
         for i, out in enumerate(outs):
             out[:, at : at + step] = total[i * count : (i + 1) * count].astype(out.dtype)
@@ -284,11 +280,13 @@
     is_inner = lambda t: (t >> 1) in (1, 2)
 
     if short:
+        is_outer = lambda t: not is_inner(t)
+        near_out = swap_tp(tokens, 2, is_outer)
         far = swap_tp(tokens, 4)
-        near = swap_tp(tokens, 2)
+        near_in = swap_tp(tokens, 2, is_inner)
         middle = swap_tp(tokens, 6, is_inner)
         relayed = swap_tp(far, 2, is_inner)
-        firsts, last = [tokens, near, far], [middle, relayed]
+        firsts, last = [tokens, near_out, near_in, far], [middle, relayed]
     else:
         came = [swap_tp(tokens, 2 * k) for k in range(1, slabs)]
         firsts, last = [tokens] + came[:-1], [came[-1], came[-1]]
@@ -323,7 +321,11 @@
     weights = [w_query, *turned_kv, came_kv, swap_sp(came_kv), came_q, cross_q]
     weights += [swap_sp(came_q), swap_sp(cross_q)]
     early = call(
-        early_kernel, [((len(firsts) * rows, 4 * head_dim), jnp.float32)], [flags], firsts + weights
+        lambda *refs: early_kernel(short, *refs),
+        [(((slabs - 1) * rows, 4 * head_dim), jnp.float32)],
+        [flags],
+        firsts + weights,
+        [pltpu.VMEM((rows, width), jnp.bfloat16)],
     )[0]
 
     in_order = lambda a, b, flag: [jnp.where(flag, a, b), jnp.where(flag, b, a)]
@@ -336,11 +338,8 @@
         far=[w_out],
     )[0]
     if short:
-        is_outer = lambda t: not is_inner(t)
-        out_outer = swap_by_core(out_own, (4, 2), is_outer)
-        out_inner = swap_by_core(out_own, (2, 4), is_inner)
-        held = [out_outer, swap_sp(out_outer)]
-        held += [out_inner, swap_sp(out_inner)]
+        out_first = swap_by_core(out_own, (2, 4))
+        out_swapped = swap_sp(out_first)
 
     count = slabs * rows
     half_head = head_dim // 2
@@ -370,20 +369,19 @@
         limit=16 if short else 56,
     )
 
-    mixed = list(mixed)
-    if short:
-        out_outer, mixed[1] = fence(out_outer, mixed[1])
-        out_sent = jnp.where(core_low, out_outer, out_own)
     parts = [mixed[0]]
     for k in range(1, slabs):
         parts.append(swap_tp(mixed[k], 2 * k))
+    if short:
+        parts[1:3] = in_order(parts[1], parts[2], core_low)
     merged = jnp.concatenate(parts, axis=1)
     peers = ((0, 0), (0, 1), (1, 0), (1, 1))
     stacked = [merged] + [swap_in_slab(merged, g, t) for g, t in peers[1:]]
     if short:
-        out_last = swap_by_core(out_sent, (2, 6), is_inner)
+        out_sent = jnp.where(core_low, out_own, out_first)
+        out_last = swap_by_core(out_sent, (6, 2), is_inner)
         out_last, stacked[2] = fence(out_last, stacked[2])
-        pieces = [out_own, *held, out_last, swap_sp(out_last)]
+        pieces = [out_own, out_first, out_swapped, out_last, swap_sp(out_last)]
     else:
         pieces = [out_own]
         mine_of = lax.dynamic_slice_in_dim(out_own, sp_place * head_dim, head_dim, 0)

time: 103 us -> 116 us (1.13)
  waiting for transfers between devices: 54.5 us -> 69.3 us
  starting transfers between devices: 35.8 us -> 33.7 us
    ppermute x11 -> x12, waiting for transfers between devices: 36.8 us -> 53.4 us  [swap_tp(): return lax.ppermute(block, 'tp', route)]
    ppermute x3 -> x2, starting transfers between devices: 7.31 us -> 2.34 us  [swap_by_core(): return lax.ppermute(block, ('tp', 'sp'), route)]
    ppermute x7, waiting for transfers between devices: 17 us -> 12.7 us  [swap_in_slab(): return lax.ppermute(block, ('groups', 'tp'), route)]
    ppermute x11 -> x12, starting transfers between devices: 18 us -> 21.1 us  [swap_tp(): return lax.ppermute(block, 'tp', route)]
    ppermute x9 -> x8, waiting for transfers between devices: 0.65 us -> 3.31 us  [swap_sp(): return lax.ppermute(block, 'sp', [(s, s ^ 1) for s in range(count)])]
  transfers between devices with their start and end apart: 30 -> 29, of which waited for: 12 -> 15; matrix products, arithmetic and copies ran while one was open for 0% -> 0% of each run, Pallas kernels for 7% -> 6%
where the time goes in v3:
time: 116 us; the launch traced here: 115 us
  waiting for transfers between devices  69.3 us (60%)
  starting transfers between devices  33.7 us (29%)
  Pallas kernels  12 us (10%)
    ppermute x12, waiting for transfers between devices, swap_tp(): return lax.ppermute(block, 'tp', route)  53.4 us
    ppermute x12, starting transfers between devices, swap_tp(): return lax.ppermute(block, 'tp', route)  21.1 us
    ppermute x7, waiting for transfers between devices, swap_in_slab(): return lax.ppermute(block, ('groups', 'tp'), route)  12.7 us
    pallas_call x8, Pallas kernels, call(): pl.pallas_call(kernel, in_specs=specs, out_specs=[pl.BlockSpec(memory_spa...  12 us
    ppermute x7, starting transfers between devices, swap_in_slab(): return lax.ppermute(block, ('groups', 'tp'), route)  9.57 us
    ppermute x8, waiting for transfers between devices, swap_sp(): return lax.ppermute(block, 'sp', [(s, s ^ 1) for s in range(count)])  3.31 us
    ppermute x2, starting transfers between devices, swap_by_core(): return lax.ppermute(block, ('tp', 'sp'), route)  2.34 us
  transfers between devices with their start and end apart: 29, of which 15 were waited for; matrix products, arithmetic and copies ran while one was open for 0% of the time, Pallas kernels for 6%

profile of v3, /device:TPU:0, one launch (start us, length us, event | category | flops | bytes accessed | tf_op | source)
XLA Modules:
  0.0 115.5 jit_solution(9438479127652088808)
XLA Ops:
  0.1 1.9 %shard_map.73 = (bf16[1152,128]{1,0:T(8,128)(2,1)S(1)}, bf16[128,2304]{1,0:T(8,128)(2,1)S(1)}, bf16[64,1152]{1,0:T(8,128)(2,1)S(1)}) custom-call(s32[6]{0:T(128)S(1)} %stack.31.flags.refs_0_, bf16[4608,128]{1,0:T(8,128)(2,1)} %refs_0_.1, bf16[64,4608]{1,0:T(8,128)(2,1)} %bitcast.8, bf16[64,4608]{1,0:T(8,128)(2,1)} %bitcast.11, bf16[128,4608]{1,0:T(8,128)(2,1)} %w_out.3), custom_call_target="tpu_custom_call" | custom-call | tf_op jit(solution)/shard_map/pallas_call | solution.py:60
  2.0 3.1 %collective-permute-start.3 = (bf16[128,2304]{1,0:T(8,128)(2,1)S(1)}, bf16[128,2304]{1,0:T(8,128)(2,1)S(1)}, u32[]{:S(2)}, u32[]{:S(2)}) collective-permute-start(bf16[128,2304]{1,0:T(8,128)(2,1)S(1)} %get-tuple-element.27), channel_id=1, source_target_pairs={{0,2},{2,0},{4,6},{6,4},{8,10},{10,8},{12,14},{14,12},{1,3},{3,1},... | collective-permute-start | bytes 1769480 | tf_op jit(solution)/shard_map/ppermute | solution.py:17
  5.1 3.9 %collective-permute-start = (bf16[48,4608]{1,0:T(8,128)(2,1)S(1)}, bf16[48,4608]{1,0:T(8,128)(2,1)S(1)}, u32[]{:S(2)}, u32[]{:S(2)}) collective-permute-start(bf16[48,4608]{1,0:T(8,128)(2,1)S(1)} %copy-done.4), channel_id=1, source_target_pairs={{0,4},{2,6},{12,8},{14,10},{1,5},{3,7},{13,9},{15,11},{16,20},{18,... | collective-permute-start | bytes 1327112 | tf_op jit(solution)/shard_map/ppermute | solution.py:17
  9.1 1.6 %collective-permute-start.18 = (bf16[64,1152]{1,0:T(8,128)(2,1)S(1)}, bf16[64,1152]{1,0:T(8,128)(2,1)S(1)}, u32[]{:S(2)}, u32[]{:S(2)}) collective-permute-start(bf16[64,1152]{1,0:T(8,128)(2,1)S(1)} %get-tuple-element.38), channel_id=1, source_target_pairs={{0,2},{2,0},{4,6},{6,4},{8,10},{10,8},{12,14},{14,12},{1,3},{3,1},... | collective-permute-start | bytes 442376 | tf_op jit(solution)/shard_map/ppermute | solution.py:17
  12.0 15.9 %collective-permute-done.18.came = bf16[64,1152]{1,0:T(8,128)(2,1)S(1)} collective-permute-done((bf16[64,1152]{1,0:T(8,128)(2,1)S(1)}, bf16[64,1152]{1,0:T(8,128)(2,1)S(1)}, u32[]{:S(2)}, u32[]{:S(2)}) %collective-permute-start.18) | collective-permute-done | bytes 147488 | tf_op jit(solution)/shard_map/ppermute | solution.py:17
  27.9 2.8 %collective-permute-start.2 = (bf16[48,4608]{1,0:T(8,128)(2,1)S(1)}, bf16[48,4608]{1,0:T(8,128)(2,1)S(1)}, u32[]{:S(2)}, u32[]{:S(2)}) collective-permute-start(bf16[48,4608]{1,0:T(8,128)(2,1)S(1)} %copy-done.4), channel_id=1, source_target_pairs={{0,8},{2,10},{4,12},{6,14},{8,0},{10,2},{12,4},{14,6},{1,9},{3,11}... | collective-permute-start | bytes 1327112 | tf_op jit(solution)/shard_map/ppermute | solution.py:17
  34.7 1.6 %collective-permute-start.20 = (bf16[256,1152]{1,0:T(8,128)(2,1)S(1)}, bf16[256,1152]{1,0:T(8,128)(2,1)S(1)}, u32[]{:S(2)}, u32[]{:S(2)}) collective-permute-start(bf16[256,1152]{1,0:T(8,128)(2,1)S(1)} %shard_map.78.refs_5_), channel_id=1, source_target_pairs={{0,4},{1,9},{2,6},{3,11},{4,0},{5,13},{6,2},{7,15},{8,12},{9,1},{1... | collective-permute-start | bytes 1769480 | tf_op jit(solution)/shard_map/ppermute | solution.py:33
  36.3 20.6 %collective-permute-done.2.refs_4_ = bf16[48,4608]{1,0:T(8,128)(2,1)S(1)} collective-permute-done((bf16[48,4608]{1,0:T(8,128)(2,1)S(1)}, bf16[48,4608]{1,0:T(8,128)(2,1)S(1)}, u32[]{:S(2)}, u32[]{:S(2)}) %collective-permute-start.2) | collective-permute-done | bytes 442400 | tf_op jit(solution)/shard_map/ppermute | solution.py:17
  60.6 2.1 %shard_map.74.early = f32[144,512]{1,0:T(8,128)S(1)} custom-call(s32[6]{0:T(128)S(1)} %stack.31.flags.refs_0_, bf16[48,4608]{1,0:T(8,128)(2,1)S(1)} %copy-done.4, bf16[48,4608]{1,0:T(8,128)(2,1)S(1)} %collective-permute-done.refs_2_, bf16[48,4608]{1,0:T(8,128)(2,1)S(1)} %collective-permute-done.1.refs_3_, ...), custom_call_target="tpu_custom_call" | custom-call | tf_op jit(solution)/shard_map/pallas_call | solution.py:60
  62.8 8.9 %collective-permute-done.10.relayed = bf16[48,4608]{1,0:T(8,128)(2,1)S(1)} collective-permute-done((bf16[48,4608]{1,0:T(8,128)(2,1)S(1)}, bf16[48,4608]{1,0:T(8,128)(2,1)S(1)}, u32[]{:S(2)}, u32[]{:S(2)}) %collective-permute-start.10) | collective-permute-done | bytes 442400 | tf_op jit(solution)/shard_map/ppermute | solution.py:17
  71.7 2.0 %shard_map.76 = (bf16[384,128]{1,0:T(8,128)(2,1)S(1)}, bf16[192,256]{1,0:T(8,128)(2,1)S(1)}) custom-call(s32[6]{0:T(128)S(1)} %stack.31.flags.refs_0_, f32[144,512]{1,0:T(8,128)S(1)} %shard_map.74.early, bf16[48,4608]{1,0:T(8,128)(2,1)S(1)} %collective-permute-done.9.middle, bf16[48,4608]{1,0:T(8,128)(2,1)S(1)} %collective-permute-done.10.relayed, ...), custom_call_target="tpu_custom_call" | custom-call | tf_op jit(solution)/shard_map/pallas_call | solution.py:60
  73.7 1.5 %collective-permute-start.11 = (bf16[192,256]{1,0:T(8,128)(2,1)S(1)}, bf16[192,256]{1,0:T(8,128)(2,1)S(1)}, u32[]{:S(2)}, u32[]{:S(2)}) collective-permute-start(bf16[192,256]{1,0:T(8,128)(2,1)S(1)} %get-tuple-element.32.refs_3_), channel_id=1, source_target_pairs={{0,2},{2,0},{4,6},{6,4},{8,10},{10,8},{12,14},{14,12},{1,3},{3,1},... | collective-permute-start | bytes 294920 | tf_op jit(solution)/shard_map/ppermute | solution.py:17
  76.1 2.3 %collective-permute-done.11.refs_4_ = bf16[192,256]{1,0:T(8,128)(2,1)S(1)} collective-permute-done((bf16[192,256]{1,0:T(8,128)(2,1)S(1)}, bf16[192,256]{1,0:T(8,128)(2,1)S(1)}, u32[]{:S(2)}, u32[]{:S(2)}) %collective-permute-start.11) | collective-permute-done | bytes 98336 | tf_op jit(solution)/shard_map/ppermute | solution.py:17
  79.7 1.8 %shard_map.77 = (bf16[48,256]{1,0:T(8,128)(2,1)S(1)}, bf16[48,256]{1,0:T(8,128)(2,1)S(1)}, bf16[48,256]{1,0:T(8,128)(2,1)S(1)}, bf16[48,256]{1,0:T(8,128)(2,1)S(1)}) custom-call(s32[6]{0:T(128)S(1)} %stack.31.flags.refs_0_, s32[8]{0:T(128)S(1)} %copy-done.5, bf16[384,128]{1,0:T(8,128)(2,1)S(1)} %get-tuple-element.31.refs_2_, ...), custom_call_target="tpu_custom_call" | custom-call | tf_op jit(solution)/shard_map/pallas_call | solution.py:60
  81.5 2.1 %collective-permute-start.14 = (bf16[48,256]{1,0:T(8,128)(2,1)S(1)}, bf16[48,256]{1,0:T(8,128)(2,1)S(1)}, u32[]{:S(2)}, u32[]{:S(2)}) collective-permute-start(bf16[48,256]{1,0:T(8,128)(2,1)S(1)} %get-tuple-element.35), channel_id=1, source_target_pairs={{0,4},{2,6},{4,0},{6,2},{8,12},{10,14},{12,8},{14,10},{1,5},{3,7},... | collective-permute-start | bytes 73736 | tf_op jit(solution)/shard_map/ppermute | solution.py:17
  83.6 2.8 %collective-permute-start.15 = (bf16[48,256]{1,0:T(8,128)(2,1)S(1)}, bf16[48,256]{1,0:T(8,128)(2,1)S(1)}, u32[]{:S(2)}, u32[]{:S(2)}) collective-permute-start(bf16[48,256]{1,0:T(8,128)(2,1)S(1)} %get-tuple-element.36), channel_id=1, source_target_pairs={{0,8},{2,10},{4,12},{6,14},{8,0},{10,2},{12,4},{14,6},{1,9},{3,11}... | collective-permute-start | bytes 73736 | tf_op jit(solution)/shard_map/ppermute | solution.py:17
  86.4 2.2 %collective-permute-done.15 = bf16[48,256]{1,0:T(8,128)(2,1)S(1)} collective-permute-done((bf16[48,256]{1,0:T(8,128)(2,1)S(1)}, bf16[48,256]{1,0:T(8,128)(2,1)S(1)}, u32[]{:S(2)}, u32[]{:S(2)}) %collective-permute-start.15) | collective-permute-done | bytes 24608 | tf_op jit(solution)/shard_map/ppermute | solution.py:17
  88.7 3.4 %collective-permute-done.16 = bf16[48,256]{1,0:T(8,128)(2,1)S(1)} collective-permute-done((bf16[48,256]{1,0:T(8,128)(2,1)S(1)}, bf16[48,256]{1,0:T(8,128)(2,1)S(1)}, u32[]{:S(2)}, u32[]{:S(2)}) %collective-permute-start.16) | collective-permute-done | bytes 24608 | tf_op jit(solution)/shard_map/ppermute | solution.py:17
  92.1 1.6 %collective-permute-start.22 = (bf16[48,1024]{1,0:T(8,128)(2,1)S(1)}, bf16[48,1024]{1,0:T(8,128)(2,1)S(1)}, u32[]{:S(2)}, u32[]{:S(2)}) collective-permute-start(bf16[48,1024]{1,0:T(8,128)(2,1)S(1)} %pad_maximum_fusion.refs_1_), channel_id=1, source_target_pairs={{0,16},{2,18},{4,20},{6,22},{8,24},{10,26},{12,28},{14,30},{16,0},... | collective-permute-start | bytes 294920 | tf_op jit(solution)/shard_map/ppermute | solution.py:44
  93.6 3.1 %collective-permute-done.22.refs_3_ = bf16[48,1024]{1,0:T(8,128)(2,1)S(1)} collective-permute-done((bf16[48,1024]{1,0:T(8,128)(2,1)S(1)}, bf16[48,1024]{1,0:T(8,128)(2,1)S(1)}, u32[]{:S(2)}, u32[]{:S(2)}) %collective-permute-start.22) | collective-permute-done | bytes 98336 | tf_op jit(solution)/shard_map/ppermute | solution.py:44
  99.7 3.4 %collective-permute-done.17.refs_2_ = bf16[48,1024]{1,0:T(8,128)(2,1)S(1)} collective-permute-done((bf16[48,1024]{1,0:T(8,128)(2,1)S(1)}, bf16[48,1024]{1,0:T(8,128)(2,1)S(1)}, u32[]{:S(2)}, u32[]{:S(2)}) %collective-permute-start.17) | collective-permute-done | bytes 98336 | tf_op jit(solution)/shard_map/ppermute | solution.py:44
  105.4 1.6 %collective-permute-start.26 = (bf16[48,1152]{1,0:T(8,128)(2,1)S(1)}, bf16[48,1152]{1,0:T(8,128)(2,1)S(1)}, u32[]{:S(2)}, u32[]{:S(2)}) collective-permute-start(bf16[48,1152]{1,0:T(8,128)(2,1)S(1)} %get-tuple-element.42), channel_id=1, source_target_pairs={{0,2},{2,0},{4,6},{6,4},{8,10},{10,8},{12,14},{14,12},{16,18},{18,... | collective-permute-start | bytes 331784 | tf_op jit(solution)/shard_map/ppermute | solution.py:44
  110.2 2.3 %collective-permute-done.27.refs_2_ = bf16[48,1152]{1,0:T(8,128)(2,1)S(1)} collective-permute-done((bf16[48,1152]{1,0:T(8,128)(2,1)S(1)}, bf16[48,1152]{1,0:T(8,128)(2,1)S(1)}, u32[]{:S(2)}, u32[]{:S(2)}) %collective-permute-start.27) | collective-permute-done | bytes 110624 | tf_op jit(solution)/shard_map/ppermute | solution.py:44
  112.5 1.6 %collective-permute-done.28.refs_3_ = bf16[48,1152]{1,0:T(8,128)(2,1)S(1)} collective-permute-done((bf16[48,1152]{1,0:T(8,128)(2,1)S(1)}, bf16[48,1152]{1,0:T(8,128)(2,1)S(1)}, u32[]{:S(2)}, u32[]{:S(2)}) %collective-permute-start.28) | collective-permute-done | bytes 110624 | tf_op jit(solution)/shard_map/ppermute | solution.py:44
  (60 shorter events, 21.1 us)
Async XLA Ops:
  2.0 31.6 %collective-permute-start.3 = (bf16[128,2304]{1,0:T(8,128)(2,1)S(1)}, bf16[128,2304]{1,0:T(8,128)(2,1)S(1)}, u32[]{:S(2)}, u32[]{:S(2)}) collective-permute-start(bf16[128,2304]{1,0:T(8,128)(2,1)S(1)} %get-tuple-element.27), channel_id=1, source_target_pairs={{0,2},{2,0},{4,6},{6,4},{8,10},{10,8},{12,14},{14,12},{1,3},{3,1},... | collective-permute-start | bytes 1769480 | tf_op jit(solution)/shard_map/ppermute | solution.py:17
  5.1 25.6 %collective-permute-start.5 = (bf16[1152,128]{1,0:T(8,128)(2,1)S(1)}, bf16[1152,128]{1,0:T(8,128)(2,1)S(1)}, u32[]{:S(2)}, u32[]{:S(2)}) collective-permute-start(bf16[1152,128]{1,0:T(8,128)(2,1)S(1)} %get-tuple-element.28), channel_id=1, source_target_pairs={{0,2},{2,0},{4,6},{6,4},{8,10},{10,8},{12,14},{14,12},{1,3},{3,1},... | collective-permute-start | bytes 884744 | tf_op jit(solution)/shard_map/ppermute | solution.py:17
  5.1 28.4 %collective-permute-start = (bf16[48,4608]{1,0:T(8,128)(2,1)S(1)}, bf16[48,4608]{1,0:T(8,128)(2,1)S(1)}, u32[]{:S(2)}, u32[]{:S(2)}) collective-permute-start(bf16[48,4608]{1,0:T(8,128)(2,1)S(1)} %copy-done.4), channel_id=1, source_target_pairs={{0,4},{2,6},{12,8},{14,10},{1,5},{3,7},{13,9},{15,11},{16,20},{18,... | collective-permute-start | bytes 1327112 | tf_op jit(solution)/shard_map/ppermute | solution.py:17
  9.1 18.8 %collective-permute-start.18 = (bf16[64,1152]{1,0:T(8,128)(2,1)S(1)}, bf16[64,1152]{1,0:T(8,128)(2,1)S(1)}, u32[]{:S(2)}, u32[]{:S(2)}) collective-permute-start(bf16[64,1152]{1,0:T(8,128)(2,1)S(1)} %get-tuple-element.38), channel_id=1, source_target_pairs={{0,2},{2,0},{4,6},{6,4},{8,10},{10,8},{12,14},{14,12},{1,3},{3,1},... | collective-permute-start | bytes 442376 | tf_op jit(solution)/shard_map/ppermute | solution.py:17
  10.7 24.0 %collective-permute-start.1 = (bf16[48,4608]{1,0:T(8,128)(2,1)S(1)}, bf16[48,4608]{1,0:T(8,128)(2,1)S(1)}, u32[]{:S(2)}, u32[]{:S(2)}) collective-permute-start(bf16[48,4608]{1,0:T(8,128)(2,1)S(1)} %copy-done.4), channel_id=1, source_target_pairs={{4,0},{6,2},{8,12},{10,14},{5,1},{7,3},{9,13},{11,15},{20,16},{22,... | collective-permute-start | bytes 1327112 | tf_op jit(solution)/shard_map/ppermute | solution.py:17
  27.9 29.1 %collective-permute-start.2 = (bf16[48,4608]{1,0:T(8,128)(2,1)S(1)}, bf16[48,4608]{1,0:T(8,128)(2,1)S(1)}, u32[]{:S(2)}, u32[]{:S(2)}) collective-permute-start(bf16[48,4608]{1,0:T(8,128)(2,1)S(1)} %copy-done.4), channel_id=1, source_target_pairs={{0,8},{2,10},{4,12},{6,14},{8,0},{10,2},{12,4},{14,6},{1,9},{3,11}... | collective-permute-start | bytes 1327112 | tf_op jit(solution)/shard_map/ppermute | solution.py:17
  32.1 25.6 %collective-permute-start.6 = (bf16[1152,128]{1,0:T(8,128)(2,1)S(1)}, bf16[1152,128]{1,0:T(8,128)(2,1)S(1)}, u32[]{:S(2)}, u32[]{:S(2)}) collective-permute-start(bf16[1152,128]{1,0:T(8,128)(2,1)S(1)} %collective-permute-done.5.refs_10_.refs_5_), channel_id=1, source_target_pairs={{0,16},{2,18},{4,20},{6,22},{8,24},{10,26},{12,28},{14,30},{16,0},... | collective-permute-start | bytes 884744 | tf_op jit(solution)/shard_map/ppermute | solution.py:44
  33.6 25.4 %collective-permute-start.7 = (bf16[1152,128]{1,0:T(8,128)(2,1)S(1)}, bf16[1152,128]{1,0:T(8,128)(2,1)S(1)}, u32[]{:S(2)}, u32[]{:S(2)}) collective-permute-start(bf16[1152,128]{1,0:T(8,128)(2,1)S(1)} %collective-permute-done.5.refs_10_.refs_5_), channel_id=1, source_target_pairs={{0,1},{1,0},{2,3},{3,2},{4,5},{5,4},{6,7},{7,6},{8,9},{9,8},{10,11... | collective-permute-start | bytes 884744 | tf_op jit(solution)/shard_map/ppermute | solution.py:22
  33.6 27.0 %collective-permute-start.4 = (bf16[128,2304]{1,0:T(8,128)(2,1)S(1)}, bf16[128,2304]{1,0:T(8,128)(2,1)S(1)}, u32[]{:S(2)}, u32[]{:S(2)}) collective-permute-start(bf16[128,2304]{1,0:T(8,128)(2,1)S(1)} %collective-permute-done.3.refs_8_.refs_3_), channel_id=1, source_target_pairs={{0,1},{1,0},{2,3},{3,2},{4,5},{5,4},{6,7},{7,6},{8,9},{9,8},{10,11... | collective-permute-start | bytes 1769480 | tf_op jit(solution)/shard_map/ppermute | solution.py:22
  34.7 40.5 %collective-permute-start.20 = (bf16[256,1152]{1,0:T(8,128)(2,1)S(1)}, bf16[256,1152]{1,0:T(8,128)(2,1)S(1)}, u32[]{:S(2)}, u32[]{:S(2)}) collective-permute-start(bf16[256,1152]{1,0:T(8,128)(2,1)S(1)} %shard_map.78.refs_5_), channel_id=1, source_target_pairs={{0,4},{1,9},{2,6},{3,11},{4,0},{5,13},{6,2},{7,15},{8,12},{9,1},{1... | collective-permute-start | bytes 1769480 | tf_op jit(solution)/shard_map/ppermute | solution.py:33
  57.0 5.8 %collective-permute-start.9 = (bf16[48,4608]{1,0:T(8,128)(2,1)S(1)}, bf16[48,4608]{1,0:T(8,128)(2,1)S(1)}, u32[]{:S(2)}, u32[]{:S(2)}) collective-permute-start(bf16[48,4608]{1,0:T(8,128)(2,1)S(1)} %copy-done.4), channel_id=1, source_target_pairs={{4,8},{6,10},{8,4},{10,6},{5,9},{7,11},{9,5},{11,7},{20,24},{22,26... | collective-permute-start | bytes 1327112 | tf_op jit(solution)/shard_map/ppermute | solution.py:17
  57.7 14.1 %collective-permute-start.10 = (bf16[48,4608]{1,0:T(8,128)(2,1)S(1)}, bf16[48,4608]{1,0:T(8,128)(2,1)S(1)}, u32[]{:S(2)}, u32[]{:S(2)}) collective-permute-start(bf16[48,4608]{1,0:T(8,128)(2,1)S(1)} %collective-permute-done.2.refs_4_), channel_id=1, source_target_pairs={{4,0},{6,2},{8,12},{10,14},{5,1},{7,3},{9,13},{11,15},{20,16},{22,... | collective-permute-start | bytes 1327112 | tf_op jit(solution)/shard_map/ppermute | solution.py:17
  73.7 4.7 %collective-permute-start.11 = (bf16[192,256]{1,0:T(8,128)(2,1)S(1)}, bf16[192,256]{1,0:T(8,128)(2,1)S(1)}, u32[]{:S(2)}, u32[]{:S(2)}) collective-permute-start(bf16[192,256]{1,0:T(8,128)(2,1)S(1)} %get-tuple-element.32.refs_3_), channel_id=1, source_target_pairs={{0,2},{2,0},{4,6},{6,4},{8,10},{10,8},{12,14},{14,12},{1,3},{3,1},... | collective-permute-start | bytes 294920 | tf_op jit(solution)/shard_map/ppermute | solution.py:17
  75.3 18.3 %collective-permute-start.21 = (bf16[256,1152]{1,0:T(8,128)(2,1)S(1)}, bf16[256,1152]{1,0:T(8,128)(2,1)S(1)}, u32[]{:S(2)}, u32[]{:S(2)}) collective-permute-start(bf16[256,1152]{1,0:T(8,128)(2,1)S(1)} %broadcast_select_fusion), channel_id=1, source_target_pairs={{4,8},{5,1},{6,10},{7,3},{8,4},{9,13},{10,6},{11,15},{20,24},{21,1... | collective-permute-start | bytes 1769480 | tf_op jit(solution)/shard_map/ppermute | solution.py:33
  81.5 4.9 %collective-permute-start.14 = (bf16[48,256]{1,0:T(8,128)(2,1)S(1)}, bf16[48,256]{1,0:T(8,128)(2,1)S(1)}, u32[]{:S(2)}, u32[]{:S(2)}) collective-permute-start(bf16[48,256]{1,0:T(8,128)(2,1)S(1)} %get-tuple-element.35), channel_id=1, source_target_pairs={{0,4},{2,6},{4,0},{6,2},{8,12},{10,14},{12,8},{14,10},{1,5},{3,7},... | collective-permute-start | bytes 73736 | tf_op jit(solution)/shard_map/ppermute | solution.py:17
  83.6 5.0 %collective-permute-start.15 = (bf16[48,256]{1,0:T(8,128)(2,1)S(1)}, bf16[48,256]{1,0:T(8,128)(2,1)S(1)}, u32[]{:S(2)}, u32[]{:S(2)}) collective-permute-start(bf16[48,256]{1,0:T(8,128)(2,1)S(1)} %get-tuple-element.36), channel_id=1, source_target_pairs={{0,8},{2,10},{4,12},{6,14},{8,0},{10,2},{12,4},{14,6},{1,9},{3,11}... | collective-permute-start | bytes 73736 | tf_op jit(solution)/shard_map/ppermute | solution.py:17
  86.4 5.6 %collective-permute-start.16 = (bf16[48,256]{1,0:T(8,128)(2,1)S(1)}, bf16[48,256]{1,0:T(8,128)(2,1)S(1)}, u32[]{:S(2)}, u32[]{:S(2)}) collective-permute-start(bf16[48,256]{1,0:T(8,128)(2,1)S(1)} %get-tuple-element.37), channel_id=1, source_target_pairs={{0,12},{2,14},{4,8},{6,10},{8,4},{10,6},{12,0},{14,2},{1,13},{3,15... | collective-permute-start | bytes 73736 | tf_op jit(solution)/shard_map/ppermute | solution.py:17
  93.6 6.1 %collective-permute-start.24 = (bf16[256,1152]{1,0:T(8,128)(2,1)S(1)}, bf16[256,1152]{1,0:T(8,128)(2,1)S(1)}, u32[]{:S(2)}, u32[]{:S(2)}) collective-permute-start(bf16[256,1152]{1,0:T(8,128)(2,1)S(1)} %collective-permute-done.20.refs_6_), channel_id=1, source_target_pairs={{0,1},{1,0},{2,3},{3,2},{4,5},{5,4},{6,7},{7,6},{8,9},{9,8},{10,11... | collective-permute-start | bytes 1769480 | tf_op jit(solution)/shard_map/ppermute | solution.py:22
  96.7 7.4 %collective-permute-start.25 = (bf16[256,1152]{1,0:T(8,128)(2,1)S(1)}, bf16[256,1152]{1,0:T(8,128)(2,1)S(1)}, u32[]{:S(2)}, u32[]{:S(2)}) collective-permute-start(bf16[256,1152]{1,0:T(8,128)(2,1)S(1)} %collective-permute-done.21.refs_8_), channel_id=1, source_target_pairs={{0,1},{1,0},{2,3},{3,2},{4,5},{5,4},{6,7},{7,6},{8,9},{9,8},{10,11... | collective-permute-start | bytes 1769480 | tf_op jit(solution)/shard_map/ppermute | solution.py:22
  96.7 6.4 %collective-permute-start.17 = (bf16[48,1024]{1,0:T(8,128)(2,1)S(1)}, bf16[48,1024]{1,0:T(8,128)(2,1)S(1)}, u32[]{:S(2)}, u32[]{:S(2)}) collective-permute-start(bf16[48,1024]{1,0:T(8,128)(2,1)S(1)} %pad_maximum_fusion.refs_1_), channel_id=1, source_target_pairs={{0,2},{2,0},{4,6},{6,4},{8,10},{10,8},{12,14},{14,12},{16,18},{18,... | collective-permute-start | bytes 294920 | tf_op jit(solution)/shard_map/ppermute | solution.py:44
  98.3 5.8 %collective-permute-start.23 = (bf16[48,1024]{1,0:T(8,128)(2,1)S(1)}, bf16[48,1024]{1,0:T(8,128)(2,1)S(1)}, u32[]{:S(2)}, u32[]{:S(2)}) collective-permute-start(bf16[48,1024]{1,0:T(8,128)(2,1)S(1)} %pad_maximum_fusion.refs_1_), channel_id=1, source_target_pairs={{0,18},{2,16},{4,22},{6,20},{8,26},{10,24},{12,30},{14,28},{16,2},... | collective-permute-start | bytes 294920 | tf_op jit(solution)/shard_map/ppermute | solution.py:44
  105.4 4.8 %collective-permute-start.26 = (bf16[48,1152]{1,0:T(8,128)(2,1)S(1)}, bf16[48,1152]{1,0:T(8,128)(2,1)S(1)}, u32[]{:S(2)}, u32[]{:S(2)}) collective-permute-start(bf16[48,1152]{1,0:T(8,128)(2,1)S(1)} %get-tuple-element.42), channel_id=1, source_target_pairs={{0,2},{2,0},{4,6},{6,4},{8,10},{10,8},{12,14},{14,12},{16,18},{18,... | collective-permute-start | bytes 331784 | tf_op jit(solution)/shard_map/ppermute | solution.py:44
  107.0 5.5 %collective-permute-start.27 = (bf16[48,1152]{1,0:T(8,128)(2,1)S(1)}, bf16[48,1152]{1,0:T(8,128)(2,1)S(1)}, u32[]{:S(2)}, u32[]{:S(2)}) collective-permute-start(bf16[48,1152]{1,0:T(8,128)(2,1)S(1)} %get-tuple-element.43), channel_id=1, source_target_pairs={{0,16},{2,18},{4,20},{6,22},{8,24},{10,26},{12,28},{14,30},{16,0},... | collective-permute-start | bytes 331784 | tf_op jit(solution)/shard_map/ppermute | solution.py:44
  108.5 5.6 %collective-permute-start.28 = (bf16[48,1152]{1,0:T(8,128)(2,1)S(1)}, bf16[48,1152]{1,0:T(8,128)(2,1)S(1)}, u32[]{:S(2)}, u32[]{:S(2)}) collective-permute-start(bf16[48,1152]{1,0:T(8,128)(2,1)S(1)} %get-tuple-element.44), channel_id=1, source_target_pairs={{0,18},{2,16},{4,22},{6,20},{8,26},{10,24},{12,30},{14,28},{16,2},... | collective-permute-start | bytes 331784 | tf_op jit(solution)/shard_map/ppermute | solution.py:44
  (12 other events, 291.3 us)

commit v4 on v1

--- a/solution.py
+++ b/solution.py
@@ -20,17 +20,6 @@
 def swap_sp(block):
     count = lax.axis_size("sp")
     return lax.ppermute(block, "sp", [(s, s ^ 1) for s in range(count)])
-
-
-def swap_by_core(block, flips, only):
-    count, cores = lax.axis_size("tp"), lax.axis_size("sp")
-    route = [
-        (t * cores + s, (t ^ flips[s]) * cores + s)
-        for t in range(count)
-        for s in range(cores)
-        if only(t)
-    ]
-    return lax.ppermute(block, ("tp", "sp"), route)
 
 
 def swap_in_slab(block, group_flip, tp_flip):
@@ -56,8 +45,7 @@
         params = pltpu.CompilerParams(vmem_limit_bytes=limit << 20)
     specs = [pl.BlockSpec(memory_space=pltpu.SMEM)] * len(scalars)
     specs += [pl.BlockSpec(memory_space=pltpu.VMEM)] * len(operands)
-    specs += [pl.BlockSpec(memory_space=pltpu.HBM)] * len(far)
-    far = [pltpu.with_memory_space_constraint(x, pltpu.HBM) for x in far]
+    specs += [pl.BlockSpec(memory_space=pl.ANY)] * len(far)
     return pl.pallas_call(
         kernel,
         in_specs=specs,
@@ -237,27 +225,27 @@
     out_head[...] = out[pl.ds(pl.multiple_of(flags[0] * head, head), head)]
 
 
-def project_kernel(peers, split, flags, *refs):
+def project_kernel(peers, flags, *refs):
     stacked, pieces, outs = refs[:peers], list(refs[peers:-peers]), refs[-peers:]
     count, width = outs[0].shape
     rows = jnp.concatenate([m[...] for m in stacked], axis=0)
     step = 384 if width % 384 == 0 else width
-    low, inner = flags[0] == 0, flags[2] != 0
+    low = flags[0] == 0
     for at in range(0, width, step):
-        parts = [p[:, at : at + step] for p in pieces]
-        if split:
-            own, outer, outer2, near, near2, far, far2, last, last2 = parts
-            pick = lambda flag, a, b: jnp.where(flag, a, b)
-            heads = lambda a, b: jnp.concatenate([pick(low, a, b), pick(low, b, a)], axis=0)
-            parts = [
-                own,
-                pick(inner, pick(low, outer2, outer), heads(near, near2)),
-                pick(inner, pick(low, outer, outer2), heads(far, far2)),
-                pick(low == inner, last2, last),
-            ]
+        tiles = [p[:, at : at + step] for p in pieces]
+        parts = tiles[:1]
+        for mine, other in zip(tiles[1::2], tiles[2::2]):
+            parts += [jnp.where(low, mine, other), jnp.where(low, other, mine)]
         total = plain(rows, jnp.concatenate(parts, axis=0))
         for i, out in enumerate(outs):
             out[:, at : at + step] = total[i * count : (i + 1) * count].astype(out.dtype)
+
+
+def merge_kernel(flags, *refs):
+    parts, out = refs[:-1], refs[-1]
+    width = parts[0].shape[1]
+    for i, part in enumerate(parts):
+        out[:, i * width : (i + 1) * width] = part[...]
 
 
 def assemble_kernel(flags, *refs):
@@ -303,8 +291,8 @@
     inner = ((slab == 1) | (slab == 2)).astype(jnp.int32)
     flags = jnp.stack([sp_place, side, inner, group, mine, slab]).astype(jnp.int32)
     turned_kv = [w_key.T, w_value.T]
-    core_low = sp_place == 0
-    flags, doc_lengths, core_low = fence(flags, doc_lengths, core_low)
+    is_inside = inner != 0
+    flags, doc_lengths, is_inside = fence(flags, doc_lengths, is_inside)
     share_q, share_kv, out_sent = call(
         cut_kernel,
         [
@@ -316,7 +304,7 @@
         [],
         [pltpu.SemaphoreType.DMA((4,))],
         pltpu.VMEM if short else pl.ANY,
-        [w_query, *turned_kv, w_out],
+        [pltpu.with_memory_space_constraint(x, pltpu.HBM) for x in (w_query, *turned_kv, w_out)],
     )
     came_q = swap_tp(share_q, 1)
     cross_q = swap_in_slab(came_q, 1, 0)
@@ -329,7 +317,6 @@
         early_kernel, [((len(firsts) * rows, 4 * head_dim), jnp.float32)], [flags], firsts + weights
     )[0]
 
-    in_order = lambda a, b, flag: [jnp.where(flag, a, b), jnp.where(flag, b, a)]
     out_own, out_head = call(
         head_kernel,
         [((2 * head_dim, quarter), jnp.bfloat16), ((head_dim, quarter), jnp.bfloat16)],
@@ -339,12 +326,8 @@
         far=[w_out],
     )
     if short:
-        is_outer = lambda t: not is_inner(t)
-        out_outer = swap_by_core(out_own, (4, 2), is_outer)
-        out_near = swap_by_core(out_head, (2, 2), is_inner)
-        out_far = swap_by_core(out_head, (4, 4), is_inner)
-        held = [out_outer, swap_sp(out_outer), out_near, swap_sp(out_near)]
-        held += [out_far, swap_sp(out_far)]
+        out_far = swap_tp(out_head, 4)
+        out_near = swap_tp(out_head, 2)
 
     count = slabs * rows
     half_head = head_dim // 2
@@ -373,29 +356,26 @@
         [queries] + every,
         limit=16 if short else 56,
     )
-    mixed = list(mixed)
-
-    if short:
-        out_outer, mixed[1] = fence(out_outer, mixed[1])
-        out_sent = jnp.where(core_low, out_outer, out_own)
+
     parts = [mixed[0]]
     for k in range(1, slabs):
         parts.append(swap_tp(mixed[k], 2 * k))
-    merged = jnp.concatenate(parts, axis=1)
+    shape = ((rows, slabs * 2 * head_dim), jnp.bfloat16)
+    merged = call(merge_kernel, [shape], [flags], parts)[0]
     peers = ((0, 0), (0, 1), (1, 0), (1, 1))
     stacked = [merged] + [swap_in_slab(merged, g, t) for g, t in peers[1:]]
     if short:
-        out_last = swap_by_core(out_sent, (2, 6), is_inner)
-        out_last, stacked[2] = fence(out_last, stacked[2])
-        pieces = [out_own, *held, out_last, swap_sp(out_last)]
+        out_relay = swap_tp(out_far, 2, is_inner)
+        out_middle = swap_tp(out_head, 6, is_inner)
+        out_relay, out_middle, stacked[2] = fence(out_relay, out_middle, stacked[2])
+        others = [out_near, out_far, jnp.where(is_inside, out_middle, out_relay)]
     else:
-        pieces = [out_own]
-        for k in range(1, slabs):
-            piece = swap_tp(out_head, 2 * k)
-            both = in_order(piece, swap_sp(piece), core_low)
-            pieces.append(jnp.concatenate(both, axis=0))
+        others = [swap_tp(out_head, 2 * k) for k in range(1, slabs)]
+    pieces = [out_own]
+    for piece in others:
+        pieces += [piece, swap_sp(piece)]
     outs = call(
-        lambda *refs: project_kernel(len(peers), short, *refs),
+        lambda *refs: project_kernel(len(peers), *refs),
         [((rows, quarter), jnp.bfloat16)] * len(peers),
         [flags],
         stacked + pieces,

time: 105 us -> 102 us (0.971)
  waiting for transfers between devices: 54.1 us -> 47.4 us
  starting transfers between devices: 37.2 us -> 40.9 us
    ppermute x11 -> x15, starting transfers between devices: 18 us -> 30.1 us  [swap_tp(): return lax.ppermute(block, 'tp', route)]
    ppermute x4 -> x0, waiting for transfers between devices: 12.1 us -> none  [swap_by_core(): return lax.ppermute(block, ('tp', 'sp'), route)]
    ppermute x4 -> x0, starting transfers between devices: 8.6 us -> none  [swap_by_core(): return lax.ppermute(block, ('tp', 'sp'), route)]
    ppermute x7, waiting for transfers between devices: 12.9 us -> 17.9 us  [swap_in_slab(): return lax.ppermute(block, ('groups', 'tp'), route)]
    ppermute x11 -> x15, waiting for transfers between devices: 27.2 us -> 28.5 us  [swap_tp(): return lax.ppermute(block, 'tp', route)]
    pallas_call x8 -> x9, Pallas kernels: 12.9 us -> 12.7 us  [call(): pl.pallas_call(kernel, in_specs=specs, out_specs=[pl.BlockSpec(memory_spa...]
  transfers between devices with their start and end apart: 32 -> 31, of which waited for: 14 -> 14; matrix products, arithmetic and copies ran while one was open for 0% -> 0% of each run, Pallas kernels for 8% -> 8%
where the time goes in v4:
time: 102 us; the launch traced here: 101 us
  waiting for transfers between devices  47.4 us (46%)
  starting transfers between devices  40.9 us (40%)
  Pallas kernels  12.7 us (12%)
    ppermute x15, starting transfers between devices, swap_tp(): return lax.ppermute(block, 'tp', route)  30.1 us
    ppermute x15, waiting for transfers between devices, swap_tp(): return lax.ppermute(block, 'tp', route)  28.5 us
    ppermute x7, waiting for transfers between devices, swap_in_slab(): return lax.ppermute(block, ('groups', 'tp'), route)  17.9 us
    pallas_call x9, Pallas kernels, call(): pl.pallas_call(kernel, in_specs=specs, out_specs=[pl.BlockSpec(memory_spa...  12.7 us
    ppermute x7, starting transfers between devices, swap_in_slab(): return lax.ppermute(block, ('groups', 'tp'), route)  9.12 us
  transfers between devices with their start and end apart: 31, of which 14 were waited for; matrix products, arithmetic and copies ran while one was open for 0% of the time, Pallas kernels for 8%

profile of v4, /device:TPU:0, one launch (start us, length us, event | category | flops | bytes accessed | tf_op | source)
XLA Modules:
  0.0 101.4 jit_solution(6627234074507878619)
XLA Ops:
  0.1 2.0 %shard_map.73 = (bf16[1152,128]{1,0:T(8,128)(2,1)S(1)}, bf16[128,2304]{1,0:T(8,128)(2,1)S(1)}, bf16[64,1152]{1,0:T(8,128)(2,1)S(1)}) custom-call(s32[6]{0:T(128)S(1)} %stack.27.flags.refs_0_, bf16[4608,128]{1,0:T(8,128)(2,1)} %refs_0_.3, bf16[64,4608]{1,0:T(8,128)(2,1)} %bitcast.8, bf16[64,4608]{1,0:T(8,128)(2,1)} %bitcast.11, bf16[128,4608]{1,0:T(8,128)(2,1)} %w_out.3), custom_call_target="tpu_custom_call" | custom-call | tf_op jit(solution)/shard_map/pallas_call | solution.py:49
  2.2 3.1 %collective-permute-start.2 = (bf16[128,2304]{1,0:T(8,128)(2,1)S(1)}, bf16[128,2304]{1,0:T(8,128)(2,1)S(1)}, u32[]{:S(2)}, u32[]{:S(2)}) collective-permute-start(bf16[128,2304]{1,0:T(8,128)(2,1)S(1)} %get-tuple-element.30), channel_id=1, source_target_pairs={{0,2},{2,0},{4,6},{6,4},{8,10},{10,8},{12,14},{14,12},{1,3},{3,1},... | collective-permute-start | bytes 1769480 | tf_op jit(solution)/shard_map/ppermute | solution.py:17
  5.3 3.0 %collective-permute-start.1 = (bf16[48,4608]{1,0:T(8,128)(2,1)S(1)}, bf16[48,4608]{1,0:T(8,128)(2,1)S(1)}, u32[]{:S(2)}, u32[]{:S(2)}) collective-permute-start(bf16[48,4608]{1,0:T(8,128)(2,1)S(1)} %copy-done.4), channel_id=1, source_target_pairs={{0,8},{2,10},{4,12},{6,14},{8,0},{10,2},{12,4},{14,6},{1,9},{3,11}... | collective-permute-start | bytes 1327112 | tf_op jit(solution)/shard_map/ppermute | solution.py:17
  8.3 1.6 %collective-permute-start = (bf16[48,4608]{1,0:T(8,128)(2,1)S(1)}, bf16[48,4608]{1,0:T(8,128)(2,1)S(1)}, u32[]{:S(2)}, u32[]{:S(2)}) collective-permute-start(bf16[48,4608]{1,0:T(8,128)(2,1)S(1)} %copy-done.4), channel_id=1, source_target_pairs={{0,4},{2,6},{4,0},{6,2},{8,12},{10,14},{12,8},{14,10},{1,5},{3,7},... | collective-permute-start | bytes 1327112 | tf_op jit(solution)/shard_map/ppermute | solution.py:17
  11.4 16.6 %collective-permute-done.17.came = bf16[64,1152]{1,0:T(8,128)(2,1)S(1)} collective-permute-done((bf16[64,1152]{1,0:T(8,128)(2,1)S(1)}, bf16[64,1152]{1,0:T(8,128)(2,1)S(1)}, u32[]{:S(2)}, u32[]{:S(2)}) %collective-permute-start.17) | collective-permute-done | bytes 147488 | tf_op jit(solution)/shard_map/ppermute | solution.py:17
  28.0 1.7 %collective-permute-start.5 = (bf16[1152,128]{1,0:T(8,128)(2,1)S(1)}, bf16[1152,128]{1,0:T(8,128)(2,1)S(1)}, u32[]{:S(2)}, u32[]{:S(2)}) collective-permute-start(bf16[1152,128]{1,0:T(8,128)(2,1)S(1)} %collective-permute-done.4.refs_8_.refs_5_), channel_id=1, source_target_pairs={{0,16},{2,18},{4,20},{6,22},{8,24},{10,26},{12,28},{14,30},{16,0},... | collective-permute-start | bytes 884744 | tf_op jit(solution)/shard_map/ppermute | solution.py:33
  32.3 5.2 %collective-permute-done.5.refs_9_.refs_6_ = bf16[1152,128]{1,0:T(8,128)(2,1)S(1)} collective-permute-done((bf16[1152,128]{1,0:T(8,128)(2,1)S(1)}, bf16[1152,128]{1,0:T(8,128)(2,1)S(1)}, u32[]{:S(2)}, u32[]{:S(2)}) %collective-permute-start.5) | collective-permute-done | bytes 294944 | tf_op jit(solution)/shard_map/ppermute | solution.py:33
  38.1 2.9 %collective-permute-start.19 = (bf16[128,1152]{1,0:T(8,128)(2,1)S(1)}, bf16[128,1152]{1,0:T(8,128)(2,1)S(1)}, u32[]{:S(2)}, u32[]{:S(2)}) collective-permute-start(bf16[128,1152]{1,0:T(8,128)(2,1)S(1)} %get-tuple-element.41), channel_id=1, source_target_pairs={{0,8},{2,10},{4,12},{6,14},{8,0},{10,2},{12,4},{14,6},{1,9},{3,11}... | collective-permute-start | bytes 884744 | tf_op jit(solution)/shard_map/ppermute | solution.py:17
  42.0 2.1 %shard_map.74.early = f32[144,512]{1,0:T(8,128)S(1)} custom-call(s32[6]{0:T(128)S(1)} %stack.27.flags.refs_0_, bf16[48,4608]{1,0:T(8,128)(2,1)S(1)} %copy-done.4, bf16[48,4608]{1,0:T(8,128)(2,1)S(1)} %collective-permute-done.refs_1_, bf16[48,4608]{1,0:T(8,128)(2,1)S(1)} %collective-permute-done.1.refs_2_, bf16[4608,128]{1,0:T(8,128)(2,1)S(1)} %copy-done, ...), custom_call_target="tpu_custom_call" | custom-call | tf_op jit(solution)/shard_map/pallas_call | solution.py:49
  44.1 2.8 %collective-permute-done.9.relayed = bf16[48,4608]{1,0:T(8,128)(2,1)S(1)} collective-permute-done((bf16[48,4608]{1,0:T(8,128)(2,1)S(1)}, bf16[48,4608]{1,0:T(8,128)(2,1)S(1)}, u32[]{:S(2)}, u32[]{:S(2)}) %collective-permute-start.9) | collective-permute-done | bytes 442400 | tf_op jit(solution)/shard_map/ppermute | solution.py:17
  46.9 2.0 %shard_map.76 = (bf16[384,128]{1,0:T(8,128)(2,1)S(1)}, bf16[192,256]{1,0:T(8,128)(2,1)S(1)}) custom-call(s32[6]{0:T(128)S(1)} %stack.27.flags.refs_0_, f32[144,512]{1,0:T(8,128)S(1)} %shard_map.74.early, bf16[48,4608]{1,0:T(8,128)(2,1)S(1)} %collective-permute-done.8.middle, bf16[48,4608]{1,0:T(8,128)(2,1)S(1)} %collective-permute-done.9.relayed, ...), custom_call_target="tpu_custom_call" | custom-call | tf_op jit(solution)/shard_map/pallas_call | solution.py:49
  48.9 1.6 %collective-permute-start.10 = (bf16[192,256]{1,0:T(8,128)(2,1)S(1)}, bf16[192,256]{1,0:T(8,128)(2,1)S(1)}, u32[]{:S(2)}, u32[]{:S(2)}) collective-permute-start(bf16[192,256]{1,0:T(8,128)(2,1)S(1)} %get-tuple-element.35.refs_3_), channel_id=1, source_target_pairs={{0,2},{2,0},{4,6},{6,4},{8,10},{10,8},{12,14},{14,12},{1,3},{3,1},... | collective-permute-start | bytes 294920 | tf_op jit(solution)/shard_map/ppermute | solution.py:17
  50.5 6.2 %collective-permute-start.24 = (bf16[128,1152]{1,0:T(8,128)(2,1)S(1)}, bf16[128,1152]{1,0:T(8,128)(2,1)S(1)}, u32[]{:S(2)}, u32[]{:S(2)}) collective-permute-start(bf16[128,1152]{1,0:T(8,128)(2,1)S(1)} %get-tuple-element.41), channel_id=1, source_target_pairs={{0,4},{2,6},{4,0},{6,2},{8,12},{10,14},{12,8},{14,10},{1,5},{3,7},... | collective-permute-start | bytes 884744 | tf_op jit(solution)/shard_map/ppermute | solution.py:17
  61.0 1.8 %shard_map.77 = (bf16[48,256]{1,0:T(8,128)(2,1)S(1)}, bf16[48,256]{1,0:T(8,128)(2,1)S(1)}, bf16[48,256]{1,0:T(8,128)(2,1)S(1)}, bf16[48,256]{1,0:T(8,128)(2,1)S(1)}) custom-call(s32[6]{0:T(128)S(1)} %stack.27.flags.refs_0_, s32[8]{0:T(128)S(1)} %copy-done.5, bf16[384,128]{1,0:T(8,128)(2,1)S(1)} %get-tuple-element.34.refs_2_, ...), custom_call_target="tpu_custom_call" | custom-call | tf_op jit(solution)/shard_map/pallas_call | solution.py:49
  62.9 2.7 %collective-permute-start.13 = (bf16[48,256]{1,0:T(8,128)(2,1)S(1)}, bf16[48,256]{1,0:T(8,128)(2,1)S(1)}, u32[]{:S(2)}, u32[]{:S(2)}) collective-permute-start(bf16[48,256]{1,0:T(8,128)(2,1)S(1)} %get-tuple-element.37), channel_id=1, source_target_pairs={{0,4},{2,6},{4,0},{6,2},{8,12},{10,14},{12,8},{14,10},{1,5},{3,7},... | collective-permute-start | bytes 73736 | tf_op jit(solution)/shard_map/ppermute | solution.py:17
  66.7 5.1 %collective-permute-done.13.refs_1_ = bf16[48,256]{1,0:T(8,128)(2,1)S(1)} collective-permute-done((bf16[48,256]{1,0:T(8,128)(2,1)S(1)}, bf16[48,256]{1,0:T(8,128)(2,1)S(1)}, u32[]{:S(2)}, u32[]{:S(2)}) %collective-permute-start.13) | collective-permute-done | bytes 24608 | tf_op jit(solution)/shard_map/ppermute | solution.py:17
  71.8 2.5 %collective-permute-start.15 = (bf16[48,256]{1,0:T(8,128)(2,1)S(1)}, bf16[48,256]{1,0:T(8,128)(2,1)S(1)}, u32[]{:S(2)}, u32[]{:S(2)}) collective-permute-start(bf16[48,256]{1,0:T(8,128)(2,1)S(1)} %get-tuple-element.39), channel_id=1, source_target_pairs={{0,12},{2,14},{4,8},{6,10},{8,4},{10,6},{12,0},{14,2},{1,13},{3,15... | collective-permute-start | bytes 73736 | tf_op jit(solution)/shard_map/ppermute | solution.py:17
  74.3 3.1 %collective-permute-done.15.refs_3_ = bf16[48,256]{1,0:T(8,128)(2,1)S(1)} collective-permute-done((bf16[48,256]{1,0:T(8,128)(2,1)S(1)}, bf16[48,256]{1,0:T(8,128)(2,1)S(1)}, u32[]{:S(2)}, u32[]{:S(2)}) %collective-permute-start.15) | collective-permute-done | bytes 24608 | tf_op jit(solution)/shard_map/ppermute | solution.py:17
  79.7 3.0 %collective-permute-done.22.refs_3_ = bf16[48,1024]{1,0:T(8,128)(2,1)S(1)} collective-permute-done((bf16[48,1024]{1,0:T(8,128)(2,1)S(1)}, bf16[48,1024]{1,0:T(8,128)(2,1)S(1)}, u32[]{:S(2)}, u32[]{:S(2)}) %collective-permute-start.22) | collective-permute-done | bytes 98336 | tf_op jit(solution)/shard_map/ppermute | solution.py:33
  82.8 1.6 %collective-permute-start.16 = (bf16[48,1024]{1,0:T(8,128)(2,1)S(1)}, bf16[48,1024]{1,0:T(8,128)(2,1)S(1)}, u32[]{:S(2)}, u32[]{:S(2)}) collective-permute-start(bf16[48,1024]{1,0:T(8,128)(2,1)S(1)} %shard_map.78.refs_1_), channel_id=1, source_target_pairs={{0,2},{2,0},{4,6},{6,4},{8,10},{10,8},{12,14},{14,12},{16,18},{18,... | collective-permute-start | bytes 294920 | tf_op jit(solution)/shard_map/ppermute | solution.py:33
  85.5 3.7 %collective-permute-done.16.refs_2_ = bf16[48,1024]{1,0:T(8,128)(2,1)S(1)} collective-permute-done((bf16[48,1024]{1,0:T(8,128)(2,1)S(1)}, bf16[48,1024]{1,0:T(8,128)(2,1)S(1)}, u32[]{:S(2)}, u32[]{:S(2)}) %collective-permute-start.16) | collective-permute-done | bytes 98336 | tf_op jit(solution)/shard_map/ppermute | solution.py:33
  91.5 1.6 %collective-permute-start.28 = (bf16[48,1152]{1,0:T(8,128)(2,1)S(1)}, bf16[48,1152]{1,0:T(8,128)(2,1)S(1)}, u32[]{:S(2)}, u32[]{:S(2)}) collective-permute-start(bf16[48,1152]{1,0:T(8,128)(2,1)S(1)} %get-tuple-element.48), channel_id=1, source_target_pairs={{0,2},{2,0},{4,6},{6,4},{8,10},{10,8},{12,14},{14,12},{16,18},{18,... | collective-permute-start | bytes 331784 | tf_op jit(solution)/shard_map/ppermute | solution.py:33
  96.3 2.2 %collective-permute-done.29.refs_2_ = bf16[48,1152]{1,0:T(8,128)(2,1)S(1)} collective-permute-done((bf16[48,1152]{1,0:T(8,128)(2,1)S(1)}, bf16[48,1152]{1,0:T(8,128)(2,1)S(1)}, u32[]{:S(2)}, u32[]{:S(2)}) %collective-permute-start.29) | collective-permute-done | bytes 110624 | tf_op jit(solution)/shard_map/ppermute | solution.py:33
  98.5 1.6 %collective-permute-done.30.refs_3_ = bf16[48,1152]{1,0:T(8,128)(2,1)S(1)} collective-permute-done((bf16[48,1152]{1,0:T(8,128)(2,1)S(1)}, bf16[48,1152]{1,0:T(8,128)(2,1)S(1)}, u32[]{:S(2)}, u32[]{:S(2)}) %collective-permute-start.30) | collective-permute-done | bytes 110624 | tf_op jit(solution)/shard_map/ppermute | solution.py:33
  (63 shorter events, 21.6 us)
Async XLA Ops:
  2.2 27.6 %collective-permute-start.2 = (bf16[128,2304]{1,0:T(8,128)(2,1)S(1)}, bf16[128,2304]{1,0:T(8,128)(2,1)S(1)}, u32[]{:S(2)}, u32[]{:S(2)}) collective-permute-start(bf16[128,2304]{1,0:T(8,128)(2,1)S(1)} %get-tuple-element.30), channel_id=1, source_target_pairs={{0,2},{2,0},{4,6},{6,4},{8,10},{10,8},{12,14},{14,12},{1,3},{3,1},... | collective-permute-start | bytes 1769480 | tf_op jit(solution)/shard_map/ppermute | solution.py:17
  5.2 22.8 %collective-permute-start.4 = (bf16[1152,128]{1,0:T(8,128)(2,1)S(1)}, bf16[1152,128]{1,0:T(8,128)(2,1)S(1)}, u32[]{:S(2)}, u32[]{:S(2)}) collective-permute-start(bf16[1152,128]{1,0:T(8,128)(2,1)S(1)} %get-tuple-element.31), channel_id=1, source_target_pairs={{0,2},{2,0},{4,6},{6,4},{8,10},{10,8},{12,14},{14,12},{1,3},{3,1},... | collective-permute-start | bytes 884744 | tf_op jit(solution)/shard_map/ppermute | solution.py:17
  5.3 25.0 %collective-permute-start.1 = (bf16[48,4608]{1,0:T(8,128)(2,1)S(1)}, bf16[48,4608]{1,0:T(8,128)(2,1)S(1)}, u32[]{:S(2)}, u32[]{:S(2)}) collective-permute-start(bf16[48,4608]{1,0:T(8,128)(2,1)S(1)} %copy-done.4), channel_id=1, source_target_pairs={{0,8},{2,10},{4,12},{6,14},{8,0},{10,2},{12,4},{14,6},{1,9},{3,11}... | collective-permute-start | bytes 1327112 | tf_op jit(solution)/shard_map/ppermute | solution.py:17
  8.3 22.6 %collective-permute-start = (bf16[48,4608]{1,0:T(8,128)(2,1)S(1)}, bf16[48,4608]{1,0:T(8,128)(2,1)S(1)}, u32[]{:S(2)}, u32[]{:S(2)}) collective-permute-start(bf16[48,4608]{1,0:T(8,128)(2,1)S(1)} %copy-done.4), channel_id=1, source_target_pairs={{0,4},{2,6},{4,0},{6,2},{8,12},{10,14},{12,8},{14,10},{1,5},{3,7},... | collective-permute-start | bytes 1327112 | tf_op jit(solution)/shard_map/ppermute | solution.py:17
  9.9 18.1 %collective-permute-start.17 = (bf16[64,1152]{1,0:T(8,128)(2,1)S(1)}, bf16[64,1152]{1,0:T(8,128)(2,1)S(1)}, u32[]{:S(2)}, u32[]{:S(2)}) collective-permute-start(bf16[64,1152]{1,0:T(8,128)(2,1)S(1)} %get-tuple-element.40), channel_id=1, source_target_pairs={{0,2},{2,0},{4,6},{6,4},{8,10},{10,8},{12,14},{14,12},{1,3},{3,1},... | collective-permute-start | bytes 442376 | tf_op jit(solution)/shard_map/ppermute | solution.py:17
  28.0 9.4 %collective-permute-start.5 = (bf16[1152,128]{1,0:T(8,128)(2,1)S(1)}, bf16[1152,128]{1,0:T(8,128)(2,1)S(1)}, u32[]{:S(2)}, u32[]{:S(2)}) collective-permute-start(bf16[1152,128]{1,0:T(8,128)(2,1)S(1)} %collective-permute-done.4.refs_8_.refs_5_), channel_id=1, source_target_pairs={{0,16},{2,18},{4,20},{6,22},{8,24},{10,26},{12,28},{14,30},{16,0},... | collective-permute-start | bytes 884744 | tf_op jit(solution)/shard_map/ppermute | solution.py:33
  29.8 12.2 %collective-permute-start.3 = (bf16[128,2304]{1,0:T(8,128)(2,1)S(1)}, bf16[128,2304]{1,0:T(8,128)(2,1)S(1)}, u32[]{:S(2)}, u32[]{:S(2)}) collective-permute-start(bf16[128,2304]{1,0:T(8,128)(2,1)S(1)} %collective-permute-done.2.refs_6_.refs_3_), channel_id=1, source_target_pairs={{0,1},{1,0},{2,3},{3,2},{4,5},{5,4},{6,7},{7,6},{8,9},{9,8},{10,11... | collective-permute-start | bytes 1769480 | tf_op jit(solution)/shard_map/ppermute | solution.py:22
  30.0 8.1 %collective-permute-start.6 = (bf16[1152,128]{1,0:T(8,128)(2,1)S(1)}, bf16[1152,128]{1,0:T(8,128)(2,1)S(1)}, u32[]{:S(2)}, u32[]{:S(2)}) collective-permute-start(bf16[1152,128]{1,0:T(8,128)(2,1)S(1)} %collective-permute-done.4.refs_8_.refs_5_), channel_id=1, source_target_pairs={{0,1},{1,0},{2,3},{3,2},{4,5},{5,4},{6,7},{7,6},{8,9},{9,8},{10,11... | collective-permute-start | bytes 884744 | tf_op jit(solution)/shard_map/ppermute | solution.py:22
  30.3 13.9 %collective-permute-start.8 = (bf16[48,4608]{1,0:T(8,128)(2,1)S(1)}, bf16[48,4608]{1,0:T(8,128)(2,1)S(1)}, u32[]{:S(2)}, u32[]{:S(2)}) collective-permute-start(bf16[48,4608]{1,0:T(8,128)(2,1)S(1)} %copy-done.4), channel_id=1, source_target_pairs={{4,8},{6,10},{8,4},{10,6},{5,9},{7,11},{9,5},{11,7},{20,24},{22,26... | collective-permute-start | bytes 1327112 | tf_op jit(solution)/shard_map/ppermute | solution.py:17
  31.0 15.9 %collective-permute-start.9 = (bf16[48,4608]{1,0:T(8,128)(2,1)S(1)}, bf16[48,4608]{1,0:T(8,128)(2,1)S(1)}, u32[]{:S(2)}, u32[]{:S(2)}) collective-permute-start(bf16[48,4608]{1,0:T(8,128)(2,1)S(1)} %collective-permute-done.1.refs_2_), channel_id=1, source_target_pairs={{4,0},{6,2},{8,12},{10,14},{5,1},{7,3},{9,13},{11,15},{20,16},{22,... | collective-permute-start | bytes 1327112 | tf_op jit(solution)/shard_map/ppermute | solution.py:17
  38.1 20.1 %collective-permute-start.19 = (bf16[128,1152]{1,0:T(8,128)(2,1)S(1)}, bf16[128,1152]{1,0:T(8,128)(2,1)S(1)}, u32[]{:S(2)}, u32[]{:S(2)}) collective-permute-start(bf16[128,1152]{1,0:T(8,128)(2,1)S(1)} %get-tuple-element.41), channel_id=1, source_target_pairs={{0,8},{2,10},{4,12},{6,14},{8,0},{10,2},{12,4},{14,6},{1,9},{3,11}... | collective-permute-start | bytes 884744 | tf_op jit(solution)/shard_map/ppermute | solution.py:17
  48.9 10.7 %collective-permute-start.10 = (bf16[192,256]{1,0:T(8,128)(2,1)S(1)}, bf16[192,256]{1,0:T(8,128)(2,1)S(1)}, u32[]{:S(2)}, u32[]{:S(2)}) collective-permute-start(bf16[192,256]{1,0:T(8,128)(2,1)S(1)} %get-tuple-element.35.refs_3_), channel_id=1, source_target_pairs={{0,2},{2,0},{4,6},{6,4},{8,10},{10,8},{12,14},{14,12},{1,3},{3,1},... | collective-permute-start | bytes 294920 | tf_op jit(solution)/shard_map/ppermute | solution.py:17
  50.5 28.7 %collective-permute-start.24 = (bf16[128,1152]{1,0:T(8,128)(2,1)S(1)}, bf16[128,1152]{1,0:T(8,128)(2,1)S(1)}, u32[]{:S(2)}, u32[]{:S(2)}) collective-permute-start(bf16[128,1152]{1,0:T(8,128)(2,1)S(1)} %get-tuple-element.41), channel_id=1, source_target_pairs={{0,4},{2,6},{4,0},{6,2},{8,12},{10,14},{12,8},{14,10},{1,5},{3,7},... | collective-permute-start | bytes 884744 | tf_op jit(solution)/shard_map/ppermute | solution.py:17
  56.7 23.0 %collective-permute-start.21 = (bf16[128,1152]{1,0:T(8,128)(2,1)S(1)}, bf16[128,1152]{1,0:T(8,128)(2,1)S(1)}, u32[]{:S(2)}, u32[]{:S(2)}) collective-permute-start(bf16[128,1152]{1,0:T(8,128)(2,1)S(1)} %get-tuple-element.41), channel_id=1, source_target_pairs={{4,8},{6,10},{8,4},{10,6},{5,9},{7,11},{9,5},{11,7},{20,24},{22,26... | collective-permute-start | bytes 884744 | tf_op jit(solution)/shard_map/ppermute | solution.py:17
  58.2 21.5 %collective-permute-start.20 = (bf16[128,1152]{1,0:T(8,128)(2,1)S(1)}, bf16[128,1152]{1,0:T(8,128)(2,1)S(1)}, u32[]{:S(2)}, u32[]{:S(2)}) collective-permute-start(bf16[128,1152]{1,0:T(8,128)(2,1)S(1)} %collective-permute-done.19.refs_8_), channel_id=1, source_target_pairs={{4,0},{6,2},{8,12},{10,14},{5,1},{7,3},{9,13},{11,15},{20,16},{22,... | collective-permute-start | bytes 884744 | tf_op jit(solution)/shard_map/ppermute | solution.py:17
  62.9 8.9 %collective-permute-start.13 = (bf16[48,256]{1,0:T(8,128)(2,1)S(1)}, bf16[48,256]{1,0:T(8,128)(2,1)S(1)}, u32[]{:S(2)}, u32[]{:S(2)}) collective-permute-start(bf16[48,256]{1,0:T(8,128)(2,1)S(1)} %get-tuple-element.37), channel_id=1, source_target_pairs={{0,4},{2,6},{4,0},{6,2},{8,12},{10,14},{12,8},{14,10},{1,5},{3,7},... | collective-permute-start | bytes 73736 | tf_op jit(solution)/shard_map/ppermute | solution.py:17
  65.6 8.7 %collective-permute-start.14 = (bf16[48,256]{1,0:T(8,128)(2,1)S(1)}, bf16[48,256]{1,0:T(8,128)(2,1)S(1)}, u32[]{:S(2)}, u32[]{:S(2)}) collective-permute-start(bf16[48,256]{1,0:T(8,128)(2,1)S(1)} %get-tuple-element.38), channel_id=1, source_target_pairs={{0,8},{2,10},{4,12},{6,14},{8,0},{10,2},{12,4},{14,6},{1,9},{3,11}... | collective-permute-start | bytes 73736 | tf_op jit(solution)/shard_map/ppermute | solution.py:17
  71.8 5.6 %collective-permute-start.15 = (bf16[48,256]{1,0:T(8,128)(2,1)S(1)}, bf16[48,256]{1,0:T(8,128)(2,1)S(1)}, u32[]{:S(2)}, u32[]{:S(2)}) collective-permute-start(bf16[48,256]{1,0:T(8,128)(2,1)S(1)} %get-tuple-element.39), channel_id=1, source_target_pairs={{0,12},{2,14},{4,8},{6,10},{8,4},{10,6},{12,0},{14,2},{1,13},{3,15... | collective-permute-start | bytes 73736 | tf_op jit(solution)/shard_map/ppermute | solution.py:17
  79.2 6.3 %collective-permute-start.26 = (bf16[128,1152]{1,0:T(8,128)(2,1)S(1)}, bf16[128,1152]{1,0:T(8,128)(2,1)S(1)}, u32[]{:S(2)}, u32[]{:S(2)}) collective-permute-start(bf16[128,1152]{1,0:T(8,128)(2,1)S(1)} %collective-permute-done.19.refs_8_), channel_id=1, source_target_pairs={{0,1},{1,0},{2,3},{3,2},{4,5},{5,4},{6,7},{7,6},{8,9},{9,8},{10,11... | collective-permute-start | bytes 884744 | tf_op jit(solution)/shard_map/ppermute | solution.py:22
  79.2 6.3 %collective-permute-start.25 = (bf16[128,1152]{1,0:T(8,128)(2,1)S(1)}, bf16[128,1152]{1,0:T(8,128)(2,1)S(1)}, u32[]{:S(2)}, u32[]{:S(2)}) collective-permute-start(bf16[128,1152]{1,0:T(8,128)(2,1)S(1)} %collective-permute-done.24.refs_6_), channel_id=1, source_target_pairs={{0,1},{1,0},{2,3},{3,2},{4,5},{5,4},{6,7},{7,6},{8,9},{9,8},{10,11... | collective-permute-start | bytes 884744 | tf_op jit(solution)/shard_map/ppermute | solution.py:22
  82.7 7.4 %collective-permute-start.27 = (bf16[128,1152]{1,0:T(8,128)(2,1)S(1)}, bf16[128,1152]{1,0:T(8,128)(2,1)S(1)}, u32[]{:S(2)}, u32[]{:S(2)}) collective-permute-start(bf16[128,1152]{1,0:T(8,128)(2,1)S(1)} %broadcast_select_fusion.refs_10_), channel_id=1, source_target_pairs={{0,1},{1,0},{2,3},{3,2},{4,5},{5,4},{6,7},{7,6},{8,9},{9,8},{10,11... | collective-permute-start | bytes 884744 | tf_op jit(solution)/shard_map/ppermute | solution.py:22
  82.8 6.3 %collective-permute-start.16 = (bf16[48,1024]{1,0:T(8,128)(2,1)S(1)}, bf16[48,1024]{1,0:T(8,128)(2,1)S(1)}, u32[]{:S(2)}, u32[]{:S(2)}) collective-permute-start(bf16[48,1024]{1,0:T(8,128)(2,1)S(1)} %shard_map.78.refs_1_), channel_id=1, source_target_pairs={{0,2},{2,0},{4,6},{6,4},{8,10},{10,8},{12,14},{14,12},{16,18},{18,... | collective-permute-start | bytes 294920 | tf_op jit(solution)/shard_map/ppermute | solution.py:33
  84.4 5.8 %collective-permute-start.23 = (bf16[48,1024]{1,0:T(8,128)(2,1)S(1)}, bf16[48,1024]{1,0:T(8,128)(2,1)S(1)}, u32[]{:S(2)}, u32[]{:S(2)}) collective-permute-start(bf16[48,1024]{1,0:T(8,128)(2,1)S(1)} %shard_map.78.refs_1_), channel_id=1, source_target_pairs={{0,18},{2,16},{4,22},{6,20},{8,26},{10,24},{12,30},{14,28},{16,2},... | collective-permute-start | bytes 294920 | tf_op jit(solution)/shard_map/ppermute | solution.py:33
  94.2 6.0 %collective-permute-start.30 = (bf16[48,1152]{1,0:T(8,128)(2,1)S(1)}, bf16[48,1152]{1,0:T(8,128)(2,1)S(1)}, u32[]{:S(2)}, u32[]{:S(2)}) collective-permute-start(bf16[48,1152]{1,0:T(8,128)(2,1)S(1)} %get-tuple-element.50), channel_id=1, source_target_pairs={{0,18},{2,16},{4,22},{6,20},{8,26},{10,24},{12,30},{14,28},{16,2},... | collective-permute-start | bytes 331784 | tf_op jit(solution)/shard_map/ppermute | solution.py:33
  (14 other events, 243.3 us)

commit v5 on v3

--- a/solution.py
+++ b/solution.py
@@ -98,11 +98,8 @@
     return own_query, own_kv, pair_query, pair_kv
 
 
-def early_kernel(short, flags, *refs):
-    blocks, weights, (out, near) = list(refs[:-11]), refs[-11:-2], refs[-2:]
-    if short:
-        near[...] = jnp.where(flags[2] != 0, blocks[1][...], blocks[2][...])
-        blocks[1:3] = [near]
+def early_kernel(flags, *refs):
+    blocks, weights, out = refs[:-10], refs[-10:-1], refs[-1]
     head = weights[0].shape[1]
     for i, part in enumerate(products(blocks, weights, flags[0], flags[3])):
         out[:, i * head : (i + 1) * head] = part
@@ -157,50 +154,47 @@
     pieces, outs = refs[:4], refs[4:]
     count, head = pieces[0].shape[0], queries.shape[1]
     rows = count // slabs
-    place = lambda shape, axis, a, b: place_of(
-        flags, lax.broadcasted_iota(jnp.int32, shape, axis), a, b, slabs, rows, cores
-    )
     end = 0
     ends = []
     for i in range(lengths.shape[0]):
         end = end + lengths[i]
         ends.append(end)
-    step = min(count, 4 * rows)
     even = flags[1] == 0
-    for at in range(0, count, step):
-        index = at + lax.broadcasted_iota(jnp.int32, (step, 1), 0)
+    reach = max(1, -(-slabs // 4))
+    for j in range(slabs):
+        slab = flags[5] ^ j
+        index = j * rows + lax.broadcasted_iota(jnp.int32, (rows, 1), 0)
         query_places = place_of(flags, index, 0, 0, slabs, rows, cores)
         starts = jnp.zeros_like(query_places)
         for end in ends:
             starts = jnp.where(query_places >= end, end, starts)
-        masks = []
-        for c in range(4):
-            key_places = place((1, count), 1, c % 2, c // 2)
-            masks.append((key_places <= query_places) & (key_places >= starts))
-        mixed = []
-        for h in range(2):
-            query = queries[h * count + at : h * count + at + step]
-            scores = [
-                jnp.where(mask, turned(query, piece[:, :head]), masked_low)
-                for piece, mask in zip(pieces, masks)
-            ]
-            largest = scores[0]
-            for part in scores[1:]:
-                largest = jnp.maximum(largest, part)
-            largest = jnp.max(largest, axis=1, keepdims=True)
-            total, acc = 0.0, 0.0
-            for part, piece, mask in zip(scores, pieces, masks):
-                e = jnp.where(mask, jnp.exp(part - largest), 0.0)
-                total = total + e
-                acc = acc + plain(e.astype(jnp.bfloat16), piece[:, head:])
-            total = jnp.sum(total, axis=1, keepdims=True)
-            mixed.append((acc / total).astype(jnp.bfloat16))
-        low = jnp.where(even, mixed[0], mixed[1])
-        high = jnp.where(even, mixed[1], mixed[0])
-        for k in range(step // rows):
-            out = outs[at // rows + k]
-            out[:, :head] = low[k * rows : (k + 1) * rows]
-            out[:, head:] = high[k * rows : (k + 1) * rows]
+        keys, values, key_places = [], [], []
+        for back in range(reach + 1):
+            held = jnp.maximum(slab - back, 0)
+            at = pl.ds(pl.multiple_of((held ^ flags[5]) * rows, 16), rows)
+            for c, piece in enumerate(pieces):
+                keys.append(piece[at, :head])
+                values.append(piece[at, head:])
+                first = ((slab - back) * 2 + (flags[1] ^ (c % 2))) * cores + (flags[0] ^ (c // 2))
+                key_places.append(first * rows)
+        lane = lax.broadcasted_iota(jnp.int32, (1, len(keys) * rows), 1)
+        place = key_places[0] + lane
+        for i in range(1, len(keys)):
+            place = jnp.where(lane >= i * rows, key_places[i] + lane - i * rows, place)
+        mask = (place <= query_places) & (place >= starts)
+        mask = jnp.concatenate([mask, mask], axis=0)
+        query = jnp.concatenate(
+            [queries[h * count + j * rows : h * count + (j + 1) * rows] for h in range(2)], axis=0
+        )
+        scores = turned(query, jnp.concatenate(keys, axis=0))
+        scores = jnp.where(mask, scores, masked_low)
+        largest = jnp.max(scores, axis=1, keepdims=True)
+        e = jnp.where(mask, jnp.exp(scores - largest), 0.0)
+        total = jnp.sum(e, axis=1, keepdims=True)
+        mixed = plain(e.astype(jnp.bfloat16), jnp.concatenate(values, axis=0)) / total
+        mixed = mixed.astype(jnp.bfloat16)
+        outs[j][:, :head] = jnp.where(even, mixed[:rows], mixed[rows:])
+        outs[j][:, head:] = jnp.where(even, mixed[rows:], mixed[:rows])
 
 
 def cut_kernel(flags, w_query, w_key, w_value, w_out, share_q, share_kv, out_sent, sems):
@@ -238,19 +232,30 @@
     copy.wait()
 
 
-def project_kernel(peers, split, flags, *refs):
-    stacked, pieces, outs = refs[:peers], list(refs[peers:-peers]), refs[-peers:]
+def tiles_of(width):
+    step = 384 if width % 384 == 0 else width
+    return [(at, at + step) for at in range(0, width, step)]
+
+
+def begin_kernel(peers, flags, *refs):
+    stacked, pieces, out = refs[:peers], refs[peers:-1], refs[-1]
+    inner = sum(piece.shape[0] for piece in pieces)
+    rows = jnp.concatenate([m[:, :inner] for m in stacked], axis=0)
+    for a, b in tiles_of(out.shape[1]):
+        out[:, a:b] = plain(rows, jnp.concatenate([p[:, a:b] for p in pieces], axis=0))
+
+
+def finish_kernel(peers, flags, *refs):
+    stacked, (begun, came, other), outs = refs[:peers], refs[peers:-peers], refs[-peers:]
     count, width = outs[0].shape
-    rows = jnp.concatenate([m[...] for m in stacked], axis=0)
-    step = 384 if width % 384 == 0 else width
+    inner = stacked[0].shape[1] - came.shape[0]
+    rows = jnp.concatenate([m[:, inner:] for m in stacked], axis=0)
     received = flags[2] != flags[0]
-    for at in range(0, width, step):
-        parts = [p[:, at : at + step] for p in pieces]
-        if split:
-            parts[-2:] = [jnp.where(received, parts[-2], parts[-1])]
-        total = plain(rows, jnp.concatenate(parts, axis=0))
+    for a, b in tiles_of(width):
+        weight = jnp.where(received, came[:, a:b], other[:, a:b])
+        total = begun[:, a:b] + plain(rows, weight)
         for i, out in enumerate(outs):
-            out[:, at : at + step] = total[i * count : (i + 1) * count].astype(out.dtype)
+            out[:, a:b] = total[i * count : (i + 1) * count].astype(out.dtype)
 
 
 def assemble_kernel(flags, *refs):
@@ -280,13 +285,11 @@
     is_inner = lambda t: (t >> 1) in (1, 2)
 
     if short:
-        is_outer = lambda t: not is_inner(t)
-        near_out = swap_tp(tokens, 2, is_outer)
         far = swap_tp(tokens, 4)
-        near_in = swap_tp(tokens, 2, is_inner)
+        near = swap_tp(tokens, 2)
         middle = swap_tp(tokens, 6, is_inner)
         relayed = swap_tp(far, 2, is_inner)
-        firsts, last = [tokens, near_out, near_in, far], [middle, relayed]
+        firsts, last = [tokens, near, far], [middle, relayed]
     else:
         came = [swap_tp(tokens, 2 * k) for k in range(1, slabs)]
         firsts, last = [tokens] + came[:-1], [came[-1], came[-1]]
@@ -321,11 +324,7 @@
     weights = [w_query, *turned_kv, came_kv, swap_sp(came_kv), came_q, cross_q]
     weights += [swap_sp(came_q), swap_sp(cross_q)]
     early = call(
-        lambda *refs: early_kernel(short, *refs),
-        [(((slabs - 1) * rows, 4 * head_dim), jnp.float32)],
-        [flags],
-        firsts + weights,
-        [pltpu.VMEM((rows, width), jnp.bfloat16)],
+        early_kernel, [((len(firsts) * rows, 4 * head_dim), jnp.float32)], [flags], firsts + weights
     )[0]
 
     in_order = lambda a, b, flag: [jnp.where(flag, a, b), jnp.where(flag, b, a)]
@@ -389,11 +388,20 @@
             piece = swap_tp(mine_of, 2 * k)
             both = in_order(piece, swap_sp(piece), core_low)
             pieces.append(jnp.concatenate(both, axis=0))
+    if not short:
+        pieces.append(pieces[-1])
+    count, kept = len(peers), pieces[:-2]
+    begun = call(
+        lambda *refs: begin_kernel(count, *refs),
+        [((count * rows, quarter), jnp.float32)],
+        [flags],
+        stacked + kept,
+    )
     outs = call(
-        lambda *refs: project_kernel(len(peers), short, *refs),
-        [((rows, quarter), jnp.bfloat16)] * len(peers),
-        [flags],
-        stacked + pieces,
+        lambda *refs: finish_kernel(count, *refs),
+        [((rows, quarter), jnp.bfloat16)] * count,
+        [flags],
+        stacked + list(begun) + pieces[-2:],
     )
     outs = [outs[0]] + [swap_in_slab(o, g, t) for o, (g, t) in zip(outs[1:], peers[1:])]
     sems = [pltpu.SemaphoreType.DMA((len(outs),))]

time: 116 us -> 100 us (0.86)
  waiting for transfers between devices: 69.3 us -> 57.3 us
  starting transfers between devices: 33.7 us -> 29.8 us
    ppermute x12 -> x11, waiting for transfers between devices: 53.4 us -> 38.3 us  [swap_tp(): return lax.ppermute(block, 'tp', route)]
    ppermute x7, waiting for transfers between devices: 12.7 us -> 17 us  [swap_in_slab(): return lax.ppermute(block, ('groups', 'tp'), route)]
    ppermute x12 -> x11, starting transfers between devices: 21.1 us -> 17.2 us  [swap_tp(): return lax.ppermute(block, 'tp', route)]
    ppermute x8, waiting for transfers between devices: 3.31 us -> 1.94 us  [swap_sp(): return lax.ppermute(block, 'sp', [(s, s ^ 1) for s in range(count)])]
    pallas_call x8 -> x9, Pallas kernels: 12 us -> 12.6 us  [call(): pl.pallas_call(kernel, in_specs=specs, out_specs=[pl.BlockSpec(memory_spa...]
  transfers between devices with their start and end apart: 29 -> 28, of which waited for: 15 -> 14; matrix products, arithmetic and copies ran while one was open for 0% -> 0% of each run, Pallas kernels for 6% -> 9%
where the time goes in v5:
time: 100 us
  waiting for transfers between devices  57.3 us (57%)
  starting transfers between devices  29.8 us (30%)
  Pallas kernels  12.6 us (13%)
    ppermute x11, waiting for transfers between devices, swap_tp(): return lax.ppermute(block, 'tp', route)  38.3 us
    ppermute x11, starting transfers between devices, swap_tp(): return lax.ppermute(block, 'tp', route)  17.2 us
    ppermute x7, waiting for transfers between devices, swap_in_slab(): return lax.ppermute(block, ('groups', 'tp'), route)  17 us
    pallas_call x9, Pallas kernels, call(): pl.pallas_call(kernel, in_specs=specs, out_specs=[pl.BlockSpec(memory_spa...  12.6 us
    ppermute x7, starting transfers between devices, swap_in_slab(): return lax.ppermute(block, ('groups', 'tp'), route)  9.55 us
    ppermute x2, starting transfers between devices, swap_by_core(): return lax.ppermute(block, ('tp', 'sp'), route)  2.34 us
  transfers between devices with their start and end apart: 28, of which 14 were waited for; matrix products, arithmetic and copies ran while one was open for 0% of the time, Pallas kernels for 9%

profile of v5, /device:TPU:0, one launch (start us, length us, event | category | flops | bytes accessed | tf_op | source)
XLA Modules:
  0.0 100.1 jit_solution(10406009788725059660)
XLA Ops:
  0.1 1.9 %shard_map.73 = (bf16[1152,128]{1,0:T(8,128)(2,1)S(1)}, bf16[128,2304]{1,0:T(8,128)(2,1)S(1)}, bf16[64,1152]{1,0:T(8,128)(2,1)S(1)}) custom-call(s32[6]{0:T(128)S(1)} %stack.31.flags.refs_0_, bf16[4608,128]{1,0:T(8,128)(2,1)} %refs_0_.3, bf16[64,4608]{1,0:T(8,128)(2,1)} %bitcast.8, bf16[64,4608]{1,0:T(8,128)(2,1)} %bitcast.11, bf16[128,4608]{1,0:T(8,128)(2,1)} %w_out.3), custom_call_target="tpu_custom_call" | custom-call | tf_op jit(solution)/shard_map/pallas_call | solution.py:60
  2.0 3.1 %collective-permute-start.2 = (bf16[128,2304]{1,0:T(8,128)(2,1)S(1)}, bf16[128,2304]{1,0:T(8,128)(2,1)S(1)}, u32[]{:S(2)}, u32[]{:S(2)}) collective-permute-start(bf16[128,2304]{1,0:T(8,128)(2,1)S(1)} %get-tuple-element.27), channel_id=1, source_target_pairs={{0,2},{2,0},{4,6},{6,4},{8,10},{10,8},{12,14},{14,12},{1,3},{3,1},... | collective-permute-start | bytes 1769480 | tf_op jit(solution)/shard_map/ppermute | solution.py:17
  5.1 2.0 %collective-permute-start = (bf16[48,4608]{1,0:T(8,128)(2,1)S(1)}, bf16[48,4608]{1,0:T(8,128)(2,1)S(1)}, u32[]{:S(2)}, u32[]{:S(2)}) collective-permute-start(bf16[48,4608]{1,0:T(8,128)(2,1)S(1)} %copy-done.4), channel_id=1, source_target_pairs={{0,4},{2,6},{4,0},{6,2},{8,12},{10,14},{12,8},{14,10},{1,5},{3,7},... | collective-permute-start | bytes 1327112 | tf_op jit(solution)/shard_map/ppermute | solution.py:17
  7.2 1.5 %collective-permute-start.17 = (bf16[64,1152]{1,0:T(8,128)(2,1)S(1)}, bf16[64,1152]{1,0:T(8,128)(2,1)S(1)}, u32[]{:S(2)}, u32[]{:S(2)}) collective-permute-start(bf16[64,1152]{1,0:T(8,128)(2,1)S(1)} %get-tuple-element.38), channel_id=1, source_target_pairs={{0,2},{2,0},{4,6},{6,4},{8,10},{10,8},{12,14},{14,12},{1,3},{3,1},... | collective-permute-start | bytes 442376 | tf_op jit(solution)/shard_map/ppermute | solution.py:17
  8.7 2.6 %collective-permute-start.1 = (bf16[48,4608]{1,0:T(8,128)(2,1)S(1)}, bf16[48,4608]{1,0:T(8,128)(2,1)S(1)}, u32[]{:S(2)}, u32[]{:S(2)}) collective-permute-start(bf16[48,4608]{1,0:T(8,128)(2,1)S(1)} %copy-done.4), channel_id=1, source_target_pairs={{0,8},{2,10},{4,12},{6,14},{8,0},{10,2},{12,4},{14,6},{1,9},{3,11}... | collective-permute-start | bytes 1327112 | tf_op jit(solution)/shard_map/ppermute | solution.py:17
  11.3 16.6 %collective-permute-done.17.came = bf16[64,1152]{1,0:T(8,128)(2,1)S(1)} collective-permute-done((bf16[64,1152]{1,0:T(8,128)(2,1)S(1)}, bf16[64,1152]{1,0:T(8,128)(2,1)S(1)}, u32[]{:S(2)}, u32[]{:S(2)}) %collective-permute-start.17) | collective-permute-done | bytes 147488 | tf_op jit(solution)/shard_map/ppermute | solution.py:17
  27.9 1.7 %collective-permute-start.5 = (bf16[1152,128]{1,0:T(8,128)(2,1)S(1)}, bf16[1152,128]{1,0:T(8,128)(2,1)S(1)}, u32[]{:S(2)}, u32[]{:S(2)}) collective-permute-start(bf16[1152,128]{1,0:T(8,128)(2,1)S(1)} %collective-permute-done.4.refs_8_.refs_5_), channel_id=1, source_target_pairs={{0,16},{2,18},{4,20},{6,22},{8,24},{10,26},{12,28},{14,30},{16,0},... | collective-permute-start | bytes 884744 | tf_op jit(solution)/shard_map/ppermute | solution.py:44
  30.7 1.6 %collective-permute-start.19 = (bf16[256,1152]{1,0:T(8,128)(2,1)S(1)}, bf16[256,1152]{1,0:T(8,128)(2,1)S(1)}, u32[]{:S(2)}, u32[]{:S(2)}) collective-permute-start(bf16[256,1152]{1,0:T(8,128)(2,1)S(1)} %shard_map.78.refs_5_), channel_id=1, source_target_pairs={{0,4},{1,9},{2,6},{3,11},{4,0},{5,13},{6,2},{7,15},{8,12},{9,1},{1... | collective-permute-start | bytes 1769480 | tf_op jit(solution)/shard_map/ppermute | solution.py:33
  33.1 4.2 %collective-permute-done.5.refs_9_.refs_6_ = bf16[1152,128]{1,0:T(8,128)(2,1)S(1)} collective-permute-done((bf16[1152,128]{1,0:T(8,128)(2,1)S(1)}, bf16[1152,128]{1,0:T(8,128)(2,1)S(1)}, u32[]{:S(2)}, u32[]{:S(2)}) %collective-permute-start.5) | collective-permute-done | bytes 294944 | tf_op jit(solution)/shard_map/ppermute | solution.py:44
  40.3 2.1 %shard_map.74.early = f32[144,512]{1,0:T(8,128)S(1)} custom-call(s32[6]{0:T(128)S(1)} %stack.31.flags.refs_0_, bf16[48,4608]{1,0:T(8,128)(2,1)S(1)} %copy-done.4, bf16[48,4608]{1,0:T(8,128)(2,1)S(1)} %collective-permute-done.refs_1_, bf16[48,4608]{1,0:T(8,128)(2,1)S(1)} %collective-permute-done.1.refs_2_, bf16[4608,128]{1,0:T(8,128)(2,1)S(1)} %copy-done, ...), custom_call_target="tpu_custom_call" | custom-call | tf_op jit(solution)/shard_map/pallas_call | solution.py:60
  42.4 14.1 %collective-permute-done.9.relayed = bf16[48,4608]{1,0:T(8,128)(2,1)S(1)} collective-permute-done((bf16[48,4608]{1,0:T(8,128)(2,1)S(1)}, bf16[48,4608]{1,0:T(8,128)(2,1)S(1)}, u32[]{:S(2)}, u32[]{:S(2)}) %collective-permute-start.9) | collective-permute-done | bytes 442400 | tf_op jit(solution)/shard_map/ppermute | solution.py:17
  56.5 2.0 %shard_map.76 = (bf16[384,128]{1,0:T(8,128)(2,1)S(1)}, bf16[192,256]{1,0:T(8,128)(2,1)S(1)}) custom-call(s32[6]{0:T(128)S(1)} %stack.31.flags.refs_0_, f32[144,512]{1,0:T(8,128)S(1)} %shard_map.74.early, bf16[48,4608]{1,0:T(8,128)(2,1)S(1)} %collective-permute-done.8.middle, bf16[48,4608]{1,0:T(8,128)(2,1)S(1)} %collective-permute-done.9.relayed, ...), custom_call_target="tpu_custom_call" | custom-call | tf_op jit(solution)/shard_map/pallas_call | solution.py:60
  58.5 1.6 %collective-permute-start.10 = (bf16[192,256]{1,0:T(8,128)(2,1)S(1)}, bf16[192,256]{1,0:T(8,128)(2,1)S(1)}, u32[]{:S(2)}, u32[]{:S(2)}) collective-permute-start(bf16[192,256]{1,0:T(8,128)(2,1)S(1)} %get-tuple-element.32.refs_3_), channel_id=1, source_target_pairs={{0,2},{2,0},{4,6},{6,4},{8,10},{10,8},{12,14},{14,12},{1,3},{3,1},... | collective-permute-start | bytes 294920 | tf_op jit(solution)/shard_map/ppermute | solution.py:17
  60.9 2.2 %collective-permute-done.10.refs_4_ = bf16[192,256]{1,0:T(8,128)(2,1)S(1)} collective-permute-done((bf16[192,256]{1,0:T(8,128)(2,1)S(1)}, bf16[192,256]{1,0:T(8,128)(2,1)S(1)}, u32[]{:S(2)}, u32[]{:S(2)}) %collective-permute-start.10) | collective-permute-done | bytes 98336 | tf_op jit(solution)/shard_map/ppermute | solution.py:17
  64.5 1.7 %shard_map.77 = (bf16[48,256]{1,0:T(8,128)(2,1)S(1)}, bf16[48,256]{1,0:T(8,128)(2,1)S(1)}, bf16[48,256]{1,0:T(8,128)(2,1)S(1)}, bf16[48,256]{1,0:T(8,128)(2,1)S(1)}) custom-call(s32[6]{0:T(128)S(1)} %stack.31.flags.refs_0_, s32[8]{0:T(128)S(1)} %copy-done.5, bf16[384,128]{1,0:T(8,128)(2,1)S(1)} %get-tuple-element.31.refs_2_, ...), custom_call_target="tpu_custom_call" | custom-call | tf_op jit(solution)/shard_map/pallas_call | solution.py:60
  67.7 2.8 %collective-permute-start.14 = (bf16[48,256]{1,0:T(8,128)(2,1)S(1)}, bf16[48,256]{1,0:T(8,128)(2,1)S(1)}, u32[]{:S(2)}, u32[]{:S(2)}) collective-permute-start(bf16[48,256]{1,0:T(8,128)(2,1)S(1)} %get-tuple-element.36), channel_id=1, source_target_pairs={{0,8},{2,10},{4,12},{6,14},{8,0},{10,2},{12,4},{14,6},{1,9},{3,11}... | collective-permute-start | bytes 73736 | tf_op jit(solution)/shard_map/ppermute | solution.py:17
  70.7 2.0 %collective-permute-done.14 = bf16[48,256]{1,0:T(8,128)(2,1)S(1)} collective-permute-done((bf16[48,256]{1,0:T(8,128)(2,1)S(1)}, bf16[48,256]{1,0:T(8,128)(2,1)S(1)}, u32[]{:S(2)}, u32[]{:S(2)}) %collective-permute-start.14) | collective-permute-done | bytes 24608 | tf_op jit(solution)/shard_map/ppermute | solution.py:17
  72.7 3.4 %collective-permute-done.15 = bf16[48,256]{1,0:T(8,128)(2,1)S(1)} collective-permute-done((bf16[48,256]{1,0:T(8,128)(2,1)S(1)}, bf16[48,256]{1,0:T(8,128)(2,1)S(1)}, u32[]{:S(2)}, u32[]{:S(2)}) %collective-permute-start.15) | collective-permute-done | bytes 24608 | tf_op jit(solution)/shard_map/ppermute | solution.py:17
  77.5 3.2 %collective-permute-done.21.refs_3_ = bf16[48,1024]{1,0:T(8,128)(2,1)S(1)} collective-permute-done((bf16[48,1024]{1,0:T(8,128)(2,1)S(1)}, bf16[48,1024]{1,0:T(8,128)(2,1)S(1)}, u32[]{:S(2)}, u32[]{:S(2)}) %collective-permute-start.21) | collective-permute-done | bytes 98336 | tf_op jit(solution)/shard_map/ppermute | solution.py:44
  80.8 1.5 %collective-permute-start.16 = (bf16[48,1024]{1,0:T(8,128)(2,1)S(1)}, bf16[48,1024]{1,0:T(8,128)(2,1)S(1)}, u32[]{:S(2)}, u32[]{:S(2)}) collective-permute-start(bf16[48,1024]{1,0:T(8,128)(2,1)S(1)} %pad_maximum_fusion.refs_1_), channel_id=1, source_target_pairs={{0,2},{2,0},{4,6},{6,4},{8,10},{10,8},{12,14},{14,12},{16,18},{18,... | collective-permute-start | bytes 294920 | tf_op jit(solution)/shard_map/ppermute | solution.py:44
  83.6 3.5 %collective-permute-done.16.refs_2_ = bf16[48,1024]{1,0:T(8,128)(2,1)S(1)} collective-permute-done((bf16[48,1024]{1,0:T(8,128)(2,1)S(1)}, bf16[48,1024]{1,0:T(8,128)(2,1)S(1)}, u32[]{:S(2)}, u32[]{:S(2)}) %collective-permute-start.16) | collective-permute-done | bytes 98336 | tf_op jit(solution)/shard_map/ppermute | solution.py:44
  90.2 1.6 %collective-permute-start.25 = (bf16[48,1152]{1,0:T(8,128)(2,1)S(1)}, bf16[48,1152]{1,0:T(8,128)(2,1)S(1)}, u32[]{:S(2)}, u32[]{:S(2)}) collective-permute-start(bf16[48,1152]{1,0:T(8,128)(2,1)S(1)} %get-tuple-element.42), channel_id=1, source_target_pairs={{0,2},{2,0},{4,6},{6,4},{8,10},{10,8},{12,14},{14,12},{16,18},{18,... | collective-permute-start | bytes 331784 | tf_op jit(solution)/shard_map/ppermute | solution.py:44
  95.0 2.3 %collective-permute-done.26.refs_2_ = bf16[48,1152]{1,0:T(8,128)(2,1)S(1)} collective-permute-done((bf16[48,1152]{1,0:T(8,128)(2,1)S(1)}, bf16[48,1152]{1,0:T(8,128)(2,1)S(1)}, u32[]{:S(2)}, u32[]{:S(2)}) %collective-permute-start.26) | collective-permute-done | bytes 110624 | tf_op jit(solution)/shard_map/ppermute | solution.py:44
  97.2 1.6 %collective-permute-done.27.refs_3_ = bf16[48,1152]{1,0:T(8,128)(2,1)S(1)} collective-permute-done((bf16[48,1152]{1,0:T(8,128)(2,1)S(1)}, bf16[48,1152]{1,0:T(8,128)(2,1)S(1)}, u32[]{:S(2)}, u32[]{:S(2)}) %collective-permute-start.27) | collective-permute-done | bytes 110624 | tf_op jit(solution)/shard_map/ppermute | solution.py:44
  (59 shorter events, 19.1 us)
Async XLA Ops:
  2.0 27.8 %collective-permute-start.2 = (bf16[128,2304]{1,0:T(8,128)(2,1)S(1)}, bf16[128,2304]{1,0:T(8,128)(2,1)S(1)}, u32[]{:S(2)}, u32[]{:S(2)}) collective-permute-start(bf16[128,2304]{1,0:T(8,128)(2,1)S(1)} %get-tuple-element.27), channel_id=1, source_target_pairs={{0,2},{2,0},{4,6},{6,4},{8,10},{10,8},{12,14},{14,12},{1,3},{3,1},... | collective-permute-start | bytes 1769480 | tf_op jit(solution)/shard_map/ppermute | solution.py:17
  5.1 22.8 %collective-permute-start.4 = (bf16[1152,128]{1,0:T(8,128)(2,1)S(1)}, bf16[1152,128]{1,0:T(8,128)(2,1)S(1)}, u32[]{:S(2)}, u32[]{:S(2)}) collective-permute-start(bf16[1152,128]{1,0:T(8,128)(2,1)S(1)} %get-tuple-element.28), channel_id=1, source_target_pairs={{0,2},{2,0},{4,6},{6,4},{8,10},{10,8},{12,14},{14,12},{1,3},{3,1},... | collective-permute-start | bytes 884744 | tf_op jit(solution)/shard_map/ppermute | solution.py:17
  5.1 25.6 %collective-permute-start = (bf16[48,4608]{1,0:T(8,128)(2,1)S(1)}, bf16[48,4608]{1,0:T(8,128)(2,1)S(1)}, u32[]{:S(2)}, u32[]{:S(2)}) collective-permute-start(bf16[48,4608]{1,0:T(8,128)(2,1)S(1)} %copy-done.4), channel_id=1, source_target_pairs={{0,4},{2,6},{4,0},{6,2},{8,12},{10,14},{12,8},{14,10},{1,5},{3,7},... | collective-permute-start | bytes 1327112 | tf_op jit(solution)/shard_map/ppermute | solution.py:17
  7.2 20.7 %collective-permute-start.17 = (bf16[64,1152]{1,0:T(8,128)(2,1)S(1)}, bf16[64,1152]{1,0:T(8,128)(2,1)S(1)}, u32[]{:S(2)}, u32[]{:S(2)}) collective-permute-start(bf16[64,1152]{1,0:T(8,128)(2,1)S(1)} %get-tuple-element.38), channel_id=1, source_target_pairs={{0,2},{2,0},{4,6},{6,4},{8,10},{10,8},{12,14},{14,12},{1,3},{3,1},... | collective-permute-start | bytes 442376 | tf_op jit(solution)/shard_map/ppermute | solution.py:17
  8.7 23.7 %collective-permute-start.1 = (bf16[48,4608]{1,0:T(8,128)(2,1)S(1)}, bf16[48,4608]{1,0:T(8,128)(2,1)S(1)}, u32[]{:S(2)}, u32[]{:S(2)}) collective-permute-start(bf16[48,4608]{1,0:T(8,128)(2,1)S(1)} %copy-done.4), channel_id=1, source_target_pairs={{0,8},{2,10},{4,12},{6,14},{8,0},{10,2},{12,4},{14,6},{1,9},{3,11}... | collective-permute-start | bytes 1327112 | tf_op jit(solution)/shard_map/ppermute | solution.py:17
  27.9 9.4 %collective-permute-start.5 = (bf16[1152,128]{1,0:T(8,128)(2,1)S(1)}, bf16[1152,128]{1,0:T(8,128)(2,1)S(1)}, u32[]{:S(2)}, u32[]{:S(2)}) collective-permute-start(bf16[1152,128]{1,0:T(8,128)(2,1)S(1)} %collective-permute-done.4.refs_8_.refs_5_), channel_id=1, source_target_pairs={{0,16},{2,18},{4,20},{6,22},{8,24},{10,26},{12,28},{14,30},{16,0},... | collective-permute-start | bytes 884744 | tf_op jit(solution)/shard_map/ppermute | solution.py:44
  29.6 9.0 %collective-permute-start.6 = (bf16[1152,128]{1,0:T(8,128)(2,1)S(1)}, bf16[1152,128]{1,0:T(8,128)(2,1)S(1)}, u32[]{:S(2)}, u32[]{:S(2)}) collective-permute-start(bf16[1152,128]{1,0:T(8,128)(2,1)S(1)} %collective-permute-done.4.refs_8_.refs_5_), channel_id=1, source_target_pairs={{0,1},{1,0},{2,3},{3,2},{4,5},{5,4},{6,7},{7,6},{8,9},{9,8},{10,11... | collective-permute-start | bytes 884744 | tf_op jit(solution)/shard_map/ppermute | solution.py:22
  29.8 10.4 %collective-permute-start.3 = (bf16[128,2304]{1,0:T(8,128)(2,1)S(1)}, bf16[128,2304]{1,0:T(8,128)(2,1)S(1)}, u32[]{:S(2)}, u32[]{:S(2)}) collective-permute-start(bf16[128,2304]{1,0:T(8,128)(2,1)S(1)} %collective-permute-done.2.refs_6_.refs_3_), channel_id=1, source_target_pairs={{0,1},{1,0},{2,3},{3,2},{4,5},{5,4},{6,7},{7,6},{8,9},{9,8},{10,11... | collective-permute-start | bytes 1769480 | tf_op jit(solution)/shard_map/ppermute | solution.py:22
  30.7 29.3 %collective-permute-start.19 = (bf16[256,1152]{1,0:T(8,128)(2,1)S(1)}, bf16[256,1152]{1,0:T(8,128)(2,1)S(1)}, u32[]{:S(2)}, u32[]{:S(2)}) collective-permute-start(bf16[256,1152]{1,0:T(8,128)(2,1)S(1)} %shard_map.78.refs_5_), channel_id=1, source_target_pairs={{0,4},{1,9},{2,6},{3,11},{4,0},{5,13},{6,2},{7,15},{8,12},{9,1},{1... | collective-permute-start | bytes 1769480 | tf_op jit(solution)/shard_map/ppermute | solution.py:33
  32.4 10.0 %collective-permute-start.8 = (bf16[48,4608]{1,0:T(8,128)(2,1)S(1)}, bf16[48,4608]{1,0:T(8,128)(2,1)S(1)}, u32[]{:S(2)}, u32[]{:S(2)}) collective-permute-start(bf16[48,4608]{1,0:T(8,128)(2,1)S(1)} %copy-done.4), channel_id=1, source_target_pairs={{4,8},{6,10},{8,4},{10,6},{5,9},{7,11},{9,5},{11,7},{20,24},{22,26... | collective-permute-start | bytes 1327112 | tf_op jit(solution)/shard_map/ppermute | solution.py:17
  37.3 19.2 %collective-permute-start.9 = (bf16[48,4608]{1,0:T(8,128)(2,1)S(1)}, bf16[48,4608]{1,0:T(8,128)(2,1)S(1)}, u32[]{:S(2)}, u32[]{:S(2)}) collective-permute-start(bf16[48,4608]{1,0:T(8,128)(2,1)S(1)} %collective-permute-done.1.refs_2_), channel_id=1, source_target_pairs={{4,0},{6,2},{8,12},{10,14},{5,1},{7,3},{9,13},{11,15},{20,16},{22,... | collective-permute-start | bytes 1327112 | tf_op jit(solution)/shard_map/ppermute | solution.py:17
  58.5 4.7 %collective-permute-start.10 = (bf16[192,256]{1,0:T(8,128)(2,1)S(1)}, bf16[192,256]{1,0:T(8,128)(2,1)S(1)}, u32[]{:S(2)}, u32[]{:S(2)}) collective-permute-start(bf16[192,256]{1,0:T(8,128)(2,1)S(1)} %get-tuple-element.32.refs_3_), channel_id=1, source_target_pairs={{0,2},{2,0},{4,6},{6,4},{8,10},{10,8},{12,14},{14,12},{1,3},{3,1},... | collective-permute-start | bytes 294920 | tf_op jit(solution)/shard_map/ppermute | solution.py:17
  60.2 17.4 %collective-permute-start.20 = (bf16[256,1152]{1,0:T(8,128)(2,1)S(1)}, bf16[256,1152]{1,0:T(8,128)(2,1)S(1)}, u32[]{:S(2)}, u32[]{:S(2)}) collective-permute-start(bf16[256,1152]{1,0:T(8,128)(2,1)S(1)} %broadcast_select_fusion), channel_id=1, source_target_pairs={{4,8},{5,1},{6,10},{7,3},{8,4},{9,13},{10,6},{11,15},{20,24},{21,1... | collective-permute-start | bytes 1769480 | tf_op jit(solution)/shard_map/ppermute | solution.py:33
  66.2 4.5 %collective-permute-start.13 = (bf16[48,256]{1,0:T(8,128)(2,1)S(1)}, bf16[48,256]{1,0:T(8,128)(2,1)S(1)}, u32[]{:S(2)}, u32[]{:S(2)}) collective-permute-start(bf16[48,256]{1,0:T(8,128)(2,1)S(1)} %get-tuple-element.35), channel_id=1, source_target_pairs={{0,4},{2,6},{4,0},{6,2},{8,12},{10,14},{12,8},{14,10},{1,5},{3,7},... | collective-permute-start | bytes 73736 | tf_op jit(solution)/shard_map/ppermute | solution.py:17
  67.7 5.0 %collective-permute-start.14 = (bf16[48,256]{1,0:T(8,128)(2,1)S(1)}, bf16[48,256]{1,0:T(8,128)(2,1)S(1)}, u32[]{:S(2)}, u32[]{:S(2)}) collective-permute-start(bf16[48,256]{1,0:T(8,128)(2,1)S(1)} %get-tuple-element.36), channel_id=1, source_target_pairs={{0,8},{2,10},{4,12},{6,14},{8,0},{10,2},{12,4},{14,6},{1,9},{3,11}... | collective-permute-start | bytes 73736 | tf_op jit(solution)/shard_map/ppermute | solution.py:17
  70.5 5.6 %collective-permute-start.15 = (bf16[48,256]{1,0:T(8,128)(2,1)S(1)}, bf16[48,256]{1,0:T(8,128)(2,1)S(1)}, u32[]{:S(2)}, u32[]{:S(2)}) collective-permute-start(bf16[48,256]{1,0:T(8,128)(2,1)S(1)} %get-tuple-element.37), channel_id=1, source_target_pairs={{0,12},{2,14},{4,8},{6,10},{8,4},{10,6},{12,0},{14,2},{1,13},{3,15... | collective-permute-start | bytes 73736 | tf_op jit(solution)/shard_map/ppermute | solution.py:17
  76.1 4.7 %collective-permute-start.21 = (bf16[48,1024]{1,0:T(8,128)(2,1)S(1)}, bf16[48,1024]{1,0:T(8,128)(2,1)S(1)}, u32[]{:S(2)}, u32[]{:S(2)}) collective-permute-start(bf16[48,1024]{1,0:T(8,128)(2,1)S(1)} %pad_maximum_fusion.refs_1_), channel_id=1, source_target_pairs={{0,16},{2,18},{4,20},{6,22},{8,24},{10,26},{12,28},{14,30},{16,0},... | collective-permute-start | bytes 294920 | tf_op jit(solution)/shard_map/ppermute | solution.py:44
  77.5 6.1 %collective-permute-start.23 = (bf16[256,1152]{1,0:T(8,128)(2,1)S(1)}, bf16[256,1152]{1,0:T(8,128)(2,1)S(1)}, u32[]{:S(2)}, u32[]{:S(2)}) collective-permute-start(bf16[256,1152]{1,0:T(8,128)(2,1)S(1)} %collective-permute-done.19.refs_6_), channel_id=1, source_target_pairs={{0,1},{1,0},{2,3},{3,2},{4,5},{5,4},{6,7},{7,6},{8,9},{9,8},{10,11... | collective-permute-start | bytes 1769480 | tf_op jit(solution)/shard_map/ppermute | solution.py:22
  80.8 8.5 %collective-permute-start.24 = (bf16[256,1152]{1,0:T(8,128)(2,1)S(1)}, bf16[256,1152]{1,0:T(8,128)(2,1)S(1)}, u32[]{:S(2)}, u32[]{:S(2)}) collective-permute-start(bf16[256,1152]{1,0:T(8,128)(2,1)S(1)} %collective-permute-done.20.refs_6_), channel_id=1, source_target_pairs={{0,1},{1,0},{2,3},{3,2},{4,5},{5,4},{6,7},{7,6},{8,9},{9,8},{10,11... | collective-permute-start | bytes 1769480 | tf_op jit(solution)/shard_map/ppermute | solution.py:22
  80.8 6.4 %collective-permute-start.16 = (bf16[48,1024]{1,0:T(8,128)(2,1)S(1)}, bf16[48,1024]{1,0:T(8,128)(2,1)S(1)}, u32[]{:S(2)}, u32[]{:S(2)}) collective-permute-start(bf16[48,1024]{1,0:T(8,128)(2,1)S(1)} %pad_maximum_fusion.refs_1_), channel_id=1, source_target_pairs={{0,2},{2,0},{4,6},{6,4},{8,10},{10,8},{12,14},{14,12},{16,18},{18,... | collective-permute-start | bytes 294920 | tf_op jit(solution)/shard_map/ppermute | solution.py:44
  82.3 5.8 %collective-permute-start.22 = (bf16[48,1024]{1,0:T(8,128)(2,1)S(1)}, bf16[48,1024]{1,0:T(8,128)(2,1)S(1)}, u32[]{:S(2)}, u32[]{:S(2)}) collective-permute-start(bf16[48,1024]{1,0:T(8,128)(2,1)S(1)} %pad_maximum_fusion.refs_1_), channel_id=1, source_target_pairs={{0,18},{2,16},{4,22},{6,20},{8,26},{10,24},{12,30},{14,28},{16,2},... | collective-permute-start | bytes 294920 | tf_op jit(solution)/shard_map/ppermute | solution.py:44
  90.2 4.8 %collective-permute-start.25 = (bf16[48,1152]{1,0:T(8,128)(2,1)S(1)}, bf16[48,1152]{1,0:T(8,128)(2,1)S(1)}, u32[]{:S(2)}, u32[]{:S(2)}) collective-permute-start(bf16[48,1152]{1,0:T(8,128)(2,1)S(1)} %get-tuple-element.42), channel_id=1, source_target_pairs={{0,2},{2,0},{4,6},{6,4},{8,10},{10,8},{12,14},{14,12},{16,18},{18,... | collective-permute-start | bytes 331784 | tf_op jit(solution)/shard_map/ppermute | solution.py:44
  91.7 5.5 %collective-permute-start.26 = (bf16[48,1152]{1,0:T(8,128)(2,1)S(1)}, bf16[48,1152]{1,0:T(8,128)(2,1)S(1)}, u32[]{:S(2)}, u32[]{:S(2)}) collective-permute-start(bf16[48,1152]{1,0:T(8,128)(2,1)S(1)} %get-tuple-element.43), channel_id=1, source_target_pairs={{0,16},{2,18},{4,20},{6,22},{8,24},{10,26},{12,28},{14,30},{16,0},... | collective-permute-start | bytes 331784 | tf_op jit(solution)/shard_map/ppermute | solution.py:44
  93.1 5.7 %collective-permute-start.27 = (bf16[48,1152]{1,0:T(8,128)(2,1)S(1)}, bf16[48,1152]{1,0:T(8,128)(2,1)S(1)}, u32[]{:S(2)}, u32[]{:S(2)}) collective-permute-start(bf16[48,1152]{1,0:T(8,128)(2,1)S(1)} %get-tuple-element.44), channel_id=1, source_target_pairs={{0,18},{2,16},{4,22},{6,20},{8,26},{10,24},{12,30},{14,28},{16,2},... | collective-permute-start | bytes 331784 | tf_op jit(solution)/shard_map/ppermute | solution.py:44
  (11 other events, 201.5 us)

commit v6 on v3

--- a/solution.py
+++ b/solution.py
@@ -98,11 +98,8 @@
     return own_query, own_kv, pair_query, pair_kv
 
 
-def early_kernel(short, flags, *refs):
-    blocks, weights, (out, near) = list(refs[:-11]), refs[-11:-2], refs[-2:]
-    if short:
-        near[...] = jnp.where(flags[2] != 0, blocks[1][...], blocks[2][...])
-        blocks[1:3] = [near]
+def early_kernel(flags, *refs):
+    blocks, weights, out = refs[:-10], refs[-10:-1], refs[-1]
     head = weights[0].shape[1]
     for i, part in enumerate(products(blocks, weights, flags[0], flags[3])):
         out[:, i * head : (i + 1) * head] = part
@@ -280,13 +277,11 @@
     is_inner = lambda t: (t >> 1) in (1, 2)
 
     if short:
-        is_outer = lambda t: not is_inner(t)
-        near_out = swap_tp(tokens, 2, is_outer)
         far = swap_tp(tokens, 4)
-        near_in = swap_tp(tokens, 2, is_inner)
+        near = swap_tp(tokens, 2)
         middle = swap_tp(tokens, 6, is_inner)
         relayed = swap_tp(far, 2, is_inner)
-        firsts, last = [tokens, near_out, near_in, far], [middle, relayed]
+        firsts, last = [tokens, near, far], [middle, relayed]
     else:
         came = [swap_tp(tokens, 2 * k) for k in range(1, slabs)]
         firsts, last = [tokens] + came[:-1], [came[-1], came[-1]]
@@ -321,11 +316,7 @@
     weights = [w_query, *turned_kv, came_kv, swap_sp(came_kv), came_q, cross_q]
     weights += [swap_sp(came_q), swap_sp(cross_q)]
     early = call(
-        lambda *refs: early_kernel(short, *refs),
-        [(((slabs - 1) * rows, 4 * head_dim), jnp.float32)],
-        [flags],
-        firsts + weights,
-        [pltpu.VMEM((rows, width), jnp.bfloat16)],
+        early_kernel, [((len(firsts) * rows, 4 * head_dim), jnp.float32)], [flags], firsts + weights
     )[0]
 
     in_order = lambda a, b, flag: [jnp.where(flag, a, b), jnp.where(flag, b, a)]
@@ -380,7 +371,7 @@
     if short:
         out_sent = jnp.where(core_low, out_own, out_first)
         out_last = swap_by_core(out_sent, (6, 2), is_inner)
-        out_last, stacked[2] = fence(out_last, stacked[2])
+        out_last, stacked[3] = fence(out_last, stacked[3])
         pieces = [out_own, out_first, out_swapped, out_last, swap_sp(out_last)]
     else:
         pieces = [out_own]

time: 116 us -> 99 us (0.85)
  waiting for transfers between devices: 69.3 us -> 55.6 us
  starting transfers between devices: 33.7 us -> 30.8 us
    ppermute x12 -> x11, waiting for transfers between devices: 53.4 us -> 38.3 us  [swap_tp(): return lax.ppermute(block, 'tp', route)]
    ppermute x12 -> x11, starting transfers between devices: 21.1 us -> 17.2 us  [swap_tp(): return lax.ppermute(block, 'tp', route)]
    ppermute x7, waiting for transfers between devices: 12.7 us -> 15.4 us  [swap_in_slab(): return lax.ppermute(block, ('groups', 'tp'), route)]
    ppermute x8, waiting for transfers between devices: 3.31 us -> 1.94 us  [swap_sp(): return lax.ppermute(block, 'sp', [(s, s ^ 1) for s in range(count)])]
  transfers between devices with their start and end apart: 29 -> 28, of which waited for: 15 -> 14; matrix products, arithmetic and copies ran while one was open for 0% -> 0% of each run, Pallas kernels for 6% -> 8%
where the time goes in v6:
time: 99 us; the launch traced here: 98.8 us
  waiting for transfers between devices  55.6 us (56%)
  starting transfers between devices  30.8 us (31%)
  Pallas kernels  12 us (12%)
    ppermute x11, waiting for transfers between devices, swap_tp(): return lax.ppermute(block, 'tp', route)  38.3 us
    ppermute x11, starting transfers between devices, swap_tp(): return lax.ppermute(block, 'tp', route)  17.2 us
    ppermute x7, waiting for transfers between devices, swap_in_slab(): return lax.ppermute(block, ('groups', 'tp'), route)  15.4 us
    pallas_call x8, Pallas kernels, call(): pl.pallas_call(kernel, in_specs=specs, out_specs=[pl.BlockSpec(memory_spa...  12 us
    ppermute x7, starting transfers between devices, swap_in_slab(): return lax.ppermute(block, ('groups', 'tp'), route)  10.6 us
    ppermute x2, starting transfers between devices, swap_by_core(): return lax.ppermute(block, ('tp', 'sp'), route)  2.34 us
  transfers between devices with their start and end apart: 28, of which 14 were waited for; matrix products, arithmetic and copies ran while one was open for 0% of the time, Pallas kernels for 8%

profile of v6, /device:TPU:0, one launch (start us, length us, event | category | flops | bytes accessed | tf_op | source)
XLA Modules:
  0.0 98.8 jit_solution(12275068383973484956)
XLA Ops:
  0.1 1.9 %shard_map.73 = (bf16[1152,128]{1,0:T(8,128)(2,1)S(1)}, bf16[128,2304]{1,0:T(8,128)(2,1)S(1)}, bf16[64,1152]{1,0:T(8,128)(2,1)S(1)}) custom-call(s32[6]{0:T(128)S(1)} %stack.31.flags.refs_0_, bf16[4608,128]{1,0:T(8,128)(2,1)} %refs_0_.3, bf16[64,4608]{1,0:T(8,128)(2,1)} %bitcast.8, bf16[64,4608]{1,0:T(8,128)(2,1)} %bitcast.11, bf16[128,4608]{1,0:T(8,128)(2,1)} %w_out.3), custom_call_target="tpu_custom_call" | custom-call | tf_op jit(solution)/shard_map/pallas_call | solution.py:60
  2.0 3.1 %collective-permute-start.2 = (bf16[128,2304]{1,0:T(8,128)(2,1)S(1)}, bf16[128,2304]{1,0:T(8,128)(2,1)S(1)}, u32[]{:S(2)}, u32[]{:S(2)}) collective-permute-start(bf16[128,2304]{1,0:T(8,128)(2,1)S(1)} %get-tuple-element.27), channel_id=1, source_target_pairs={{0,2},{2,0},{4,6},{6,4},{8,10},{10,8},{12,14},{14,12},{1,3},{3,1},... | collective-permute-start | bytes 1769480 | tf_op jit(solution)/shard_map/ppermute | solution.py:17
  5.1 2.0 %collective-permute-start = (bf16[48,4608]{1,0:T(8,128)(2,1)S(1)}, bf16[48,4608]{1,0:T(8,128)(2,1)S(1)}, u32[]{:S(2)}, u32[]{:S(2)}) collective-permute-start(bf16[48,4608]{1,0:T(8,128)(2,1)S(1)} %copy-done.4), channel_id=1, source_target_pairs={{0,4},{2,6},{4,0},{6,2},{8,12},{10,14},{12,8},{14,10},{1,5},{3,7},... | collective-permute-start | bytes 1327112 | tf_op jit(solution)/shard_map/ppermute | solution.py:17
  8.7 2.6 %collective-permute-start.1 = (bf16[48,4608]{1,0:T(8,128)(2,1)S(1)}, bf16[48,4608]{1,0:T(8,128)(2,1)S(1)}, u32[]{:S(2)}, u32[]{:S(2)}) collective-permute-start(bf16[48,4608]{1,0:T(8,128)(2,1)S(1)} %copy-done.4), channel_id=1, source_target_pairs={{0,8},{2,10},{4,12},{6,14},{8,0},{10,2},{12,4},{14,6},{1,9},{3,11}... | collective-permute-start | bytes 1327112 | tf_op jit(solution)/shard_map/ppermute | solution.py:17
  11.3 16.6 %collective-permute-done.18.came = bf16[64,1152]{1,0:T(8,128)(2,1)S(1)} collective-permute-done((bf16[64,1152]{1,0:T(8,128)(2,1)S(1)}, bf16[64,1152]{1,0:T(8,128)(2,1)S(1)}, u32[]{:S(2)}, u32[]{:S(2)}) %collective-permute-start.18) | collective-permute-done | bytes 147488 | tf_op jit(solution)/shard_map/ppermute | solution.py:17
  27.9 1.7 %collective-permute-start.5 = (bf16[1152,128]{1,0:T(8,128)(2,1)S(1)}, bf16[1152,128]{1,0:T(8,128)(2,1)S(1)}, u32[]{:S(2)}, u32[]{:S(2)}) collective-permute-start(bf16[1152,128]{1,0:T(8,128)(2,1)S(1)} %collective-permute-done.4.refs_8_.refs_5_), channel_id=1, source_target_pairs={{0,16},{2,18},{4,20},{6,22},{8,24},{10,26},{12,28},{14,30},{16,0},... | collective-permute-start | bytes 884744 | tf_op jit(solution)/shard_map/ppermute | solution.py:44
  30.7 1.6 %collective-permute-start.20 = (bf16[256,1152]{1,0:T(8,128)(2,1)S(1)}, bf16[256,1152]{1,0:T(8,128)(2,1)S(1)}, u32[]{:S(2)}, u32[]{:S(2)}) collective-permute-start(bf16[256,1152]{1,0:T(8,128)(2,1)S(1)} %shard_map.78.refs_5_), channel_id=1, source_target_pairs={{0,4},{1,9},{2,6},{3,11},{4,0},{5,13},{6,2},{7,15},{8,12},{9,1},{1... | collective-permute-start | bytes 1769480 | tf_op jit(solution)/shard_map/ppermute | solution.py:33
  33.1 4.2 %collective-permute-done.5.refs_9_.refs_6_ = bf16[1152,128]{1,0:T(8,128)(2,1)S(1)} collective-permute-done((bf16[1152,128]{1,0:T(8,128)(2,1)S(1)}, bf16[1152,128]{1,0:T(8,128)(2,1)S(1)}, u32[]{:S(2)}, u32[]{:S(2)}) %collective-permute-start.5) | collective-permute-done | bytes 294944 | tf_op jit(solution)/shard_map/ppermute | solution.py:44
  40.3 2.1 %shard_map.74.early = f32[144,512]{1,0:T(8,128)S(1)} custom-call(s32[6]{0:T(128)S(1)} %stack.31.flags.refs_0_, bf16[48,4608]{1,0:T(8,128)(2,1)S(1)} %copy-done.4, bf16[48,4608]{1,0:T(8,128)(2,1)S(1)} %collective-permute-done.refs_1_, bf16[48,4608]{1,0:T(8,128)(2,1)S(1)} %collective-permute-done.1.refs_2_, bf16[4608,128]{1,0:T(8,128)(2,1)S(1)} %copy-done, ...), custom_call_target="tpu_custom_call" | custom-call | tf_op jit(solution)/shard_map/pallas_call | solution.py:60
  42.4 14.1 %collective-permute-done.9.relayed = bf16[48,4608]{1,0:T(8,128)(2,1)S(1)} collective-permute-done((bf16[48,4608]{1,0:T(8,128)(2,1)S(1)}, bf16[48,4608]{1,0:T(8,128)(2,1)S(1)}, u32[]{:S(2)}, u32[]{:S(2)}) %collective-permute-start.9) | collective-permute-done | bytes 442400 | tf_op jit(solution)/shard_map/ppermute | solution.py:17
  56.5 2.0 %shard_map.76 = (bf16[384,128]{1,0:T(8,128)(2,1)S(1)}, bf16[192,256]{1,0:T(8,128)(2,1)S(1)}) custom-call(s32[6]{0:T(128)S(1)} %stack.31.flags.refs_0_, f32[144,512]{1,0:T(8,128)S(1)} %shard_map.74.early, bf16[48,4608]{1,0:T(8,128)(2,1)S(1)} %collective-permute-done.8.middle, bf16[48,4608]{1,0:T(8,128)(2,1)S(1)} %collective-permute-done.9.relayed, ...), custom_call_target="tpu_custom_call" | custom-call | tf_op jit(solution)/shard_map/pallas_call | solution.py:60
  58.5 1.6 %collective-permute-start.10 = (bf16[192,256]{1,0:T(8,128)(2,1)S(1)}, bf16[192,256]{1,0:T(8,128)(2,1)S(1)}, u32[]{:S(2)}, u32[]{:S(2)}) collective-permute-start(bf16[192,256]{1,0:T(8,128)(2,1)S(1)} %get-tuple-element.32.refs_3_), channel_id=1, source_target_pairs={{0,2},{2,0},{4,6},{6,4},{8,10},{10,8},{12,14},{14,12},{1,3},{3,1},... | collective-permute-start | bytes 294920 | tf_op jit(solution)/shard_map/ppermute | solution.py:17
  60.9 2.2 %collective-permute-done.10.refs_4_ = bf16[192,256]{1,0:T(8,128)(2,1)S(1)} collective-permute-done((bf16[192,256]{1,0:T(8,128)(2,1)S(1)}, bf16[192,256]{1,0:T(8,128)(2,1)S(1)}, u32[]{:S(2)}, u32[]{:S(2)}) %collective-permute-start.10) | collective-permute-done | bytes 98336 | tf_op jit(solution)/shard_map/ppermute | solution.py:17
  64.5 1.8 %shard_map.77 = (bf16[48,256]{1,0:T(8,128)(2,1)S(1)}, bf16[48,256]{1,0:T(8,128)(2,1)S(1)}, bf16[48,256]{1,0:T(8,128)(2,1)S(1)}, bf16[48,256]{1,0:T(8,128)(2,1)S(1)}) custom-call(s32[6]{0:T(128)S(1)} %stack.31.flags.refs_0_, s32[8]{0:T(128)S(1)} %copy-done.5, bf16[384,128]{1,0:T(8,128)(2,1)S(1)} %get-tuple-element.31.refs_2_, ...), custom_call_target="tpu_custom_call" | custom-call | tf_op jit(solution)/shard_map/pallas_call | solution.py:60
  67.7 2.8 %collective-permute-start.14 = (bf16[48,256]{1,0:T(8,128)(2,1)S(1)}, bf16[48,256]{1,0:T(8,128)(2,1)S(1)}, u32[]{:S(2)}, u32[]{:S(2)}) collective-permute-start(bf16[48,256]{1,0:T(8,128)(2,1)S(1)} %get-tuple-element.36), channel_id=1, source_target_pairs={{0,8},{2,10},{4,12},{6,14},{8,0},{10,2},{12,4},{14,6},{1,9},{3,11}... | collective-permute-start | bytes 73736 | tf_op jit(solution)/shard_map/ppermute | solution.py:17
  70.8 2.0 %collective-permute-done.14 = bf16[48,256]{1,0:T(8,128)(2,1)S(1)} collective-permute-done((bf16[48,256]{1,0:T(8,128)(2,1)S(1)}, bf16[48,256]{1,0:T(8,128)(2,1)S(1)}, u32[]{:S(2)}, u32[]{:S(2)}) %collective-permute-start.14) | collective-permute-done | bytes 24608 | tf_op jit(solution)/shard_map/ppermute | solution.py:17
  72.7 3.4 %collective-permute-done.15 = bf16[48,256]{1,0:T(8,128)(2,1)S(1)} collective-permute-done((bf16[48,256]{1,0:T(8,128)(2,1)S(1)}, bf16[48,256]{1,0:T(8,128)(2,1)S(1)}, u32[]{:S(2)}, u32[]{:S(2)}) %collective-permute-start.15) | collective-permute-done | bytes 24608 | tf_op jit(solution)/shard_map/ppermute | solution.py:17
  76.2 2.4 %collective-permute-start.22 = (bf16[48,1024]{1,0:T(8,128)(2,1)S(1)}, bf16[48,1024]{1,0:T(8,128)(2,1)S(1)}, u32[]{:S(2)}, u32[]{:S(2)}) collective-permute-start(bf16[48,1024]{1,0:T(8,128)(2,1)S(1)} %pad_maximum_fusion.refs_1_), channel_id=1, source_target_pairs={{0,18},{2,16},{4,22},{6,20},{8,26},{10,24},{12,30},{14,28},{16,2},... | collective-permute-start | bytes 294920 | tf_op jit(solution)/shard_map/ppermute | solution.py:44
  78.6 3.2 %collective-permute-done.22.refs_4_ = bf16[48,1024]{1,0:T(8,128)(2,1)S(1)} collective-permute-done((bf16[48,1024]{1,0:T(8,128)(2,1)S(1)}, bf16[48,1024]{1,0:T(8,128)(2,1)S(1)}, u32[]{:S(2)}, u32[]{:S(2)}) %collective-permute-start.22) | collective-permute-done | bytes 98336 | tf_op jit(solution)/shard_map/ppermute | solution.py:44
  81.8 1.5 %collective-permute-start.16 = (bf16[48,1024]{1,0:T(8,128)(2,1)S(1)}, bf16[48,1024]{1,0:T(8,128)(2,1)S(1)}, u32[]{:S(2)}, u32[]{:S(2)}) collective-permute-start(bf16[48,1024]{1,0:T(8,128)(2,1)S(1)} %pad_maximum_fusion.refs_1_), channel_id=1, source_target_pairs={{0,2},{2,0},{4,6},{6,4},{8,10},{10,8},{12,14},{14,12},{16,18},{18,... | collective-permute-start | bytes 294920 | tf_op jit(solution)/shard_map/ppermute | solution.py:44
  84.7 2.3 %collective-permute-done.16.refs_2_ = bf16[48,1024]{1,0:T(8,128)(2,1)S(1)} collective-permute-done((bf16[48,1024]{1,0:T(8,128)(2,1)S(1)}, bf16[48,1024]{1,0:T(8,128)(2,1)S(1)}, u32[]{:S(2)}, u32[]{:S(2)}) %collective-permute-start.16) | collective-permute-done | bytes 98336 | tf_op jit(solution)/shard_map/ppermute | solution.py:44
  91.5 1.6 %collective-permute-start.27 = (bf16[48,1152]{1,0:T(8,128)(2,1)S(1)}, bf16[48,1152]{1,0:T(8,128)(2,1)S(1)}, u32[]{:S(2)}, u32[]{:S(2)}) collective-permute-start(bf16[48,1152]{1,0:T(8,128)(2,1)S(1)} %get-tuple-element.44), channel_id=1, source_target_pairs={{0,18},{2,16},{4,22},{6,20},{8,26},{10,24},{12,30},{14,28},{16,2},... | collective-permute-start | bytes 331784 | tf_op jit(solution)/shard_map/ppermute | solution.py:44
  93.1 2.4 %collective-permute-done.25.refs_1_ = bf16[48,1152]{1,0:T(8,128)(2,1)S(1)} collective-permute-done((bf16[48,1152]{1,0:T(8,128)(2,1)S(1)}, bf16[48,1152]{1,0:T(8,128)(2,1)S(1)}, u32[]{:S(2)}, u32[]{:S(2)}) %collective-permute-start.25) | collective-permute-done | bytes 110624 | tf_op jit(solution)/shard_map/ppermute | solution.py:44
  95.9 1.6 %collective-permute-done.27.refs_3_ = bf16[48,1152]{1,0:T(8,128)(2,1)S(1)} collective-permute-done((bf16[48,1152]{1,0:T(8,128)(2,1)S(1)}, bf16[48,1152]{1,0:T(8,128)(2,1)S(1)}, u32[]{:S(2)}, u32[]{:S(2)}) %collective-permute-start.27) | collective-permute-done | bytes 110624 | tf_op jit(solution)/shard_map/ppermute | solution.py:44
  (58 shorter events, 17.9 us)
Async XLA Ops:
  2.0 27.8 %collective-permute-start.2 = (bf16[128,2304]{1,0:T(8,128)(2,1)S(1)}, bf16[128,2304]{1,0:T(8,128)(2,1)S(1)}, u32[]{:S(2)}, u32[]{:S(2)}) collective-permute-start(bf16[128,2304]{1,0:T(8,128)(2,1)S(1)} %get-tuple-element.27), channel_id=1, source_target_pairs={{0,2},{2,0},{4,6},{6,4},{8,10},{10,8},{12,14},{14,12},{1,3},{3,1},... | collective-permute-start | bytes 1769480 | tf_op jit(solution)/shard_map/ppermute | solution.py:17
  5.1 22.8 %collective-permute-start.4 = (bf16[1152,128]{1,0:T(8,128)(2,1)S(1)}, bf16[1152,128]{1,0:T(8,128)(2,1)S(1)}, u32[]{:S(2)}, u32[]{:S(2)}) collective-permute-start(bf16[1152,128]{1,0:T(8,128)(2,1)S(1)} %get-tuple-element.28), channel_id=1, source_target_pairs={{0,2},{2,0},{4,6},{6,4},{8,10},{10,8},{12,14},{14,12},{1,3},{3,1},... | collective-permute-start | bytes 884744 | tf_op jit(solution)/shard_map/ppermute | solution.py:17
  5.1 25.6 %collective-permute-start = (bf16[48,4608]{1,0:T(8,128)(2,1)S(1)}, bf16[48,4608]{1,0:T(8,128)(2,1)S(1)}, u32[]{:S(2)}, u32[]{:S(2)}) collective-permute-start(bf16[48,4608]{1,0:T(8,128)(2,1)S(1)} %copy-done.4), channel_id=1, source_target_pairs={{0,4},{2,6},{4,0},{6,2},{8,12},{10,14},{12,8},{14,10},{1,5},{3,7},... | collective-permute-start | bytes 1327112 | tf_op jit(solution)/shard_map/ppermute | solution.py:17
  7.2 20.7 %collective-permute-start.18 = (bf16[64,1152]{1,0:T(8,128)(2,1)S(1)}, bf16[64,1152]{1,0:T(8,128)(2,1)S(1)}, u32[]{:S(2)}, u32[]{:S(2)}) collective-permute-start(bf16[64,1152]{1,0:T(8,128)(2,1)S(1)} %get-tuple-element.38), channel_id=1, source_target_pairs={{0,2},{2,0},{4,6},{6,4},{8,10},{10,8},{12,14},{14,12},{1,3},{3,1},... | collective-permute-start | bytes 442376 | tf_op jit(solution)/shard_map/ppermute | solution.py:17
  8.7 23.7 %collective-permute-start.1 = (bf16[48,4608]{1,0:T(8,128)(2,1)S(1)}, bf16[48,4608]{1,0:T(8,128)(2,1)S(1)}, u32[]{:S(2)}, u32[]{:S(2)}) collective-permute-start(bf16[48,4608]{1,0:T(8,128)(2,1)S(1)} %copy-done.4), channel_id=1, source_target_pairs={{0,8},{2,10},{4,12},{6,14},{8,0},{10,2},{12,4},{14,6},{1,9},{3,11}... | collective-permute-start | bytes 1327112 | tf_op jit(solution)/shard_map/ppermute | solution.py:17
  27.9 9.4 %collective-permute-start.5 = (bf16[1152,128]{1,0:T(8,128)(2,1)S(1)}, bf16[1152,128]{1,0:T(8,128)(2,1)S(1)}, u32[]{:S(2)}, u32[]{:S(2)}) collective-permute-start(bf16[1152,128]{1,0:T(8,128)(2,1)S(1)} %collective-permute-done.4.refs_8_.refs_5_), channel_id=1, source_target_pairs={{0,16},{2,18},{4,20},{6,22},{8,24},{10,26},{12,28},{14,30},{16,0},... | collective-permute-start | bytes 884744 | tf_op jit(solution)/shard_map/ppermute | solution.py:44
  29.6 9.0 %collective-permute-start.6 = (bf16[1152,128]{1,0:T(8,128)(2,1)S(1)}, bf16[1152,128]{1,0:T(8,128)(2,1)S(1)}, u32[]{:S(2)}, u32[]{:S(2)}) collective-permute-start(bf16[1152,128]{1,0:T(8,128)(2,1)S(1)} %collective-permute-done.4.refs_8_.refs_5_), channel_id=1, source_target_pairs={{0,1},{1,0},{2,3},{3,2},{4,5},{5,4},{6,7},{7,6},{8,9},{9,8},{10,11... | collective-permute-start | bytes 884744 | tf_op jit(solution)/shard_map/ppermute | solution.py:22
  29.8 10.4 %collective-permute-start.3 = (bf16[128,2304]{1,0:T(8,128)(2,1)S(1)}, bf16[128,2304]{1,0:T(8,128)(2,1)S(1)}, u32[]{:S(2)}, u32[]{:S(2)}) collective-permute-start(bf16[128,2304]{1,0:T(8,128)(2,1)S(1)} %collective-permute-done.2.refs_6_.refs_3_), channel_id=1, source_target_pairs={{0,1},{1,0},{2,3},{3,2},{4,5},{5,4},{6,7},{7,6},{8,9},{9,8},{10,11... | collective-permute-start | bytes 1769480 | tf_op jit(solution)/shard_map/ppermute | solution.py:22
  30.7 29.3 %collective-permute-start.20 = (bf16[256,1152]{1,0:T(8,128)(2,1)S(1)}, bf16[256,1152]{1,0:T(8,128)(2,1)S(1)}, u32[]{:S(2)}, u32[]{:S(2)}) collective-permute-start(bf16[256,1152]{1,0:T(8,128)(2,1)S(1)} %shard_map.78.refs_5_), channel_id=1, source_target_pairs={{0,4},{1,9},{2,6},{3,11},{4,0},{5,13},{6,2},{7,15},{8,12},{9,1},{1... | collective-permute-start | bytes 1769480 | tf_op jit(solution)/shard_map/ppermute | solution.py:33
  32.4 10.0 %collective-permute-start.8 = (bf16[48,4608]{1,0:T(8,128)(2,1)S(1)}, bf16[48,4608]{1,0:T(8,128)(2,1)S(1)}, u32[]{:S(2)}, u32[]{:S(2)}) collective-permute-start(bf16[48,4608]{1,0:T(8,128)(2,1)S(1)} %copy-done.4), channel_id=1, source_target_pairs={{4,8},{6,10},{8,4},{10,6},{5,9},{7,11},{9,5},{11,7},{20,24},{22,26... | collective-permute-start | bytes 1327112 | tf_op jit(solution)/shard_map/ppermute | solution.py:17
  37.3 19.2 %collective-permute-start.9 = (bf16[48,4608]{1,0:T(8,128)(2,1)S(1)}, bf16[48,4608]{1,0:T(8,128)(2,1)S(1)}, u32[]{:S(2)}, u32[]{:S(2)}) collective-permute-start(bf16[48,4608]{1,0:T(8,128)(2,1)S(1)} %collective-permute-done.1.refs_2_), channel_id=1, source_target_pairs={{4,0},{6,2},{8,12},{10,14},{5,1},{7,3},{9,13},{11,15},{20,16},{22,... | collective-permute-start | bytes 1327112 | tf_op jit(solution)/shard_map/ppermute | solution.py:17
  58.5 4.7 %collective-permute-start.10 = (bf16[192,256]{1,0:T(8,128)(2,1)S(1)}, bf16[192,256]{1,0:T(8,128)(2,1)S(1)}, u32[]{:S(2)}, u32[]{:S(2)}) collective-permute-start(bf16[192,256]{1,0:T(8,128)(2,1)S(1)} %get-tuple-element.32.refs_3_), channel_id=1, source_target_pairs={{0,2},{2,0},{4,6},{6,4},{8,10},{10,8},{12,14},{14,12},{1,3},{3,1},... | collective-permute-start | bytes 294920 | tf_op jit(solution)/shard_map/ppermute | solution.py:17
  60.2 18.4 %collective-permute-start.21 = (bf16[256,1152]{1,0:T(8,128)(2,1)S(1)}, bf16[256,1152]{1,0:T(8,128)(2,1)S(1)}, u32[]{:S(2)}, u32[]{:S(2)}) collective-permute-start(bf16[256,1152]{1,0:T(8,128)(2,1)S(1)} %broadcast_select_fusion), channel_id=1, source_target_pairs={{4,8},{5,1},{6,10},{7,3},{8,4},{9,13},{10,6},{11,15},{20,24},{21,1... | collective-permute-start | bytes 1769480 | tf_op jit(solution)/shard_map/ppermute | solution.py:33
  66.3 4.5 %collective-permute-start.13 = (bf16[48,256]{1,0:T(8,128)(2,1)S(1)}, bf16[48,256]{1,0:T(8,128)(2,1)S(1)}, u32[]{:S(2)}, u32[]{:S(2)}) collective-permute-start(bf16[48,256]{1,0:T(8,128)(2,1)S(1)} %get-tuple-element.35), channel_id=1, source_target_pairs={{0,4},{2,6},{4,0},{6,2},{8,12},{10,14},{12,8},{14,10},{1,5},{3,7},... | collective-permute-start | bytes 73736 | tf_op jit(solution)/shard_map/ppermute | solution.py:17
  67.7 5.0 %collective-permute-start.14 = (bf16[48,256]{1,0:T(8,128)(2,1)S(1)}, bf16[48,256]{1,0:T(8,128)(2,1)S(1)}, u32[]{:S(2)}, u32[]{:S(2)}) collective-permute-start(bf16[48,256]{1,0:T(8,128)(2,1)S(1)} %get-tuple-element.36), channel_id=1, source_target_pairs={{0,8},{2,10},{4,12},{6,14},{8,0},{10,2},{12,4},{14,6},{1,9},{3,11}... | collective-permute-start | bytes 73736 | tf_op jit(solution)/shard_map/ppermute | solution.py:17
  70.5 5.6 %collective-permute-start.15 = (bf16[48,256]{1,0:T(8,128)(2,1)S(1)}, bf16[48,256]{1,0:T(8,128)(2,1)S(1)}, u32[]{:S(2)}, u32[]{:S(2)}) collective-permute-start(bf16[48,256]{1,0:T(8,128)(2,1)S(1)} %get-tuple-element.37), channel_id=1, source_target_pairs={{0,12},{2,14},{4,8},{6,10},{8,4},{10,6},{12,0},{14,2},{1,13},{3,15... | collective-permute-start | bytes 73736 | tf_op jit(solution)/shard_map/ppermute | solution.py:17
  76.2 5.6 %collective-permute-start.22 = (bf16[48,1024]{1,0:T(8,128)(2,1)S(1)}, bf16[48,1024]{1,0:T(8,128)(2,1)S(1)}, u32[]{:S(2)}, u32[]{:S(2)}) collective-permute-start(bf16[48,1024]{1,0:T(8,128)(2,1)S(1)} %pad_maximum_fusion.refs_1_), channel_id=1, source_target_pairs={{0,18},{2,16},{4,22},{6,20},{8,26},{10,24},{12,30},{14,28},{16,2},... | collective-permute-start | bytes 294920 | tf_op jit(solution)/shard_map/ppermute | solution.py:44
  78.6 6.1 %collective-permute-start.23 = (bf16[256,1152]{1,0:T(8,128)(2,1)S(1)}, bf16[256,1152]{1,0:T(8,128)(2,1)S(1)}, u32[]{:S(2)}, u32[]{:S(2)}) collective-permute-start(bf16[256,1152]{1,0:T(8,128)(2,1)S(1)} %collective-permute-done.20.refs_6_), channel_id=1, source_target_pairs={{0,1},{1,0},{2,3},{3,2},{4,5},{5,4},{6,7},{7,6},{8,9},{9,8},{10,11... | collective-permute-start | bytes 1769480 | tf_op jit(solution)/shard_map/ppermute | solution.py:22
  81.8 6.5 %collective-permute-start.24 = (bf16[256,1152]{1,0:T(8,128)(2,1)S(1)}, bf16[256,1152]{1,0:T(8,128)(2,1)S(1)}, u32[]{:S(2)}, u32[]{:S(2)}) collective-permute-start(bf16[256,1152]{1,0:T(8,128)(2,1)S(1)} %collective-permute-done.21.refs_8_), channel_id=1, source_target_pairs={{0,1},{1,0},{2,3},{3,2},{4,5},{5,4},{6,7},{7,6},{8,9},{9,8},{10,11... | collective-permute-start | bytes 1769480 | tf_op jit(solution)/shard_map/ppermute | solution.py:22
  81.8 5.2 %collective-permute-start.16 = (bf16[48,1024]{1,0:T(8,128)(2,1)S(1)}, bf16[48,1024]{1,0:T(8,128)(2,1)S(1)}, u32[]{:S(2)}, u32[]{:S(2)}) collective-permute-start(bf16[48,1024]{1,0:T(8,128)(2,1)S(1)} %pad_maximum_fusion.refs_1_), channel_id=1, source_target_pairs={{0,2},{2,0},{4,6},{6,4},{8,10},{10,8},{12,14},{14,12},{16,18},{18,... | collective-permute-start | bytes 294920 | tf_op jit(solution)/shard_map/ppermute | solution.py:44
  83.3 4.9 %collective-permute-start.17 = (bf16[48,1024]{1,0:T(8,128)(2,1)S(1)}, bf16[48,1024]{1,0:T(8,128)(2,1)S(1)}, u32[]{:S(2)}, u32[]{:S(2)}) collective-permute-start(bf16[48,1024]{1,0:T(8,128)(2,1)S(1)} %pad_maximum_fusion.refs_1_), channel_id=1, source_target_pairs={{0,16},{2,18},{4,20},{6,22},{8,24},{10,26},{12,28},{14,30},{16,0},... | collective-permute-start | bytes 294920 | tf_op jit(solution)/shard_map/ppermute | solution.py:44
  89.5 5.9 %collective-permute-start.25 = (bf16[48,1152]{1,0:T(8,128)(2,1)S(1)}, bf16[48,1152]{1,0:T(8,128)(2,1)S(1)}, u32[]{:S(2)}, u32[]{:S(2)}) collective-permute-start(bf16[48,1152]{1,0:T(8,128)(2,1)S(1)} %get-tuple-element.42), channel_id=1, source_target_pairs={{0,2},{2,0},{4,6},{6,4},{8,10},{10,8},{12,14},{14,12},{16,18},{18,... | collective-permute-start | bytes 331784 | tf_op jit(solution)/shard_map/ppermute | solution.py:44
  90.1 5.8 %collective-permute-start.26 = (bf16[48,1152]{1,0:T(8,128)(2,1)S(1)}, bf16[48,1152]{1,0:T(8,128)(2,1)S(1)}, u32[]{:S(2)}, u32[]{:S(2)}) collective-permute-start(bf16[48,1152]{1,0:T(8,128)(2,1)S(1)} %get-tuple-element.43), channel_id=1, source_target_pairs={{0,16},{2,18},{4,20},{6,22},{8,24},{10,26},{12,28},{14,30},{16,0},... | collective-permute-start | bytes 331784 | tf_op jit(solution)/shard_map/ppermute | solution.py:44
  91.5 6.0 %collective-permute-start.27 = (bf16[48,1152]{1,0:T(8,128)(2,1)S(1)}, bf16[48,1152]{1,0:T(8,128)(2,1)S(1)}, u32[]{:S(2)}, u32[]{:S(2)}) collective-permute-start(bf16[48,1152]{1,0:T(8,128)(2,1)S(1)} %get-tuple-element.44), channel_id=1, source_target_pairs={{0,18},{2,16},{4,22},{6,20},{8,26},{10,24},{12,30},{14,28},{16,2},... | collective-permute-start | bytes 331784 | tf_op jit(solution)/shard_map/ppermute | solution.py:44
  (11 other events, 201.5 us)

commit v7 on v3

--- a/solution.py
+++ b/solution.py
@@ -99,10 +99,10 @@
 
 
 def early_kernel(short, flags, *refs):
-    blocks, weights, (out, near) = list(refs[:-11]), refs[-11:-2], refs[-2:]
+    blocks, weights, (out, far) = list(refs[:-11]), refs[-11:-2], refs[-2:]
     if short:
-        near[...] = jnp.where(flags[2] != 0, blocks[1][...], blocks[2][...])
-        blocks[1:3] = [near]
+        far[...] = jnp.where(flags[2] != 0, blocks[2][...], blocks[3][...])
+        blocks[2:4] = [far]
     head = weights[0].shape[1]
     for i, part in enumerate(products(blocks, weights, flags[0], flags[3])):
         out[:, i * head : (i + 1) * head] = part
@@ -280,13 +280,12 @@
     is_inner = lambda t: (t >> 1) in (1, 2)
 
     if short:
-        is_outer = lambda t: not is_inner(t)
-        near_out = swap_tp(tokens, 2, is_outer)
-        far = swap_tp(tokens, 4)
-        near_in = swap_tp(tokens, 2, is_inner)
+        far_out = swap_tp(tokens, 4, lambda t: not is_inner(t))
+        far_in = swap_tp(tokens, 4, is_inner)
+        near = swap_tp(tokens, 2)
         middle = swap_tp(tokens, 6, is_inner)
-        relayed = swap_tp(far, 2, is_inner)
-        firsts, last = [tokens, near_out, near_in, far], [middle, relayed]
+        relayed = swap_tp(far_out, 2, is_inner)
+        firsts, last = [tokens, near, far_out, far_in], [middle, relayed]
     else:
         came = [swap_tp(tokens, 2 * k) for k in range(1, slabs)]
         firsts, last = [tokens] + came[:-1], [came[-1], came[-1]]
@@ -380,7 +379,7 @@
     if short:
         out_sent = jnp.where(core_low, out_own, out_first)
         out_last = swap_by_core(out_sent, (6, 2), is_inner)
-        out_last, stacked[2] = fence(out_last, stacked[2])
+        out_last, stacked[3] = fence(out_last, stacked[3])
         pieces = [out_own, out_first, out_swapped, out_last, swap_sp(out_last)]
     else:
         pieces = [out_own]

time: 116 us -> 107 us (0.922)
  waiting for transfers between devices: 69.3 us -> 56.5 us
  starting transfers between devices: 33.7 us -> 37.5 us
    ppermute x12, waiting for transfers between devices: 53.4 us -> 42.3 us  [swap_tp(): return lax.ppermute(block, 'tp', route)]
    ppermute x2, starting transfers between devices: 2.34 us -> 5.57 us  [swap_by_core(): return lax.ppermute(block, ('tp', 'sp'), route)]
    ppermute x7, waiting for transfers between devices: 12.7 us -> 10.9 us  [swap_in_slab(): return lax.ppermute(block, ('groups', 'tp'), route)]
    ppermute x7, starting transfers between devices: 9.57 us -> 10.8 us  [swap_in_slab(): return lax.ppermute(block, ('groups', 'tp'), route)]
  transfers between devices with their start and end apart: 29 -> 29, of which waited for: 15 -> 15; matrix products, arithmetic and copies ran while one was open for 0% -> 0% of each run, Pallas kernels for 6% -> 7%
where the time goes in v7:
time: 107 us; the launch traced here: 106 us
  waiting for transfers between devices  56.5 us (53%)
  starting transfers between devices  37.5 us (35%)
  Pallas kernels  12 us (11%)
    ppermute x12, waiting for transfers between devices, swap_tp(): return lax.ppermute(block, 'tp', route)  42.3 us
    ppermute x12, starting transfers between devices, swap_tp(): return lax.ppermute(block, 'tp', route)  20.4 us
    pallas_call x8, Pallas kernels, call(): pl.pallas_call(kernel, in_specs=specs, out_specs=[pl.BlockSpec(memory_spa...  12 us
    ppermute x7, waiting for transfers between devices, swap_in_slab(): return lax.ppermute(block, ('groups', 'tp'), route)  10.9 us
    ppermute x7, starting transfers between devices, swap_in_slab(): return lax.ppermute(block, ('groups', 'tp'), route)  10.8 us
    ppermute x2, starting transfers between devices, swap_by_core(): return lax.ppermute(block, ('tp', 'sp'), route)  5.57 us
    ppermute x8, waiting for transfers between devices, swap_sp(): return lax.ppermute(block, 'sp', [(s, s ^ 1) for s in range(count)])  3.3 us
  transfers between devices with their start and end apart: 29, of which 15 were waited for; matrix products, arithmetic and copies ran while one was open for 0% of the time, Pallas kernels for 7%

profile of v7, /device:TPU:0, one launch (start us, length us, event | category | flops | bytes accessed | tf_op | source)
XLA Modules:
  0.0 106.4 jit_solution(8078090467366237013)
XLA Ops:
  0.1 1.9 %shard_map.73 = (bf16[1152,128]{1,0:T(8,128)(2,1)S(1)}, bf16[128,2304]{1,0:T(8,128)(2,1)S(1)}, bf16[64,1152]{1,0:T(8,128)(2,1)S(1)}) custom-call(s32[6]{0:T(128)S(1)} %stack.31.flags.refs_0_, bf16[4608,128]{1,0:T(8,128)(2,1)} %refs_0_.1, bf16[64,4608]{1,0:T(8,128)(2,1)} %bitcast.8, bf16[64,4608]{1,0:T(8,128)(2,1)} %bitcast.11, bf16[128,4608]{1,0:T(8,128)(2,1)} %w_out.3), custom_call_target="tpu_custom_call" | custom-call | tf_op jit(solution)/shard_map/pallas_call | solution.py:60
  2.0 3.1 %collective-permute-start.3 = (bf16[128,2304]{1,0:T(8,128)(2,1)S(1)}, bf16[128,2304]{1,0:T(8,128)(2,1)S(1)}, u32[]{:S(2)}, u32[]{:S(2)}) collective-permute-start(bf16[128,2304]{1,0:T(8,128)(2,1)S(1)} %get-tuple-element.27), channel_id=1, source_target_pairs={{0,2},{2,0},{4,6},{6,4},{8,10},{10,8},{12,14},{14,12},{1,3},{3,1},... | collective-permute-start | bytes 1769480 | tf_op jit(solution)/shard_map/ppermute | solution.py:17
  5.1 2.0 %collective-permute-start = (bf16[48,4608]{1,0:T(8,128)(2,1)S(1)}, bf16[48,4608]{1,0:T(8,128)(2,1)S(1)}, u32[]{:S(2)}, u32[]{:S(2)}) collective-permute-start(bf16[48,4608]{1,0:T(8,128)(2,1)S(1)} %copy-done.4), channel_id=1, source_target_pairs={{0,4},{2,6},{4,0},{6,2},{8,12},{10,14},{12,8},{14,10},{1,5},{3,7},... | collective-permute-start | bytes 1327112 | tf_op jit(solution)/shard_map/ppermute | solution.py:17
  7.2 1.5 %collective-permute-start.19 = (bf16[64,1152]{1,0:T(8,128)(2,1)S(1)}, bf16[64,1152]{1,0:T(8,128)(2,1)S(1)}, u32[]{:S(2)}, u32[]{:S(2)}) collective-permute-start(bf16[64,1152]{1,0:T(8,128)(2,1)S(1)} %get-tuple-element.38), channel_id=1, source_target_pairs={{0,2},{2,0},{4,6},{6,4},{8,10},{10,8},{12,14},{14,12},{1,3},{3,1},... | collective-permute-start | bytes 442376 | tf_op jit(solution)/shard_map/ppermute | solution.py:17
  8.7 4.5 %collective-permute-start.1 = (bf16[48,4608]{1,0:T(8,128)(2,1)S(1)}, bf16[48,4608]{1,0:T(8,128)(2,1)S(1)}, u32[]{:S(2)}, u32[]{:S(2)}) collective-permute-start(bf16[48,4608]{1,0:T(8,128)(2,1)S(1)} %copy-done.4), channel_id=1, source_target_pairs={{0,8},{2,10},{12,4},{14,6},{1,9},{3,11},{13,5},{15,7},{16,24},{18,... | collective-permute-start | bytes 1327112 | tf_op jit(solution)/shard_map/ppermute | solution.py:17
  13.2 14.7 %collective-permute-done.19.came = bf16[64,1152]{1,0:T(8,128)(2,1)S(1)} collective-permute-done((bf16[64,1152]{1,0:T(8,128)(2,1)S(1)}, bf16[64,1152]{1,0:T(8,128)(2,1)S(1)}, u32[]{:S(2)}, u32[]{:S(2)}) %collective-permute-start.19) | collective-permute-done | bytes 147488 | tf_op jit(solution)/shard_map/ppermute | solution.py:17
  30.6 1.7 %collective-permute-start.6 = (bf16[1152,128]{1,0:T(8,128)(2,1)S(1)}, bf16[1152,128]{1,0:T(8,128)(2,1)S(1)}, u32[]{:S(2)}, u32[]{:S(2)}) collective-permute-start(bf16[1152,128]{1,0:T(8,128)(2,1)S(1)} %collective-permute-done.5.refs_10_.refs_5_), channel_id=1, source_target_pairs={{0,16},{2,18},{4,20},{6,22},{8,24},{10,26},{12,28},{14,30},{16,0},... | collective-permute-start | bytes 884744 | tf_op jit(solution)/shard_map/ppermute | solution.py:44
  33.5 4.9 %collective-permute-start.21 = (bf16[256,1152]{1,0:T(8,128)(2,1)S(1)}, bf16[256,1152]{1,0:T(8,128)(2,1)S(1)}, u32[]{:S(2)}, u32[]{:S(2)}) collective-permute-start(bf16[256,1152]{1,0:T(8,128)(2,1)S(1)} %shard_map.78.refs_5_), channel_id=1, source_target_pairs={{0,4},{1,9},{2,6},{3,11},{4,0},{5,13},{6,2},{7,15},{8,12},{9,1},{1... | collective-permute-start | bytes 1769480 | tf_op jit(solution)/shard_map/ppermute | solution.py:33
  38.3 7.7 %collective-permute-done.2.refs_4_ = bf16[48,4608]{1,0:T(8,128)(2,1)S(1)} collective-permute-done((bf16[48,4608]{1,0:T(8,128)(2,1)S(1)}, bf16[48,4608]{1,0:T(8,128)(2,1)S(1)}, u32[]{:S(2)}, u32[]{:S(2)}) %collective-permute-start.2) | collective-permute-done | bytes 442400 | tf_op jit(solution)/shard_map/ppermute | solution.py:17
  49.7 2.1 %shard_map.74.early = f32[144,512]{1,0:T(8,128)S(1)} custom-call(s32[6]{0:T(128)S(1)} %stack.31.flags.refs_0_, bf16[48,4608]{1,0:T(8,128)(2,1)S(1)} %copy-done.4, bf16[48,4608]{1,0:T(8,128)(2,1)S(1)} %collective-permute-done.refs_2_, bf16[48,4608]{1,0:T(8,128)(2,1)S(1)} %collective-permute-done.1.refs_3_, ...), custom_call_target="tpu_custom_call" | custom-call | tf_op jit(solution)/shard_map/pallas_call | solution.py:60
  51.9 12.2 %collective-permute-done.10.relayed = bf16[48,4608]{1,0:T(8,128)(2,1)S(1)} collective-permute-done((bf16[48,4608]{1,0:T(8,128)(2,1)S(1)}, bf16[48,4608]{1,0:T(8,128)(2,1)S(1)}, u32[]{:S(2)}, u32[]{:S(2)}) %collective-permute-start.10) | collective-permute-done | bytes 442400 | tf_op jit(solution)/shard_map/ppermute | solution.py:17
  64.1 2.0 %shard_map.76 = (bf16[384,128]{1,0:T(8,128)(2,1)S(1)}, bf16[192,256]{1,0:T(8,128)(2,1)S(1)}) custom-call(s32[6]{0:T(128)S(1)} %stack.31.flags.refs_0_, f32[144,512]{1,0:T(8,128)S(1)} %shard_map.74.early, bf16[48,4608]{1,0:T(8,128)(2,1)S(1)} %collective-permute-done.9.middle, bf16[48,4608]{1,0:T(8,128)(2,1)S(1)} %collective-permute-done.10.relayed, ...), custom_call_target="tpu_custom_call" | custom-call | tf_op jit(solution)/shard_map/pallas_call | solution.py:60
  66.1 1.5 %collective-permute-start.11 = (bf16[192,256]{1,0:T(8,128)(2,1)S(1)}, bf16[192,256]{1,0:T(8,128)(2,1)S(1)}, u32[]{:S(2)}, u32[]{:S(2)}) collective-permute-start(bf16[192,256]{1,0:T(8,128)(2,1)S(1)} %get-tuple-element.32.refs_3_), channel_id=1, source_target_pairs={{0,2},{2,0},{4,6},{6,4},{8,10},{10,8},{12,14},{14,12},{1,3},{3,1},... | collective-permute-start | bytes 294920 | tf_op jit(solution)/shard_map/ppermute | solution.py:17
  68.5 2.3 %collective-permute-done.11.refs_4_ = bf16[192,256]{1,0:T(8,128)(2,1)S(1)} collective-permute-done((bf16[192,256]{1,0:T(8,128)(2,1)S(1)}, bf16[192,256]{1,0:T(8,128)(2,1)S(1)}, u32[]{:S(2)}, u32[]{:S(2)}) %collective-permute-start.11) | collective-permute-done | bytes 98336 | tf_op jit(solution)/shard_map/ppermute | solution.py:17
  72.1 1.8 %shard_map.77 = (bf16[48,256]{1,0:T(8,128)(2,1)S(1)}, bf16[48,256]{1,0:T(8,128)(2,1)S(1)}, bf16[48,256]{1,0:T(8,128)(2,1)S(1)}, bf16[48,256]{1,0:T(8,128)(2,1)S(1)}) custom-call(s32[6]{0:T(128)S(1)} %stack.31.flags.refs_0_, s32[8]{0:T(128)S(1)} %copy-done.5, bf16[384,128]{1,0:T(8,128)(2,1)S(1)} %get-tuple-element.31.refs_2_, ...), custom_call_target="tpu_custom_call" | custom-call | tf_op jit(solution)/shard_map/pallas_call | solution.py:60
  75.3 2.8 %collective-permute-start.15 = (bf16[48,256]{1,0:T(8,128)(2,1)S(1)}, bf16[48,256]{1,0:T(8,128)(2,1)S(1)}, u32[]{:S(2)}, u32[]{:S(2)}) collective-permute-start(bf16[48,256]{1,0:T(8,128)(2,1)S(1)} %get-tuple-element.36), channel_id=1, source_target_pairs={{0,8},{2,10},{4,12},{6,14},{8,0},{10,2},{12,4},{14,6},{1,9},{3,11}... | collective-permute-start | bytes 73736 | tf_op jit(solution)/shard_map/ppermute | solution.py:17
  78.4 2.5 %collective-permute-done.15 = bf16[48,256]{1,0:T(8,128)(2,1)S(1)} collective-permute-done((bf16[48,256]{1,0:T(8,128)(2,1)S(1)}, bf16[48,256]{1,0:T(8,128)(2,1)S(1)}, u32[]{:S(2)}, u32[]{:S(2)}) %collective-permute-start.15) | collective-permute-done | bytes 24608 | tf_op jit(solution)/shard_map/ppermute | solution.py:17
  80.9 2.9 %collective-permute-done.16 = bf16[48,256]{1,0:T(8,128)(2,1)S(1)} collective-permute-done((bf16[48,256]{1,0:T(8,128)(2,1)S(1)}, bf16[48,256]{1,0:T(8,128)(2,1)S(1)}, u32[]{:S(2)}, u32[]{:S(2)}) %collective-permute-start.16) | collective-permute-done | bytes 24608 | tf_op jit(solution)/shard_map/ppermute | solution.py:17
  83.7 2.5 %collective-permute-start.23 = (bf16[48,1024]{1,0:T(8,128)(2,1)S(1)}, bf16[48,1024]{1,0:T(8,128)(2,1)S(1)}, u32[]{:S(2)}, u32[]{:S(2)}) collective-permute-start(bf16[48,1024]{1,0:T(8,128)(2,1)S(1)} %pad_maximum_fusion.refs_1_), channel_id=1, source_target_pairs={{0,18},{2,16},{4,22},{6,20},{8,26},{10,24},{12,30},{14,28},{16,2},... | collective-permute-start | bytes 294920 | tf_op jit(solution)/shard_map/ppermute | solution.py:44
  86.3 3.0 %collective-permute-done.23.refs_4_ = bf16[48,1024]{1,0:T(8,128)(2,1)S(1)} collective-permute-done((bf16[48,1024]{1,0:T(8,128)(2,1)S(1)}, bf16[48,1024]{1,0:T(8,128)(2,1)S(1)}, u32[]{:S(2)}, u32[]{:S(2)}) %collective-permute-start.23) | collective-permute-done | bytes 98336 | tf_op jit(solution)/shard_map/ppermute | solution.py:44
  89.3 1.5 %collective-permute-start.17 = (bf16[48,1024]{1,0:T(8,128)(2,1)S(1)}, bf16[48,1024]{1,0:T(8,128)(2,1)S(1)}, u32[]{:S(2)}, u32[]{:S(2)}) collective-permute-start(bf16[48,1024]{1,0:T(8,128)(2,1)S(1)} %pad_maximum_fusion.refs_1_), channel_id=1, source_target_pairs={{0,2},{2,0},{4,6},{6,4},{8,10},{10,8},{12,14},{14,12},{16,18},{18,... | collective-permute-start | bytes 294920 | tf_op jit(solution)/shard_map/ppermute | solution.py:44
  92.3 2.2 %collective-permute-done.17.refs_2_ = bf16[48,1024]{1,0:T(8,128)(2,1)S(1)} collective-permute-done((bf16[48,1024]{1,0:T(8,128)(2,1)S(1)}, bf16[48,1024]{1,0:T(8,128)(2,1)S(1)}, u32[]{:S(2)}, u32[]{:S(2)}) %collective-permute-start.17) | collective-permute-done | bytes 98336 | tf_op jit(solution)/shard_map/ppermute | solution.py:44
  100.6 2.3 %collective-permute-done.26.refs_1_ = bf16[48,1152]{1,0:T(8,128)(2,1)S(1)} collective-permute-done((bf16[48,1152]{1,0:T(8,128)(2,1)S(1)}, bf16[48,1152]{1,0:T(8,128)(2,1)S(1)}, u32[]{:S(2)}, u32[]{:S(2)}) %collective-permute-start.26) | collective-permute-done | bytes 110624 | tf_op jit(solution)/shard_map/ppermute | solution.py:44
  103.3 1.8 %collective-permute-done.28.refs_3_ = bf16[48,1152]{1,0:T(8,128)(2,1)S(1)} collective-permute-done((bf16[48,1152]{1,0:T(8,128)(2,1)S(1)}, bf16[48,1152]{1,0:T(8,128)(2,1)S(1)}, u32[]{:S(2)}, u32[]{:S(2)}) %collective-permute-start.28) | collective-permute-done | bytes 110624 | tf_op jit(solution)/shard_map/ppermute | solution.py:44
  (60 shorter events, 20.8 us)
Async XLA Ops:
  2.0 30.3 %collective-permute-start.3 = (bf16[128,2304]{1,0:T(8,128)(2,1)S(1)}, bf16[128,2304]{1,0:T(8,128)(2,1)S(1)}, u32[]{:S(2)}, u32[]{:S(2)}) collective-permute-start(bf16[128,2304]{1,0:T(8,128)(2,1)S(1)} %get-tuple-element.27), channel_id=1, source_target_pairs={{0,2},{2,0},{4,6},{6,4},{8,10},{10,8},{12,14},{14,12},{1,3},{3,1},... | collective-permute-start | bytes 1769480 | tf_op jit(solution)/shard_map/ppermute | solution.py:17
  5.1 24.1 %collective-permute-start.5 = (bf16[1152,128]{1,0:T(8,128)(2,1)S(1)}, bf16[1152,128]{1,0:T(8,128)(2,1)S(1)}, u32[]{:S(2)}, u32[]{:S(2)}) collective-permute-start(bf16[1152,128]{1,0:T(8,128)(2,1)S(1)} %get-tuple-element.28), channel_id=1, source_target_pairs={{0,2},{2,0},{4,6},{6,4},{8,10},{10,8},{12,14},{14,12},{1,3},{3,1},... | collective-permute-start | bytes 884744 | tf_op jit(solution)/shard_map/ppermute | solution.py:17
  5.1 27.2 %collective-permute-start = (bf16[48,4608]{1,0:T(8,128)(2,1)S(1)}, bf16[48,4608]{1,0:T(8,128)(2,1)S(1)}, u32[]{:S(2)}, u32[]{:S(2)}) collective-permute-start(bf16[48,4608]{1,0:T(8,128)(2,1)S(1)} %copy-done.4), channel_id=1, source_target_pairs={{0,4},{2,6},{4,0},{6,2},{8,12},{10,14},{12,8},{14,10},{1,5},{3,7},... | collective-permute-start | bytes 1327112 | tf_op jit(solution)/shard_map/ppermute | solution.py:17
  7.2 20.7 %collective-permute-start.19 = (bf16[64,1152]{1,0:T(8,128)(2,1)S(1)}, bf16[64,1152]{1,0:T(8,128)(2,1)S(1)}, u32[]{:S(2)}, u32[]{:S(2)}) collective-permute-start(bf16[64,1152]{1,0:T(8,128)(2,1)S(1)} %get-tuple-element.38), channel_id=1, source_target_pairs={{0,2},{2,0},{4,6},{6,4},{8,10},{10,8},{12,14},{14,12},{1,3},{3,1},... | collective-permute-start | bytes 442376 | tf_op jit(solution)/shard_map/ppermute | solution.py:17
  8.7 24.8 %collective-permute-start.1 = (bf16[48,4608]{1,0:T(8,128)(2,1)S(1)}, bf16[48,4608]{1,0:T(8,128)(2,1)S(1)}, u32[]{:S(2)}, u32[]{:S(2)}) collective-permute-start(bf16[48,4608]{1,0:T(8,128)(2,1)S(1)} %copy-done.4), channel_id=1, source_target_pairs={{0,8},{2,10},{12,4},{14,6},{1,9},{3,11},{13,5},{15,7},{16,24},{18,... | collective-permute-start | bytes 1327112 | tf_op jit(solution)/shard_map/ppermute | solution.py:17
  27.9 18.2 %collective-permute-start.2 = (bf16[48,4608]{1,0:T(8,128)(2,1)S(1)}, bf16[48,4608]{1,0:T(8,128)(2,1)S(1)}, u32[]{:S(2)}, u32[]{:S(2)}) collective-permute-start(bf16[48,4608]{1,0:T(8,128)(2,1)S(1)} %copy-done.4), channel_id=1, source_target_pairs={{4,12},{6,14},{8,0},{10,2},{5,13},{7,15},{9,1},{11,3},{20,28},{22,... | collective-permute-start | bytes 1327112 | tf_op jit(solution)/shard_map/ppermute | solution.py:17
  30.6 16.1 %collective-permute-start.6 = (bf16[1152,128]{1,0:T(8,128)(2,1)S(1)}, bf16[1152,128]{1,0:T(8,128)(2,1)S(1)}, u32[]{:S(2)}, u32[]{:S(2)}) collective-permute-start(bf16[1152,128]{1,0:T(8,128)(2,1)S(1)} %collective-permute-done.5.refs_10_.refs_5_), channel_id=1, source_target_pairs={{0,16},{2,18},{4,20},{6,22},{8,24},{10,26},{12,28},{14,30},{16,0},... | collective-permute-start | bytes 884744 | tf_op jit(solution)/shard_map/ppermute | solution.py:44
  32.3 15.7 %collective-permute-start.7 = (bf16[1152,128]{1,0:T(8,128)(2,1)S(1)}, bf16[1152,128]{1,0:T(8,128)(2,1)S(1)}, u32[]{:S(2)}, u32[]{:S(2)}) collective-permute-start(bf16[1152,128]{1,0:T(8,128)(2,1)S(1)} %collective-permute-done.5.refs_10_.refs_5_), channel_id=1, source_target_pairs={{0,1},{1,0},{2,3},{3,2},{4,5},{5,4},{6,7},{7,6},{8,9},{9,8},{10,11... | collective-permute-start | bytes 884744 | tf_op jit(solution)/shard_map/ppermute | solution.py:22
  32.3 17.4 %collective-permute-start.4 = (bf16[128,2304]{1,0:T(8,128)(2,1)S(1)}, bf16[128,2304]{1,0:T(8,128)(2,1)S(1)}, u32[]{:S(2)}, u32[]{:S(2)}) collective-permute-start(bf16[128,2304]{1,0:T(8,128)(2,1)S(1)} %collective-permute-done.3.refs_8_.refs_3_), channel_id=1, source_target_pairs={{0,1},{1,0},{2,3},{3,2},{4,5},{5,4},{6,7},{7,6},{8,9},{9,8},{10,11... | collective-permute-start | bytes 1769480 | tf_op jit(solution)/shard_map/ppermute | solution.py:22
  33.5 34.2 %collective-permute-start.21 = (bf16[256,1152]{1,0:T(8,128)(2,1)S(1)}, bf16[256,1152]{1,0:T(8,128)(2,1)S(1)}, u32[]{:S(2)}, u32[]{:S(2)}) collective-permute-start(bf16[256,1152]{1,0:T(8,128)(2,1)S(1)} %shard_map.78.refs_5_), channel_id=1, source_target_pairs={{0,4},{1,9},{2,6},{3,11},{4,0},{5,13},{6,2},{7,15},{8,12},{9,1},{1... | collective-permute-start | bytes 1769480 | tf_op jit(solution)/shard_map/ppermute | solution.py:33
  46.0 5.8 %collective-permute-start.9 = (bf16[48,4608]{1,0:T(8,128)(2,1)S(1)}, bf16[48,4608]{1,0:T(8,128)(2,1)S(1)}, u32[]{:S(2)}, u32[]{:S(2)}) collective-permute-start(bf16[48,4608]{1,0:T(8,128)(2,1)S(1)} %copy-done.4), channel_id=1, source_target_pairs={{4,8},{6,10},{8,4},{10,6},{5,9},{7,11},{9,5},{11,7},{20,24},{22,26... | collective-permute-start | bytes 1327112 | tf_op jit(solution)/shard_map/ppermute | solution.py:17
  46.7 17.4 %collective-permute-start.10 = (bf16[48,4608]{1,0:T(8,128)(2,1)S(1)}, bf16[48,4608]{1,0:T(8,128)(2,1)S(1)}, u32[]{:S(2)}, u32[]{:S(2)}) collective-permute-start(bf16[48,4608]{1,0:T(8,128)(2,1)S(1)} %collective-permute-done.1.refs_3_), channel_id=1, source_target_pairs={{4,0},{6,2},{8,12},{10,14},{5,1},{7,3},{9,13},{11,15},{20,16},{22,... | collective-permute-start | bytes 1327112 | tf_op jit(solution)/shard_map/ppermute | solution.py:17
  66.1 4.7 %collective-permute-start.11 = (bf16[192,256]{1,0:T(8,128)(2,1)S(1)}, bf16[192,256]{1,0:T(8,128)(2,1)S(1)}, u32[]{:S(2)}, u32[]{:S(2)}) collective-permute-start(bf16[192,256]{1,0:T(8,128)(2,1)S(1)} %get-tuple-element.32.refs_3_), channel_id=1, source_target_pairs={{0,2},{2,0},{4,6},{6,4},{8,10},{10,8},{12,14},{14,12},{1,3},{3,1},... | collective-permute-start | bytes 294920 | tf_op jit(solution)/shard_map/ppermute | solution.py:17
  67.7 18.6 %collective-permute-start.22 = (bf16[256,1152]{1,0:T(8,128)(2,1)S(1)}, bf16[256,1152]{1,0:T(8,128)(2,1)S(1)}, u32[]{:S(2)}, u32[]{:S(2)}) collective-permute-start(bf16[256,1152]{1,0:T(8,128)(2,1)S(1)} %broadcast_select_fusion), channel_id=1, source_target_pairs={{4,8},{5,1},{6,10},{7,3},{8,4},{9,13},{10,6},{11,15},{20,24},{21,1... | collective-permute-start | bytes 1769480 | tf_op jit(solution)/shard_map/ppermute | solution.py:33
  75.3 5.6 %collective-permute-start.15 = (bf16[48,256]{1,0:T(8,128)(2,1)S(1)}, bf16[48,256]{1,0:T(8,128)(2,1)S(1)}, u32[]{:S(2)}, u32[]{:S(2)}) collective-permute-start(bf16[48,256]{1,0:T(8,128)(2,1)S(1)} %get-tuple-element.36), channel_id=1, source_target_pairs={{0,8},{2,10},{4,12},{6,14},{8,0},{10,2},{12,4},{14,6},{1,9},{3,11}... | collective-permute-start | bytes 73736 | tf_op jit(solution)/shard_map/ppermute | solution.py:17
  78.1 5.6 %collective-permute-start.16 = (bf16[48,256]{1,0:T(8,128)(2,1)S(1)}, bf16[48,256]{1,0:T(8,128)(2,1)S(1)}, u32[]{:S(2)}, u32[]{:S(2)}) collective-permute-start(bf16[48,256]{1,0:T(8,128)(2,1)S(1)} %get-tuple-element.37), channel_id=1, source_target_pairs={{0,12},{2,14},{4,8},{6,10},{8,4},{10,6},{12,0},{14,2},{1,13},{3,15... | collective-permute-start | bytes 73736 | tf_op jit(solution)/shard_map/ppermute | solution.py:17
  83.7 5.6 %collective-permute-start.23 = (bf16[48,1024]{1,0:T(8,128)(2,1)S(1)}, bf16[48,1024]{1,0:T(8,128)(2,1)S(1)}, u32[]{:S(2)}, u32[]{:S(2)}) collective-permute-start(bf16[48,1024]{1,0:T(8,128)(2,1)S(1)} %pad_maximum_fusion.refs_1_), channel_id=1, source_target_pairs={{0,18},{2,16},{4,22},{6,20},{8,26},{10,24},{12,30},{14,28},{16,2},... | collective-permute-start | bytes 294920 | tf_op jit(solution)/shard_map/ppermute | solution.py:44
  86.3 6.1 %collective-permute-start.24 = (bf16[256,1152]{1,0:T(8,128)(2,1)S(1)}, bf16[256,1152]{1,0:T(8,128)(2,1)S(1)}, u32[]{:S(2)}, u32[]{:S(2)}) collective-permute-start(bf16[256,1152]{1,0:T(8,128)(2,1)S(1)} %collective-permute-done.21.refs_6_), channel_id=1, source_target_pairs={{0,1},{1,0},{2,3},{3,2},{4,5},{5,4},{6,7},{7,6},{8,9},{9,8},{10,11... | collective-permute-start | bytes 1769480 | tf_op jit(solution)/shard_map/ppermute | solution.py:22
  89.3 6.5 %collective-permute-start.25 = (bf16[256,1152]{1,0:T(8,128)(2,1)S(1)}, bf16[256,1152]{1,0:T(8,128)(2,1)S(1)}, u32[]{:S(2)}, u32[]{:S(2)}) collective-permute-start(bf16[256,1152]{1,0:T(8,128)(2,1)S(1)} %collective-permute-done.22.refs_8_), channel_id=1, source_target_pairs={{0,1},{1,0},{2,3},{3,2},{4,5},{5,4},{6,7},{7,6},{8,9},{9,8},{10,11... | collective-permute-start | bytes 1769480 | tf_op jit(solution)/shard_map/ppermute | solution.py:22
  89.3 5.2 %collective-permute-start.17 = (bf16[48,1024]{1,0:T(8,128)(2,1)S(1)}, bf16[48,1024]{1,0:T(8,128)(2,1)S(1)}, u32[]{:S(2)}, u32[]{:S(2)}) collective-permute-start(bf16[48,1024]{1,0:T(8,128)(2,1)S(1)} %pad_maximum_fusion.refs_1_), channel_id=1, source_target_pairs={{0,2},{2,0},{4,6},{6,4},{8,10},{10,8},{12,14},{14,12},{16,18},{18,... | collective-permute-start | bytes 294920 | tf_op jit(solution)/shard_map/ppermute | solution.py:44
  90.8 4.9 %collective-permute-start.18 = (bf16[48,1024]{1,0:T(8,128)(2,1)S(1)}, bf16[48,1024]{1,0:T(8,128)(2,1)S(1)}, u32[]{:S(2)}, u32[]{:S(2)}) collective-permute-start(bf16[48,1024]{1,0:T(8,128)(2,1)S(1)} %pad_maximum_fusion.refs_1_), channel_id=1, source_target_pairs={{0,16},{2,18},{4,20},{6,22},{8,24},{10,26},{12,28},{14,30},{16,0},... | collective-permute-start | bytes 294920 | tf_op jit(solution)/shard_map/ppermute | solution.py:44
  97.1 5.8 %collective-permute-start.26 = (bf16[48,1152]{1,0:T(8,128)(2,1)S(1)}, bf16[48,1152]{1,0:T(8,128)(2,1)S(1)}, u32[]{:S(2)}, u32[]{:S(2)}) collective-permute-start(bf16[48,1152]{1,0:T(8,128)(2,1)S(1)} %get-tuple-element.42), channel_id=1, source_target_pairs={{0,2},{2,0},{4,6},{6,4},{8,10},{10,8},{12,14},{14,12},{16,18},{18,... | collective-permute-start | bytes 331784 | tf_op jit(solution)/shard_map/ppermute | solution.py:44
  97.7 5.6 %collective-permute-start.27 = (bf16[48,1152]{1,0:T(8,128)(2,1)S(1)}, bf16[48,1152]{1,0:T(8,128)(2,1)S(1)}, u32[]{:S(2)}, u32[]{:S(2)}) collective-permute-start(bf16[48,1152]{1,0:T(8,128)(2,1)S(1)} %get-tuple-element.43), channel_id=1, source_target_pairs={{0,16},{2,18},{4,20},{6,22},{8,24},{10,26},{12,28},{14,30},{16,0},... | collective-permute-start | bytes 331784 | tf_op jit(solution)/shard_map/ppermute | solution.py:44
  99.2 5.9 %collective-permute-start.28 = (bf16[48,1152]{1,0:T(8,128)(2,1)S(1)}, bf16[48,1152]{1,0:T(8,128)(2,1)S(1)}, u32[]{:S(2)}, u32[]{:S(2)}) collective-permute-start(bf16[48,1152]{1,0:T(8,128)(2,1)S(1)} %get-tuple-element.44), channel_id=1, source_target_pairs={{0,18},{2,16},{4,22},{6,20},{8,26},{10,24},{12,30},{14,28},{16,2},... | collective-permute-start | bytes 331784 | tf_op jit(solution)/shard_map/ppermute | solution.py:44
  (12 other events, 246.3 us)

commit v8 on v7

--- a/solution.py
+++ b/solution.py
@@ -238,19 +238,30 @@
     copy.wait()
 
 
-def project_kernel(peers, split, flags, *refs):
-    stacked, pieces, outs = refs[:peers], list(refs[peers:-peers]), refs[-peers:]
+def tiles_of(width):
+    step = 384 if width % 384 == 0 else width
+    return [(at, at + step) for at in range(0, width, step)]
+
+
+def begin_kernel(peers, flags, *refs):
+    stacked, pieces, out = refs[:peers], refs[peers:-1], refs[-1]
+    inner = sum(piece.shape[0] for piece in pieces)
+    rows = jnp.concatenate([m[:, :inner] for m in stacked], axis=0)
+    for a, b in tiles_of(out.shape[1]):
+        out[:, a:b] = plain(rows, jnp.concatenate([p[:, a:b] for p in pieces], axis=0))
+
+
+def finish_kernel(peers, flags, *refs):
+    stacked, (begun, came, other), outs = refs[:peers], refs[peers:-peers], refs[-peers:]
     count, width = outs[0].shape
-    rows = jnp.concatenate([m[...] for m in stacked], axis=0)
-    step = 384 if width % 384 == 0 else width
+    inner = stacked[0].shape[1] - came.shape[0]
+    rows = jnp.concatenate([m[:, inner:] for m in stacked], axis=0)
     received = flags[2] != flags[0]
-    for at in range(0, width, step):
-        parts = [p[:, at : at + step] for p in pieces]
-        if split:
-            parts[-2:] = [jnp.where(received, parts[-2], parts[-1])]
-        total = plain(rows, jnp.concatenate(parts, axis=0))
+    for a, b in tiles_of(width):
+        weight = jnp.where(received, came[:, a:b], other[:, a:b])
+        total = begun[:, a:b] + plain(rows, weight)
         for i, out in enumerate(outs):
-            out[:, at : at + step] = total[i * count : (i + 1) * count].astype(out.dtype)
+            out[:, a:b] = total[i * count : (i + 1) * count].astype(out.dtype)
 
 
 def assemble_kernel(flags, *refs):
@@ -388,11 +399,20 @@
             piece = swap_tp(mine_of, 2 * k)
             both = in_order(piece, swap_sp(piece), core_low)
             pieces.append(jnp.concatenate(both, axis=0))
+    if not short:
+        pieces.append(pieces[-1])
+    count, kept = len(peers), pieces[:-2]
+    begun = call(
+        lambda *refs: begin_kernel(count, *refs),
+        [((count * rows, quarter), jnp.float32)],
+        [flags],
+        stacked + kept,
+    )
     outs = call(
-        lambda *refs: project_kernel(len(peers), short, *refs),
-        [((rows, quarter), jnp.bfloat16)] * len(peers),
-        [flags],
-        stacked + pieces,
+        lambda *refs: finish_kernel(count, *refs),
+        [((rows, quarter), jnp.bfloat16)] * count,
+        [flags],
+        stacked + list(begun) + pieces[-2:],
     )
     outs = [outs[0]] + [swap_in_slab(o, g, t) for o, (g, t) in zip(outs[1:], peers[1:])]
     sems = [pltpu.SemaphoreType.DMA((len(outs),))]

time: 107 us -> 107 us (level)
    pallas_call x8 -> x9, Pallas kernels: 12 us -> 12.7 us  [call(): pl.pallas_call(kernel, in_specs=specs, out_specs=[pl.BlockSpec(memory_spa...]
  transfers between devices with their start and end apart: 29 -> 29, of which waited for: 15 -> 15; matrix products, arithmetic and copies ran while one was open for 0% -> 0% of each run, Pallas kernels for 7% -> 8%
where the time goes in v8:
time: 107 us
  waiting for transfers between devices  56.5 us (53%)
  starting transfers between devices  37.5 us (35%)
  Pallas kernels  12.7 us (12%)
    ppermute x12, waiting for transfers between devices, swap_tp(): return lax.ppermute(block, 'tp', route)  42.3 us
    ppermute x12, starting transfers between devices, swap_tp(): return lax.ppermute(block, 'tp', route)  20.4 us
    pallas_call x9, Pallas kernels, call(): pl.pallas_call(kernel, in_specs=specs, out_specs=[pl.BlockSpec(memory_spa...  12.7 us
    ppermute x7, waiting for transfers between devices, swap_in_slab(): return lax.ppermute(block, ('groups', 'tp'), route)  10.9 us
    ppermute x7, starting transfers between devices, swap_in_slab(): return lax.ppermute(block, ('groups', 'tp'), route)  10.8 us
    ppermute x2, starting transfers between devices, swap_by_core(): return lax.ppermute(block, ('tp', 'sp'), route)  5.57 us
    ppermute x8, waiting for transfers between devices, swap_sp(): return lax.ppermute(block, 'sp', [(s, s ^ 1) for s in range(count)])  3.3 us
  transfers between devices with their start and end apart: 29, of which 15 were waited for; matrix products, arithmetic and copies ran while one was open for 0% of the time, Pallas kernels for 8%

profile of v8, /device:TPU:0, one launch (start us, length us, event | category | flops | bytes accessed | tf_op | source)
XLA Modules:
  0.0 107.1 jit_solution(18244568660691124379)
XLA Ops:
  0.1 1.9 %shard_map.73 = (bf16[1152,128]{1,0:T(8,128)(2,1)S(1)}, bf16[128,2304]{1,0:T(8,128)(2,1)S(1)}, bf16[64,1152]{1,0:T(8,128)(2,1)S(1)}) custom-call(s32[6]{0:T(128)S(1)} %stack.31.flags.refs_0_, bf16[4608,128]{1,0:T(8,128)(2,1)} %refs_0_.1, bf16[64,4608]{1,0:T(8,128)(2,1)} %bitcast.8, bf16[64,4608]{1,0:T(8,128)(2,1)} %bitcast.11, bf16[128,4608]{1,0:T(8,128)(2,1)} %w_out.3), custom_call_target="tpu_custom_call" | custom-call | tf_op jit(solution)/shard_map/pallas_call | solution.py:60
  2.0 3.1 %collective-permute-start.3 = (bf16[128,2304]{1,0:T(8,128)(2,1)S(1)}, bf16[128,2304]{1,0:T(8,128)(2,1)S(1)}, u32[]{:S(2)}, u32[]{:S(2)}) collective-permute-start(bf16[128,2304]{1,0:T(8,128)(2,1)S(1)} %get-tuple-element.27), channel_id=1, source_target_pairs={{0,2},{2,0},{4,6},{6,4},{8,10},{10,8},{12,14},{14,12},{1,3},{3,1},... | collective-permute-start | bytes 1769480 | tf_op jit(solution)/shard_map/ppermute | solution.py:17
  5.1 2.0 %collective-permute-start = (bf16[48,4608]{1,0:T(8,128)(2,1)S(1)}, bf16[48,4608]{1,0:T(8,128)(2,1)S(1)}, u32[]{:S(2)}, u32[]{:S(2)}) collective-permute-start(bf16[48,4608]{1,0:T(8,128)(2,1)S(1)} %copy-done.4), channel_id=1, source_target_pairs={{0,4},{2,6},{4,0},{6,2},{8,12},{10,14},{12,8},{14,10},{1,5},{3,7},... | collective-permute-start | bytes 1327112 | tf_op jit(solution)/shard_map/ppermute | solution.py:17
  7.2 1.5 %collective-permute-start.19 = (bf16[64,1152]{1,0:T(8,128)(2,1)S(1)}, bf16[64,1152]{1,0:T(8,128)(2,1)S(1)}, u32[]{:S(2)}, u32[]{:S(2)}) collective-permute-start(bf16[64,1152]{1,0:T(8,128)(2,1)S(1)} %get-tuple-element.38), channel_id=1, source_target_pairs={{0,2},{2,0},{4,6},{6,4},{8,10},{10,8},{12,14},{14,12},{1,3},{3,1},... | collective-permute-start | bytes 442376 | tf_op jit(solution)/shard_map/ppermute | solution.py:17
  8.7 4.5 %collective-permute-start.1 = (bf16[48,4608]{1,0:T(8,128)(2,1)S(1)}, bf16[48,4608]{1,0:T(8,128)(2,1)S(1)}, u32[]{:S(2)}, u32[]{:S(2)}) collective-permute-start(bf16[48,4608]{1,0:T(8,128)(2,1)S(1)} %copy-done.4), channel_id=1, source_target_pairs={{0,8},{2,10},{12,4},{14,6},{1,9},{3,11},{13,5},{15,7},{16,24},{18,... | collective-permute-start | bytes 1327112 | tf_op jit(solution)/shard_map/ppermute | solution.py:17
  13.2 14.7 %collective-permute-done.19.came = bf16[64,1152]{1,0:T(8,128)(2,1)S(1)} collective-permute-done((bf16[64,1152]{1,0:T(8,128)(2,1)S(1)}, bf16[64,1152]{1,0:T(8,128)(2,1)S(1)}, u32[]{:S(2)}, u32[]{:S(2)}) %collective-permute-start.19) | collective-permute-done | bytes 147488 | tf_op jit(solution)/shard_map/ppermute | solution.py:17
  30.6 1.7 %collective-permute-start.6 = (bf16[1152,128]{1,0:T(8,128)(2,1)S(1)}, bf16[1152,128]{1,0:T(8,128)(2,1)S(1)}, u32[]{:S(2)}, u32[]{:S(2)}) collective-permute-start(bf16[1152,128]{1,0:T(8,128)(2,1)S(1)} %collective-permute-done.5.refs_10_.refs_5_), channel_id=1, source_target_pairs={{0,16},{2,18},{4,20},{6,22},{8,24},{10,26},{12,28},{14,30},{16,0},... | collective-permute-start | bytes 884744 | tf_op jit(solution)/shard_map/ppermute | solution.py:44
  33.5 4.9 %collective-permute-start.21 = (bf16[256,1152]{1,0:T(8,128)(2,1)S(1)}, bf16[256,1152]{1,0:T(8,128)(2,1)S(1)}, u32[]{:S(2)}, u32[]{:S(2)}) collective-permute-start(bf16[256,1152]{1,0:T(8,128)(2,1)S(1)} %shard_map.78.refs_5_), channel_id=1, source_target_pairs={{0,4},{1,9},{2,6},{3,11},{4,0},{5,13},{6,2},{7,15},{8,12},{9,1},{1... | collective-permute-start | bytes 1769480 | tf_op jit(solution)/shard_map/ppermute | solution.py:33
  38.3 7.7 %collective-permute-done.2.refs_4_ = bf16[48,4608]{1,0:T(8,128)(2,1)S(1)} collective-permute-done((bf16[48,4608]{1,0:T(8,128)(2,1)S(1)}, bf16[48,4608]{1,0:T(8,128)(2,1)S(1)}, u32[]{:S(2)}, u32[]{:S(2)}) %collective-permute-start.2) | collective-permute-done | bytes 442400 | tf_op jit(solution)/shard_map/ppermute | solution.py:17
  49.7 2.1 %shard_map.74.early = f32[144,512]{1,0:T(8,128)S(1)} custom-call(s32[6]{0:T(128)S(1)} %stack.31.flags.refs_0_, bf16[48,4608]{1,0:T(8,128)(2,1)S(1)} %copy-done.4, bf16[48,4608]{1,0:T(8,128)(2,1)S(1)} %collective-permute-done.refs_2_, bf16[48,4608]{1,0:T(8,128)(2,1)S(1)} %collective-permute-done.1.refs_3_, ...), custom_call_target="tpu_custom_call" | custom-call | tf_op jit(solution)/shard_map/pallas_call | solution.py:60
  51.9 12.2 %collective-permute-done.10.relayed = bf16[48,4608]{1,0:T(8,128)(2,1)S(1)} collective-permute-done((bf16[48,4608]{1,0:T(8,128)(2,1)S(1)}, bf16[48,4608]{1,0:T(8,128)(2,1)S(1)}, u32[]{:S(2)}, u32[]{:S(2)}) %collective-permute-start.10) | collective-permute-done | bytes 442400 | tf_op jit(solution)/shard_map/ppermute | solution.py:17
  64.1 2.0 %shard_map.76 = (bf16[384,128]{1,0:T(8,128)(2,1)S(1)}, bf16[192,256]{1,0:T(8,128)(2,1)S(1)}) custom-call(s32[6]{0:T(128)S(1)} %stack.31.flags.refs_0_, f32[144,512]{1,0:T(8,128)S(1)} %shard_map.74.early, bf16[48,4608]{1,0:T(8,128)(2,1)S(1)} %collective-permute-done.9.middle, bf16[48,4608]{1,0:T(8,128)(2,1)S(1)} %collective-permute-done.10.relayed, ...), custom_call_target="tpu_custom_call" | custom-call | tf_op jit(solution)/shard_map/pallas_call | solution.py:60
  66.1 1.5 %collective-permute-start.11 = (bf16[192,256]{1,0:T(8,128)(2,1)S(1)}, bf16[192,256]{1,0:T(8,128)(2,1)S(1)}, u32[]{:S(2)}, u32[]{:S(2)}) collective-permute-start(bf16[192,256]{1,0:T(8,128)(2,1)S(1)} %get-tuple-element.32.refs_3_), channel_id=1, source_target_pairs={{0,2},{2,0},{4,6},{6,4},{8,10},{10,8},{12,14},{14,12},{1,3},{3,1},... | collective-permute-start | bytes 294920 | tf_op jit(solution)/shard_map/ppermute | solution.py:17
  68.5 2.3 %collective-permute-done.11.refs_4_ = bf16[192,256]{1,0:T(8,128)(2,1)S(1)} collective-permute-done((bf16[192,256]{1,0:T(8,128)(2,1)S(1)}, bf16[192,256]{1,0:T(8,128)(2,1)S(1)}, u32[]{:S(2)}, u32[]{:S(2)}) %collective-permute-start.11) | collective-permute-done | bytes 98336 | tf_op jit(solution)/shard_map/ppermute | solution.py:17
  72.1 1.8 %shard_map.77 = (bf16[48,256]{1,0:T(8,128)(2,1)S(1)}, bf16[48,256]{1,0:T(8,128)(2,1)S(1)}, bf16[48,256]{1,0:T(8,128)(2,1)S(1)}, bf16[48,256]{1,0:T(8,128)(2,1)S(1)}) custom-call(s32[6]{0:T(128)S(1)} %stack.31.flags.refs_0_, s32[8]{0:T(128)S(1)} %copy-done.5, bf16[384,128]{1,0:T(8,128)(2,1)S(1)} %get-tuple-element.31.refs_2_, ...), custom_call_target="tpu_custom_call" | custom-call | tf_op jit(solution)/shard_map/pallas_call | solution.py:60
  75.3 2.8 %collective-permute-start.15 = (bf16[48,256]{1,0:T(8,128)(2,1)S(1)}, bf16[48,256]{1,0:T(8,128)(2,1)S(1)}, u32[]{:S(2)}, u32[]{:S(2)}) collective-permute-start(bf16[48,256]{1,0:T(8,128)(2,1)S(1)} %get-tuple-element.36), channel_id=1, source_target_pairs={{0,8},{2,10},{4,12},{6,14},{8,0},{10,2},{12,4},{14,6},{1,9},{3,11}... | collective-permute-start | bytes 73736 | tf_op jit(solution)/shard_map/ppermute | solution.py:17
  78.4 2.5 %collective-permute-done.15 = bf16[48,256]{1,0:T(8,128)(2,1)S(1)} collective-permute-done((bf16[48,256]{1,0:T(8,128)(2,1)S(1)}, bf16[48,256]{1,0:T(8,128)(2,1)S(1)}, u32[]{:S(2)}, u32[]{:S(2)}) %collective-permute-start.15) | collective-permute-done | bytes 24608 | tf_op jit(solution)/shard_map/ppermute | solution.py:17
  80.9 2.9 %collective-permute-done.16 = bf16[48,256]{1,0:T(8,128)(2,1)S(1)} collective-permute-done((bf16[48,256]{1,0:T(8,128)(2,1)S(1)}, bf16[48,256]{1,0:T(8,128)(2,1)S(1)}, u32[]{:S(2)}, u32[]{:S(2)}) %collective-permute-start.16) | collective-permute-done | bytes 24608 | tf_op jit(solution)/shard_map/ppermute | solution.py:17
  83.7 2.5 %collective-permute-start.23 = (bf16[48,1024]{1,0:T(8,128)(2,1)S(1)}, bf16[48,1024]{1,0:T(8,128)(2,1)S(1)}, u32[]{:S(2)}, u32[]{:S(2)}) collective-permute-start(bf16[48,1024]{1,0:T(8,128)(2,1)S(1)} %pad_maximum_fusion.refs_1_), channel_id=1, source_target_pairs={{0,18},{2,16},{4,22},{6,20},{8,26},{10,24},{12,30},{14,28},{16,2},... | collective-permute-start | bytes 294920 | tf_op jit(solution)/shard_map/ppermute | solution.py:44
  86.3 3.0 %collective-permute-done.23.refs_4_ = bf16[48,1024]{1,0:T(8,128)(2,1)S(1)} collective-permute-done((bf16[48,1024]{1,0:T(8,128)(2,1)S(1)}, bf16[48,1024]{1,0:T(8,128)(2,1)S(1)}, u32[]{:S(2)}, u32[]{:S(2)}) %collective-permute-start.23) | collective-permute-done | bytes 98336 | tf_op jit(solution)/shard_map/ppermute | solution.py:44
  89.3 1.5 %collective-permute-start.17 = (bf16[48,1024]{1,0:T(8,128)(2,1)S(1)}, bf16[48,1024]{1,0:T(8,128)(2,1)S(1)}, u32[]{:S(2)}, u32[]{:S(2)}) collective-permute-start(bf16[48,1024]{1,0:T(8,128)(2,1)S(1)} %pad_maximum_fusion.refs_1_), channel_id=1, source_target_pairs={{0,2},{2,0},{4,6},{6,4},{8,10},{10,8},{12,14},{14,12},{16,18},{18,... | collective-permute-start | bytes 294920 | tf_op jit(solution)/shard_map/ppermute | solution.py:44
  92.3 2.2 %collective-permute-done.17.refs_2_ = bf16[48,1024]{1,0:T(8,128)(2,1)S(1)} collective-permute-done((bf16[48,1024]{1,0:T(8,128)(2,1)S(1)}, bf16[48,1024]{1,0:T(8,128)(2,1)S(1)}, u32[]{:S(2)}, u32[]{:S(2)}) %collective-permute-start.17) | collective-permute-done | bytes 98336 | tf_op jit(solution)/shard_map/ppermute | solution.py:44
  101.4 2.3 %collective-permute-done.26.refs_1_ = bf16[48,1152]{1,0:T(8,128)(2,1)S(1)} collective-permute-done((bf16[48,1152]{1,0:T(8,128)(2,1)S(1)}, bf16[48,1152]{1,0:T(8,128)(2,1)S(1)}, u32[]{:S(2)}, u32[]{:S(2)}) %collective-permute-start.26) | collective-permute-done | bytes 110624 | tf_op jit(solution)/shard_map/ppermute | solution.py:44
  104.0 1.8 %collective-permute-done.28.refs_3_ = bf16[48,1152]{1,0:T(8,128)(2,1)S(1)} collective-permute-done((bf16[48,1152]{1,0:T(8,128)(2,1)S(1)}, bf16[48,1152]{1,0:T(8,128)(2,1)S(1)}, u32[]{:S(2)}, u32[]{:S(2)}) %collective-permute-start.28) | collective-permute-done | bytes 110624 | tf_op jit(solution)/shard_map/ppermute | solution.py:44
  (61 shorter events, 21.4 us)
Async XLA Ops:
  2.0 30.3 %collective-permute-start.3 = (bf16[128,2304]{1,0:T(8,128)(2,1)S(1)}, bf16[128,2304]{1,0:T(8,128)(2,1)S(1)}, u32[]{:S(2)}, u32[]{:S(2)}) collective-permute-start(bf16[128,2304]{1,0:T(8,128)(2,1)S(1)} %get-tuple-element.27), channel_id=1, source_target_pairs={{0,2},{2,0},{4,6},{6,4},{8,10},{10,8},{12,14},{14,12},{1,3},{3,1},... | collective-permute-start | bytes 1769480 | tf_op jit(solution)/shard_map/ppermute | solution.py:17
  5.1 24.1 %collective-permute-start.5 = (bf16[1152,128]{1,0:T(8,128)(2,1)S(1)}, bf16[1152,128]{1,0:T(8,128)(2,1)S(1)}, u32[]{:S(2)}, u32[]{:S(2)}) collective-permute-start(bf16[1152,128]{1,0:T(8,128)(2,1)S(1)} %get-tuple-element.28), channel_id=1, source_target_pairs={{0,2},{2,0},{4,6},{6,4},{8,10},{10,8},{12,14},{14,12},{1,3},{3,1},... | collective-permute-start | bytes 884744 | tf_op jit(solution)/shard_map/ppermute | solution.py:17
  5.1 27.2 %collective-permute-start = (bf16[48,4608]{1,0:T(8,128)(2,1)S(1)}, bf16[48,4608]{1,0:T(8,128)(2,1)S(1)}, u32[]{:S(2)}, u32[]{:S(2)}) collective-permute-start(bf16[48,4608]{1,0:T(8,128)(2,1)S(1)} %copy-done.4), channel_id=1, source_target_pairs={{0,4},{2,6},{4,0},{6,2},{8,12},{10,14},{12,8},{14,10},{1,5},{3,7},... | collective-permute-start | bytes 1327112 | tf_op jit(solution)/shard_map/ppermute | solution.py:17
  7.2 20.7 %collective-permute-start.19 = (bf16[64,1152]{1,0:T(8,128)(2,1)S(1)}, bf16[64,1152]{1,0:T(8,128)(2,1)S(1)}, u32[]{:S(2)}, u32[]{:S(2)}) collective-permute-start(bf16[64,1152]{1,0:T(8,128)(2,1)S(1)} %get-tuple-element.38), channel_id=1, source_target_pairs={{0,2},{2,0},{4,6},{6,4},{8,10},{10,8},{12,14},{14,12},{1,3},{3,1},... | collective-permute-start | bytes 442376 | tf_op jit(solution)/shard_map/ppermute | solution.py:17
  8.7 24.8 %collective-permute-start.1 = (bf16[48,4608]{1,0:T(8,128)(2,1)S(1)}, bf16[48,4608]{1,0:T(8,128)(2,1)S(1)}, u32[]{:S(2)}, u32[]{:S(2)}) collective-permute-start(bf16[48,4608]{1,0:T(8,128)(2,1)S(1)} %copy-done.4), channel_id=1, source_target_pairs={{0,8},{2,10},{12,4},{14,6},{1,9},{3,11},{13,5},{15,7},{16,24},{18,... | collective-permute-start | bytes 1327112 | tf_op jit(solution)/shard_map/ppermute | solution.py:17
  27.9 18.2 %collective-permute-start.2 = (bf16[48,4608]{1,0:T(8,128)(2,1)S(1)}, bf16[48,4608]{1,0:T(8,128)(2,1)S(1)}, u32[]{:S(2)}, u32[]{:S(2)}) collective-permute-start(bf16[48,4608]{1,0:T(8,128)(2,1)S(1)} %copy-done.4), channel_id=1, source_target_pairs={{4,12},{6,14},{8,0},{10,2},{5,13},{7,15},{9,1},{11,3},{20,28},{22,... | collective-permute-start | bytes 1327112 | tf_op jit(solution)/shard_map/ppermute | solution.py:17
  30.6 16.1 %collective-permute-start.6 = (bf16[1152,128]{1,0:T(8,128)(2,1)S(1)}, bf16[1152,128]{1,0:T(8,128)(2,1)S(1)}, u32[]{:S(2)}, u32[]{:S(2)}) collective-permute-start(bf16[1152,128]{1,0:T(8,128)(2,1)S(1)} %collective-permute-done.5.refs_10_.refs_5_), channel_id=1, source_target_pairs={{0,16},{2,18},{4,20},{6,22},{8,24},{10,26},{12,28},{14,30},{16,0},... | collective-permute-start | bytes 884744 | tf_op jit(solution)/shard_map/ppermute | solution.py:44
  32.3 15.7 %collective-permute-start.7 = (bf16[1152,128]{1,0:T(8,128)(2,1)S(1)}, bf16[1152,128]{1,0:T(8,128)(2,1)S(1)}, u32[]{:S(2)}, u32[]{:S(2)}) collective-permute-start(bf16[1152,128]{1,0:T(8,128)(2,1)S(1)} %collective-permute-done.5.refs_10_.refs_5_), channel_id=1, source_target_pairs={{0,1},{1,0},{2,3},{3,2},{4,5},{5,4},{6,7},{7,6},{8,9},{9,8},{10,11... | collective-permute-start | bytes 884744 | tf_op jit(solution)/shard_map/ppermute | solution.py:22
  32.3 17.4 %collective-permute-start.4 = (bf16[128,2304]{1,0:T(8,128)(2,1)S(1)}, bf16[128,2304]{1,0:T(8,128)(2,1)S(1)}, u32[]{:S(2)}, u32[]{:S(2)}) collective-permute-start(bf16[128,2304]{1,0:T(8,128)(2,1)S(1)} %collective-permute-done.3.refs_8_.refs_3_), channel_id=1, source_target_pairs={{0,1},{1,0},{2,3},{3,2},{4,5},{5,4},{6,7},{7,6},{8,9},{9,8},{10,11... | collective-permute-start | bytes 1769480 | tf_op jit(solution)/shard_map/ppermute | solution.py:22
  33.5 34.2 %collective-permute-start.21 = (bf16[256,1152]{1,0:T(8,128)(2,1)S(1)}, bf16[256,1152]{1,0:T(8,128)(2,1)S(1)}, u32[]{:S(2)}, u32[]{:S(2)}) collective-permute-start(bf16[256,1152]{1,0:T(8,128)(2,1)S(1)} %shard_map.78.refs_5_), channel_id=1, source_target_pairs={{0,4},{1,9},{2,6},{3,11},{4,0},{5,13},{6,2},{7,15},{8,12},{9,1},{1... | collective-permute-start | bytes 1769480 | tf_op jit(solution)/shard_map/ppermute | solution.py:33
  46.0 5.8 %collective-permute-start.9 = (bf16[48,4608]{1,0:T(8,128)(2,1)S(1)}, bf16[48,4608]{1,0:T(8,128)(2,1)S(1)}, u32[]{:S(2)}, u32[]{:S(2)}) collective-permute-start(bf16[48,4608]{1,0:T(8,128)(2,1)S(1)} %copy-done.4), channel_id=1, source_target_pairs={{4,8},{6,10},{8,4},{10,6},{5,9},{7,11},{9,5},{11,7},{20,24},{22,26... | collective-permute-start | bytes 1327112 | tf_op jit(solution)/shard_map/ppermute | solution.py:17
  46.7 17.4 %collective-permute-start.10 = (bf16[48,4608]{1,0:T(8,128)(2,1)S(1)}, bf16[48,4608]{1,0:T(8,128)(2,1)S(1)}, u32[]{:S(2)}, u32[]{:S(2)}) collective-permute-start(bf16[48,4608]{1,0:T(8,128)(2,1)S(1)} %collective-permute-done.1.refs_3_), channel_id=1, source_target_pairs={{4,0},{6,2},{8,12},{10,14},{5,1},{7,3},{9,13},{11,15},{20,16},{22,... | collective-permute-start | bytes 1327112 | tf_op jit(solution)/shard_map/ppermute | solution.py:17
  66.1 4.7 %collective-permute-start.11 = (bf16[192,256]{1,0:T(8,128)(2,1)S(1)}, bf16[192,256]{1,0:T(8,128)(2,1)S(1)}, u32[]{:S(2)}, u32[]{:S(2)}) collective-permute-start(bf16[192,256]{1,0:T(8,128)(2,1)S(1)} %get-tuple-element.32.refs_3_), channel_id=1, source_target_pairs={{0,2},{2,0},{4,6},{6,4},{8,10},{10,8},{12,14},{14,12},{1,3},{3,1},... | collective-permute-start | bytes 294920 | tf_op jit(solution)/shard_map/ppermute | solution.py:17
  67.7 18.6 %collective-permute-start.22 = (bf16[256,1152]{1,0:T(8,128)(2,1)S(1)}, bf16[256,1152]{1,0:T(8,128)(2,1)S(1)}, u32[]{:S(2)}, u32[]{:S(2)}) collective-permute-start(bf16[256,1152]{1,0:T(8,128)(2,1)S(1)} %broadcast_select_fusion), channel_id=1, source_target_pairs={{4,8},{5,1},{6,10},{7,3},{8,4},{9,13},{10,6},{11,15},{20,24},{21,1... | collective-permute-start | bytes 1769480 | tf_op jit(solution)/shard_map/ppermute | solution.py:33
  75.3 5.6 %collective-permute-start.15 = (bf16[48,256]{1,0:T(8,128)(2,1)S(1)}, bf16[48,256]{1,0:T(8,128)(2,1)S(1)}, u32[]{:S(2)}, u32[]{:S(2)}) collective-permute-start(bf16[48,256]{1,0:T(8,128)(2,1)S(1)} %get-tuple-element.36), channel_id=1, source_target_pairs={{0,8},{2,10},{4,12},{6,14},{8,0},{10,2},{12,4},{14,6},{1,9},{3,11}... | collective-permute-start | bytes 73736 | tf_op jit(solution)/shard_map/ppermute | solution.py:17
  78.1 5.6 %collective-permute-start.16 = (bf16[48,256]{1,0:T(8,128)(2,1)S(1)}, bf16[48,256]{1,0:T(8,128)(2,1)S(1)}, u32[]{:S(2)}, u32[]{:S(2)}) collective-permute-start(bf16[48,256]{1,0:T(8,128)(2,1)S(1)} %get-tuple-element.37), channel_id=1, source_target_pairs={{0,12},{2,14},{4,8},{6,10},{8,4},{10,6},{12,0},{14,2},{1,13},{3,15... | collective-permute-start | bytes 73736 | tf_op jit(solution)/shard_map/ppermute | solution.py:17
  83.7 5.6 %collective-permute-start.23 = (bf16[48,1024]{1,0:T(8,128)(2,1)S(1)}, bf16[48,1024]{1,0:T(8,128)(2,1)S(1)}, u32[]{:S(2)}, u32[]{:S(2)}) collective-permute-start(bf16[48,1024]{1,0:T(8,128)(2,1)S(1)} %pad_maximum_fusion.refs_1_), channel_id=1, source_target_pairs={{0,18},{2,16},{4,22},{6,20},{8,26},{10,24},{12,30},{14,28},{16,2},... | collective-permute-start | bytes 294920 | tf_op jit(solution)/shard_map/ppermute | solution.py:44
  86.3 6.1 %collective-permute-start.24 = (bf16[256,1152]{1,0:T(8,128)(2,1)S(1)}, bf16[256,1152]{1,0:T(8,128)(2,1)S(1)}, u32[]{:S(2)}, u32[]{:S(2)}) collective-permute-start(bf16[256,1152]{1,0:T(8,128)(2,1)S(1)} %collective-permute-done.21.refs_6_), channel_id=1, source_target_pairs={{0,1},{1,0},{2,3},{3,2},{4,5},{5,4},{6,7},{7,6},{8,9},{9,8},{10,11... | collective-permute-start | bytes 1769480 | tf_op jit(solution)/shard_map/ppermute | solution.py:22
  89.3 7.6 %collective-permute-start.25 = (bf16[256,1152]{1,0:T(8,128)(2,1)S(1)}, bf16[256,1152]{1,0:T(8,128)(2,1)S(1)}, u32[]{:S(2)}, u32[]{:S(2)}) collective-permute-start(bf16[256,1152]{1,0:T(8,128)(2,1)S(1)} %collective-permute-done.22.refs_6_), channel_id=1, source_target_pairs={{0,1},{1,0},{2,3},{3,2},{4,5},{5,4},{6,7},{7,6},{8,9},{9,8},{10,11... | collective-permute-start | bytes 1769480 | tf_op jit(solution)/shard_map/ppermute | solution.py:22
  89.3 5.2 %collective-permute-start.17 = (bf16[48,1024]{1,0:T(8,128)(2,1)S(1)}, bf16[48,1024]{1,0:T(8,128)(2,1)S(1)}, u32[]{:S(2)}, u32[]{:S(2)}) collective-permute-start(bf16[48,1024]{1,0:T(8,128)(2,1)S(1)} %pad_maximum_fusion.refs_1_), channel_id=1, source_target_pairs={{0,2},{2,0},{4,6},{6,4},{8,10},{10,8},{12,14},{14,12},{16,18},{18,... | collective-permute-start | bytes 294920 | tf_op jit(solution)/shard_map/ppermute | solution.py:44
  90.8 4.9 %collective-permute-start.18 = (bf16[48,1024]{1,0:T(8,128)(2,1)S(1)}, bf16[48,1024]{1,0:T(8,128)(2,1)S(1)}, u32[]{:S(2)}, u32[]{:S(2)}) collective-permute-start(bf16[48,1024]{1,0:T(8,128)(2,1)S(1)} %pad_maximum_fusion.refs_1_), channel_id=1, source_target_pairs={{0,16},{2,18},{4,20},{6,22},{8,24},{10,26},{12,28},{14,30},{16,0},... | collective-permute-start | bytes 294920 | tf_op jit(solution)/shard_map/ppermute | solution.py:44
  97.8 5.9 %collective-permute-start.26 = (bf16[48,1152]{1,0:T(8,128)(2,1)S(1)}, bf16[48,1152]{1,0:T(8,128)(2,1)S(1)}, u32[]{:S(2)}, u32[]{:S(2)}) collective-permute-start(bf16[48,1152]{1,0:T(8,128)(2,1)S(1)} %get-tuple-element.42), channel_id=1, source_target_pairs={{0,2},{2,0},{4,6},{6,4},{8,10},{10,8},{12,14},{14,12},{16,18},{18,... | collective-permute-start | bytes 331784 | tf_op jit(solution)/shard_map/ppermute | solution.py:44
  98.4 5.6 %collective-permute-start.27 = (bf16[48,1152]{1,0:T(8,128)(2,1)S(1)}, bf16[48,1152]{1,0:T(8,128)(2,1)S(1)}, u32[]{:S(2)}, u32[]{:S(2)}) collective-permute-start(bf16[48,1152]{1,0:T(8,128)(2,1)S(1)} %get-tuple-element.43), channel_id=1, source_target_pairs={{0,16},{2,18},{4,20},{6,22},{8,24},{10,26},{12,28},{14,30},{16,0},... | collective-permute-start | bytes 331784 | tf_op jit(solution)/shard_map/ppermute | solution.py:44
  99.9 5.9 %collective-permute-start.28 = (bf16[48,1152]{1,0:T(8,128)(2,1)S(1)}, bf16[48,1152]{1,0:T(8,128)(2,1)S(1)}, u32[]{:S(2)}, u32[]{:S(2)}) collective-permute-start(bf16[48,1152]{1,0:T(8,128)(2,1)S(1)} %get-tuple-element.44), channel_id=1, source_target_pairs={{0,18},{2,16},{4,22},{6,20},{8,26},{10,24},{12,30},{14,28},{16,2},... | collective-permute-start | bytes 331784 | tf_op jit(solution)/shard_map/ppermute | solution.py:44
  (12 other events, 246.3 us)

commit v9 on v8

--- a/solution.py
+++ b/solution.py
@@ -203,17 +203,22 @@
             out[:, head:] = high[k * rows : (k + 1) * rows]
 
 
-def cut_kernel(flags, w_query, w_key, w_value, w_out, share_q, share_kv, out_sent, sems):
-    sp, group = flags[0], flags[3]
-    head = w_key.shape[0]
-    quarter_depth, depth = share_q.shape[0], share_kv.shape[1]
+def cut_query_kernel(flags, w_query, share_q, sem):
+    quarter_depth = share_q.shape[0]
+    at = pl.multiple_of((flags[0] * 2 + flags[3]) * quarter_depth, 128)
+    copy = pltpu.make_async_copy(w_query.at[pl.ds(at, quarter_depth)], share_q, sem)
+    copy.start()
+    copy.wait()
+
+
+def cut_kernel(flags, w_key, w_value, w_out, share_kv, out_sent, sems):
+    sp = flags[0]
+    head, depth = w_key.shape[0], share_kv.shape[1]
     half_rows, quarter = out_sent.shape
-    rows = pl.ds(pl.multiple_of((sp * 2 + group) * quarter_depth, 128), quarter_depth)
     deep = pl.ds(pl.multiple_of(sp * depth, 128), depth)
     columns = pl.ds(pl.multiple_of((flags[4] ^ 1) * quarter, 128), quarter)
     heads = pl.ds(pl.multiple_of(sp * half_rows, half_rows), half_rows)
     moves = (
-        (w_query.at[rows], share_q),
         (w_key.at[:, deep], share_kv.at[:head]),
         (w_value.at[:, deep], share_kv.at[head:]),
         (w_out.at[heads, columns], out_sent),
@@ -310,18 +315,25 @@
     turned_kv = [w_key.T, w_value.T]
     core_low = sp_place == 0
     flags, doc_lengths, core_low = fence(flags, doc_lengths, core_low)
-    share_q, share_kv, out_sent = call(
+    in_hbm = lambda *arrays: [pltpu.with_memory_space_constraint(x, pltpu.HBM) for x in arrays]
+    place = pltpu.VMEM if short else pl.ANY
+    share_q = call(
+        cut_query_kernel,
+        [((depth // 2, head_dim), jnp.bfloat16)],
+        [flags],
+        [],
+        [pltpu.SemaphoreType.DMA(())],
+        place,
+        in_hbm(w_query),
+    )[0]
+    share_kv, out_sent = call(
         cut_kernel,
-        [
-            ((depth // 2, head_dim), jnp.bfloat16),
-            ((head_dim, depth), jnp.bfloat16),
-            ((half_rows, quarter), jnp.bfloat16),
-        ],
+        [((head_dim, depth), jnp.bfloat16), ((half_rows, quarter), jnp.bfloat16)],
         [flags],
         [],
-        [pltpu.SemaphoreType.DMA((4,))],
-        pltpu.VMEM if short else pl.ANY,
-        [pltpu.with_memory_space_constraint(x, pltpu.HBM) for x in (w_query, *turned_kv, w_out)],
+        [pltpu.SemaphoreType.DMA((3,))],
+        place,
+        in_hbm(*turned_kv, w_out),
     )
     came_q = swap_tp(share_q, 1)
     cross_q = swap_in_slab(came_q, 1, 0)

time: 107 us -> 107 us (level)
  starting transfers between devices: 37.5 us -> 36.1 us
  Pallas kernels: 12.7 us -> 14 us
    ppermute x12, starting transfers between devices: 20.4 us -> 19 us  [swap_tp(): return lax.ppermute(block, 'tp', route)]
    pallas_call x9 -> x10, Pallas kernels: 12.7 us -> 14 us  [call(): pl.pallas_call(kernel, in_specs=specs, out_specs=[pl.BlockSpec(memory_spa...]
  transfers between devices with their start and end apart: 29 -> 29, of which waited for: 15 -> 15; matrix products, arithmetic and copies ran while one was open for 0% -> 0% of each run, Pallas kernels for 8% -> 9%
where the time goes in v9:
time: 107 us
  waiting for transfers between devices  56.3 us (53%)
  starting transfers between devices  36.1 us (34%)
  Pallas kernels  14 us (13%)
    ppermute x12, waiting for transfers between devices, swap_tp(): return lax.ppermute(block, 'tp', route)  42.1 us
    ppermute x12, starting transfers between devices, swap_tp(): return lax.ppermute(block, 'tp', route)  19 us
    pallas_call x10, Pallas kernels, call(): pl.pallas_call(kernel, in_specs=specs, out_specs=[pl.BlockSpec(memory_spa...  14 us
    ppermute x7, waiting for transfers between devices, swap_in_slab(): return lax.ppermute(block, ('groups', 'tp'), route)  10.9 us
    ppermute x7, starting transfers between devices, swap_in_slab(): return lax.ppermute(block, ('groups', 'tp'), route)  10.8 us
    ppermute x2, starting transfers between devices, swap_by_core(): return lax.ppermute(block, ('tp', 'sp'), route)  5.57 us
    ppermute x8, waiting for transfers between devices, swap_sp(): return lax.ppermute(block, 'sp', [(s, s ^ 1) for s in range(count)])  3.3 us
  transfers between devices with their start and end apart: 29, of which 15 were waited for; matrix products, arithmetic and copies ran while one was open for 0% of the time, Pallas kernels for 9%

profile of v9, /device:TPU:0, one launch (start us, length us, event | category | flops | bytes accessed | tf_op | source)
XLA Modules:
  0.0 106.9 jit_solution(8456800979875815586)
XLA Ops:
  0.1 1.7 %shard_map.73 = (bf16[128,2304]{1,0:T(8,128)(2,1)S(1)}, bf16[64,1152]{1,0:T(8,128)(2,1)S(1)}) custom-call(s32[6]{0:T(128)S(1)} %stack.31.flags.refs_0_, bf16[64,4608]{1,0:T(8,128)(2,1)} %bitcast.8, bf16[64,4608]{1,0:T(8,128)(2,1)} %bitcast.11, bf16[128,4608]{1,0:T(8,128)(2,1)} %w_out.3), custom_call_target="tpu_custom_call" | custom-call | tf_op jit(solution)/shard_map/pallas_call | solution.py:60
  1.8 3.1 %collective-permute-start.3 = (bf16[128,2304]{1,0:T(8,128)(2,1)S(1)}, bf16[128,2304]{1,0:T(8,128)(2,1)S(1)}, u32[]{:S(2)}, u32[]{:S(2)}) collective-permute-start(bf16[128,2304]{1,0:T(8,128)(2,1)S(1)} %get-tuple-element.26), channel_id=1, source_target_pairs={{0,2},{2,0},{4,6},{6,4},{8,10},{10,8},{12,14},{14,12},{1,3},{3,1},... | collective-permute-start | bytes 1769480 | tf_op jit(solution)/shard_map/ppermute | solution.py:17
  4.8 1.5 %shard_map.74 = bf16[1152,128]{1,0:T(8,128)(2,1)S(1)} custom-call(s32[6]{0:T(128)S(1)} %stack.31.flags.refs_0_, bf16[4608,128]{1,0:T(8,128)(2,1)} %refs_0_.1), custom_call_target="tpu_custom_call" | custom-call | tf_op jit(solution)/shard_map/pallas_call | solution.py:60
  6.5 5.0 %collective-permute-start.1 = (bf16[48,4608]{1,0:T(8,128)(2,1)S(1)}, bf16[48,4608]{1,0:T(8,128)(2,1)S(1)}, u32[]{:S(2)}, u32[]{:S(2)}) collective-permute-start(bf16[48,4608]{1,0:T(8,128)(2,1)S(1)} %copy-done.4), channel_id=1, source_target_pairs={{0,8},{2,10},{12,4},{14,6},{1,9},{3,11},{13,5},{15,7},{16,24},{18,... | collective-permute-start | bytes 1327112 | tf_op jit(solution)/shard_map/ppermute | solution.py:17
  11.5 1.6 %collective-permute-start.19 = (bf16[64,1152]{1,0:T(8,128)(2,1)S(1)}, bf16[64,1152]{1,0:T(8,128)(2,1)S(1)}, u32[]{:S(2)}, u32[]{:S(2)}) collective-permute-start(bf16[64,1152]{1,0:T(8,128)(2,1)S(1)} %get-tuple-element.36), channel_id=1, source_target_pairs={{0,2},{2,0},{4,6},{6,4},{8,10},{10,8},{12,14},{14,12},{1,3},{3,1},... | collective-permute-start | bytes 442376 | tf_op jit(solution)/shard_map/ppermute | solution.py:17
  13.1 14.6 %collective-permute-done.19.came = bf16[64,1152]{1,0:T(8,128)(2,1)S(1)} collective-permute-done((bf16[64,1152]{1,0:T(8,128)(2,1)S(1)}, bf16[64,1152]{1,0:T(8,128)(2,1)S(1)}, u32[]{:S(2)}, u32[]{:S(2)}) %collective-permute-start.19) | collective-permute-done | bytes 147488 | tf_op jit(solution)/shard_map/ppermute | solution.py:17
  30.4 1.7 %collective-permute-start.6 = (bf16[1152,128]{1,0:T(8,128)(2,1)S(1)}, bf16[1152,128]{1,0:T(8,128)(2,1)S(1)}, u32[]{:S(2)}, u32[]{:S(2)}) collective-permute-start(bf16[1152,128]{1,0:T(8,128)(2,1)S(1)} %collective-permute-done.5.refs_10_.refs_5_), channel_id=1, source_target_pairs={{0,16},{2,18},{4,20},{6,22},{8,24},{10,26},{12,28},{14,30},{16,0},... | collective-permute-start | bytes 884744 | tf_op jit(solution)/shard_map/ppermute | solution.py:44
  33.2 4.9 %collective-permute-start.21 = (bf16[256,1152]{1,0:T(8,128)(2,1)S(1)}, bf16[256,1152]{1,0:T(8,128)(2,1)S(1)}, u32[]{:S(2)}, u32[]{:S(2)}) collective-permute-start(bf16[256,1152]{1,0:T(8,128)(2,1)S(1)} %shard_map.79.refs_5_), channel_id=1, source_target_pairs={{0,4},{1,9},{2,6},{3,11},{4,0},{5,13},{6,2},{7,15},{8,12},{9,1},{1... | collective-permute-start | bytes 1769480 | tf_op jit(solution)/shard_map/ppermute | solution.py:33
  38.1 7.7 %collective-permute-done.2.refs_4_ = bf16[48,4608]{1,0:T(8,128)(2,1)S(1)} collective-permute-done((bf16[48,4608]{1,0:T(8,128)(2,1)S(1)}, bf16[48,4608]{1,0:T(8,128)(2,1)S(1)}, u32[]{:S(2)}, u32[]{:S(2)}) %collective-permute-start.2) | collective-permute-done | bytes 442400 | tf_op jit(solution)/shard_map/ppermute | solution.py:17
  49.5 2.1 %shard_map.75.early = f32[144,512]{1,0:T(8,128)S(1)} custom-call(s32[6]{0:T(128)S(1)} %stack.31.flags.refs_0_, bf16[48,4608]{1,0:T(8,128)(2,1)S(1)} %copy-done.4, bf16[48,4608]{1,0:T(8,128)(2,1)S(1)} %collective-permute-done.refs_2_, bf16[48,4608]{1,0:T(8,128)(2,1)S(1)} %collective-permute-done.1.refs_3_, ...), custom_call_target="tpu_custom_call" | custom-call | tf_op jit(solution)/shard_map/pallas_call | solution.py:60
  51.6 12.2 %collective-permute-done.10.relayed = bf16[48,4608]{1,0:T(8,128)(2,1)S(1)} collective-permute-done((bf16[48,4608]{1,0:T(8,128)(2,1)S(1)}, bf16[48,4608]{1,0:T(8,128)(2,1)S(1)}, u32[]{:S(2)}, u32[]{:S(2)}) %collective-permute-start.10) | collective-permute-done | bytes 442400 | tf_op jit(solution)/shard_map/ppermute | solution.py:17
  63.9 2.0 %shard_map.77 = (bf16[384,128]{1,0:T(8,128)(2,1)S(1)}, bf16[192,256]{1,0:T(8,128)(2,1)S(1)}) custom-call(s32[6]{0:T(128)S(1)} %stack.31.flags.refs_0_, f32[144,512]{1,0:T(8,128)S(1)} %shard_map.75.early, bf16[48,4608]{1,0:T(8,128)(2,1)S(1)} %collective-permute-done.9.middle, bf16[48,4608]{1,0:T(8,128)(2,1)S(1)} %collective-permute-done.10.relayed, ...), custom_call_target="tpu_custom_call" | custom-call | tf_op jit(solution)/shard_map/pallas_call | solution.py:60
  65.9 1.5 %collective-permute-start.11 = (bf16[192,256]{1,0:T(8,128)(2,1)S(1)}, bf16[192,256]{1,0:T(8,128)(2,1)S(1)}, u32[]{:S(2)}, u32[]{:S(2)}) collective-permute-start(bf16[192,256]{1,0:T(8,128)(2,1)S(1)} %get-tuple-element.30.refs_3_), channel_id=1, source_target_pairs={{0,2},{2,0},{4,6},{6,4},{8,10},{10,8},{12,14},{14,12},{1,3},{3,1},... | collective-permute-start | bytes 294920 | tf_op jit(solution)/shard_map/ppermute | solution.py:17
  68.2 2.3 %collective-permute-done.11.refs_4_ = bf16[192,256]{1,0:T(8,128)(2,1)S(1)} collective-permute-done((bf16[192,256]{1,0:T(8,128)(2,1)S(1)}, bf16[192,256]{1,0:T(8,128)(2,1)S(1)}, u32[]{:S(2)}, u32[]{:S(2)}) %collective-permute-start.11) | collective-permute-done | bytes 98336 | tf_op jit(solution)/shard_map/ppermute | solution.py:17
  71.8 1.8 %shard_map.78 = (bf16[48,256]{1,0:T(8,128)(2,1)S(1)}, bf16[48,256]{1,0:T(8,128)(2,1)S(1)}, bf16[48,256]{1,0:T(8,128)(2,1)S(1)}, bf16[48,256]{1,0:T(8,128)(2,1)S(1)}) custom-call(s32[6]{0:T(128)S(1)} %stack.31.flags.refs_0_, s32[8]{0:T(128)S(1)} %copy-done.5, bf16[384,128]{1,0:T(8,128)(2,1)S(1)} %get-tuple-element.29.refs_2_, ...), custom_call_target="tpu_custom_call" | custom-call | tf_op jit(solution)/shard_map/pallas_call | solution.py:60
  75.0 2.8 %collective-permute-start.15 = (bf16[48,256]{1,0:T(8,128)(2,1)S(1)}, bf16[48,256]{1,0:T(8,128)(2,1)S(1)}, u32[]{:S(2)}, u32[]{:S(2)}) collective-permute-start(bf16[48,256]{1,0:T(8,128)(2,1)S(1)} %get-tuple-element.34), channel_id=1, source_target_pairs={{0,8},{2,10},{4,12},{6,14},{8,0},{10,2},{12,4},{14,6},{1,9},{3,11}... | collective-permute-start | bytes 73736 | tf_op jit(solution)/shard_map/ppermute | solution.py:17
  78.1 2.5 %collective-permute-done.15 = bf16[48,256]{1,0:T(8,128)(2,1)S(1)} collective-permute-done((bf16[48,256]{1,0:T(8,128)(2,1)S(1)}, bf16[48,256]{1,0:T(8,128)(2,1)S(1)}, u32[]{:S(2)}, u32[]{:S(2)}) %collective-permute-start.15) | collective-permute-done | bytes 24608 | tf_op jit(solution)/shard_map/ppermute | solution.py:17
  80.6 2.9 %collective-permute-done.16 = bf16[48,256]{1,0:T(8,128)(2,1)S(1)} collective-permute-done((bf16[48,256]{1,0:T(8,128)(2,1)S(1)}, bf16[48,256]{1,0:T(8,128)(2,1)S(1)}, u32[]{:S(2)}, u32[]{:S(2)}) %collective-permute-start.16) | collective-permute-done | bytes 24608 | tf_op jit(solution)/shard_map/ppermute | solution.py:17
  83.5 2.5 %collective-permute-start.23 = (bf16[48,1024]{1,0:T(8,128)(2,1)S(1)}, bf16[48,1024]{1,0:T(8,128)(2,1)S(1)}, u32[]{:S(2)}, u32[]{:S(2)}) collective-permute-start(bf16[48,1024]{1,0:T(8,128)(2,1)S(1)} %pad_maximum_fusion.refs_1_), channel_id=1, source_target_pairs={{0,18},{2,16},{4,22},{6,20},{8,26},{10,24},{12,30},{14,28},{16,2},... | collective-permute-start | bytes 294920 | tf_op jit(solution)/shard_map/ppermute | solution.py:44
  86.0 3.0 %collective-permute-done.23.refs_4_ = bf16[48,1024]{1,0:T(8,128)(2,1)S(1)} collective-permute-done((bf16[48,1024]{1,0:T(8,128)(2,1)S(1)}, bf16[48,1024]{1,0:T(8,128)(2,1)S(1)}, u32[]{:S(2)}, u32[]{:S(2)}) %collective-permute-start.23) | collective-permute-done | bytes 98336 | tf_op jit(solution)/shard_map/ppermute | solution.py:44
  89.1 1.5 %collective-permute-start.17 = (bf16[48,1024]{1,0:T(8,128)(2,1)S(1)}, bf16[48,1024]{1,0:T(8,128)(2,1)S(1)}, u32[]{:S(2)}, u32[]{:S(2)}) collective-permute-start(bf16[48,1024]{1,0:T(8,128)(2,1)S(1)} %pad_maximum_fusion.refs_1_), channel_id=1, source_target_pairs={{0,2},{2,0},{4,6},{6,4},{8,10},{10,8},{12,14},{14,12},{16,18},{18,... | collective-permute-start | bytes 294920 | tf_op jit(solution)/shard_map/ppermute | solution.py:44
  92.1 2.2 %collective-permute-done.17.refs_2_ = bf16[48,1024]{1,0:T(8,128)(2,1)S(1)} collective-permute-done((bf16[48,1024]{1,0:T(8,128)(2,1)S(1)}, bf16[48,1024]{1,0:T(8,128)(2,1)S(1)}, u32[]{:S(2)}, u32[]{:S(2)}) %collective-permute-start.17) | collective-permute-done | bytes 98336 | tf_op jit(solution)/shard_map/ppermute | solution.py:44
  101.1 2.3 %collective-permute-done.26.refs_1_ = bf16[48,1152]{1,0:T(8,128)(2,1)S(1)} collective-permute-done((bf16[48,1152]{1,0:T(8,128)(2,1)S(1)}, bf16[48,1152]{1,0:T(8,128)(2,1)S(1)}, u32[]{:S(2)}, u32[]{:S(2)}) %collective-permute-start.26) | collective-permute-done | bytes 110624 | tf_op jit(solution)/shard_map/ppermute | solution.py:44
  103.7 1.8 %collective-permute-done.28.refs_3_ = bf16[48,1152]{1,0:T(8,128)(2,1)S(1)} collective-permute-done((bf16[48,1152]{1,0:T(8,128)(2,1)S(1)}, bf16[48,1152]{1,0:T(8,128)(2,1)S(1)}, u32[]{:S(2)}, u32[]{:S(2)}) %collective-permute-start.28) | collective-permute-done | bytes 110624 | tf_op jit(solution)/shard_map/ppermute | solution.py:44
  (62 shorter events, 21.5 us)
Async XLA Ops:
  1.8 30.3 %collective-permute-start.3 = (bf16[128,2304]{1,0:T(8,128)(2,1)S(1)}, bf16[128,2304]{1,0:T(8,128)(2,1)S(1)}, u32[]{:S(2)}, u32[]{:S(2)}) collective-permute-start(bf16[128,2304]{1,0:T(8,128)(2,1)S(1)} %get-tuple-element.26), channel_id=1, source_target_pairs={{0,2},{2,0},{4,6},{6,4},{8,10},{10,8},{12,14},{14,12},{1,3},{3,1},... | collective-permute-start | bytes 1769480 | tf_op jit(solution)/shard_map/ppermute | solution.py:17
  6.4 22.5 %collective-permute-start.5 = (bf16[1152,128]{1,0:T(8,128)(2,1)S(1)}, bf16[1152,128]{1,0:T(8,128)(2,1)S(1)}, u32[]{:S(2)}, u32[]{:S(2)}) collective-permute-start(bf16[1152,128]{1,0:T(8,128)(2,1)S(1)} %shard_map.74), channel_id=1, source_target_pairs={{0,2},{2,0},{4,6},{6,4},{8,10},{10,8},{12,14},{14,12},{1,3},{3,1},... | collective-permute-start | bytes 884744 | tf_op jit(solution)/shard_map/ppermute | solution.py:17
  6.5 25.6 %collective-permute-start.1 = (bf16[48,4608]{1,0:T(8,128)(2,1)S(1)}, bf16[48,4608]{1,0:T(8,128)(2,1)S(1)}, u32[]{:S(2)}, u32[]{:S(2)}) collective-permute-start(bf16[48,4608]{1,0:T(8,128)(2,1)S(1)} %copy-done.4), channel_id=1, source_target_pairs={{0,8},{2,10},{12,4},{14,6},{1,9},{3,11},{13,5},{15,7},{16,24},{18,... | collective-permute-start | bytes 1327112 | tf_op jit(solution)/shard_map/ppermute | solution.py:17
  11.5 16.2 %collective-permute-start.19 = (bf16[64,1152]{1,0:T(8,128)(2,1)S(1)}, bf16[64,1152]{1,0:T(8,128)(2,1)S(1)}, u32[]{:S(2)}, u32[]{:S(2)}) collective-permute-start(bf16[64,1152]{1,0:T(8,128)(2,1)S(1)} %get-tuple-element.36), channel_id=1, source_target_pairs={{0,2},{2,0},{4,6},{6,4},{8,10},{10,8},{12,14},{14,12},{1,3},{3,1},... | collective-permute-start | bytes 442376 | tf_op jit(solution)/shard_map/ppermute | solution.py:17
  13.1 20.2 %collective-permute-start = (bf16[48,4608]{1,0:T(8,128)(2,1)S(1)}, bf16[48,4608]{1,0:T(8,128)(2,1)S(1)}, u32[]{:S(2)}, u32[]{:S(2)}) collective-permute-start(bf16[48,4608]{1,0:T(8,128)(2,1)S(1)} %copy-done.4), channel_id=1, source_target_pairs={{0,4},{2,6},{4,0},{6,2},{8,12},{10,14},{12,8},{14,10},{1,5},{3,7},... | collective-permute-start | bytes 1327112 | tf_op jit(solution)/shard_map/ppermute | solution.py:17
  27.6 18.2 %collective-permute-start.2 = (bf16[48,4608]{1,0:T(8,128)(2,1)S(1)}, bf16[48,4608]{1,0:T(8,128)(2,1)S(1)}, u32[]{:S(2)}, u32[]{:S(2)}) collective-permute-start(bf16[48,4608]{1,0:T(8,128)(2,1)S(1)} %copy-done.4), channel_id=1, source_target_pairs={{4,12},{6,14},{8,0},{10,2},{5,13},{7,15},{9,1},{11,3},{20,28},{22,... | collective-permute-start | bytes 1327112 | tf_op jit(solution)/shard_map/ppermute | solution.py:17
  30.4 16.1 %collective-permute-start.6 = (bf16[1152,128]{1,0:T(8,128)(2,1)S(1)}, bf16[1152,128]{1,0:T(8,128)(2,1)S(1)}, u32[]{:S(2)}, u32[]{:S(2)}) collective-permute-start(bf16[1152,128]{1,0:T(8,128)(2,1)S(1)} %collective-permute-done.5.refs_10_.refs_5_), channel_id=1, source_target_pairs={{0,16},{2,18},{4,20},{6,22},{8,24},{10,26},{12,28},{14,30},{16,0},... | collective-permute-start | bytes 884744 | tf_op jit(solution)/shard_map/ppermute | solution.py:44
  32.1 15.7 %collective-permute-start.7 = (bf16[1152,128]{1,0:T(8,128)(2,1)S(1)}, bf16[1152,128]{1,0:T(8,128)(2,1)S(1)}, u32[]{:S(2)}, u32[]{:S(2)}) collective-permute-start(bf16[1152,128]{1,0:T(8,128)(2,1)S(1)} %collective-permute-done.5.refs_10_.refs_5_), channel_id=1, source_target_pairs={{0,1},{1,0},{2,3},{3,2},{4,5},{5,4},{6,7},{7,6},{8,9},{9,8},{10,11... | collective-permute-start | bytes 884744 | tf_op jit(solution)/shard_map/ppermute | solution.py:22
  32.1 17.4 %collective-permute-start.4 = (bf16[128,2304]{1,0:T(8,128)(2,1)S(1)}, bf16[128,2304]{1,0:T(8,128)(2,1)S(1)}, u32[]{:S(2)}, u32[]{:S(2)}) collective-permute-start(bf16[128,2304]{1,0:T(8,128)(2,1)S(1)} %collective-permute-done.3.refs_8_.refs_3_), channel_id=1, source_target_pairs={{0,1},{1,0},{2,3},{3,2},{4,5},{5,4},{6,7},{7,6},{8,9},{9,8},{10,11... | collective-permute-start | bytes 1769480 | tf_op jit(solution)/shard_map/ppermute | solution.py:22
  33.2 34.2 %collective-permute-start.21 = (bf16[256,1152]{1,0:T(8,128)(2,1)S(1)}, bf16[256,1152]{1,0:T(8,128)(2,1)S(1)}, u32[]{:S(2)}, u32[]{:S(2)}) collective-permute-start(bf16[256,1152]{1,0:T(8,128)(2,1)S(1)} %shard_map.79.refs_5_), channel_id=1, source_target_pairs={{0,4},{1,9},{2,6},{3,11},{4,0},{5,13},{6,2},{7,15},{8,12},{9,1},{1... | collective-permute-start | bytes 1769480 | tf_op jit(solution)/shard_map/ppermute | solution.py:33
  45.8 5.8 %collective-permute-start.9 = (bf16[48,4608]{1,0:T(8,128)(2,1)S(1)}, bf16[48,4608]{1,0:T(8,128)(2,1)S(1)}, u32[]{:S(2)}, u32[]{:S(2)}) collective-permute-start(bf16[48,4608]{1,0:T(8,128)(2,1)S(1)} %copy-done.4), channel_id=1, source_target_pairs={{4,8},{6,10},{8,4},{10,6},{5,9},{7,11},{9,5},{11,7},{20,24},{22,26... | collective-permute-start | bytes 1327112 | tf_op jit(solution)/shard_map/ppermute | solution.py:17
  46.5 17.4 %collective-permute-start.10 = (bf16[48,4608]{1,0:T(8,128)(2,1)S(1)}, bf16[48,4608]{1,0:T(8,128)(2,1)S(1)}, u32[]{:S(2)}, u32[]{:S(2)}) collective-permute-start(bf16[48,4608]{1,0:T(8,128)(2,1)S(1)} %collective-permute-done.1.refs_3_), channel_id=1, source_target_pairs={{4,0},{6,2},{8,12},{10,14},{5,1},{7,3},{9,13},{11,15},{20,16},{22,... | collective-permute-start | bytes 1327112 | tf_op jit(solution)/shard_map/ppermute | solution.py:17
  65.9 4.7 %collective-permute-start.11 = (bf16[192,256]{1,0:T(8,128)(2,1)S(1)}, bf16[192,256]{1,0:T(8,128)(2,1)S(1)}, u32[]{:S(2)}, u32[]{:S(2)}) collective-permute-start(bf16[192,256]{1,0:T(8,128)(2,1)S(1)} %get-tuple-element.30.refs_3_), channel_id=1, source_target_pairs={{0,2},{2,0},{4,6},{6,4},{8,10},{10,8},{12,14},{14,12},{1,3},{3,1},... | collective-permute-start | bytes 294920 | tf_op jit(solution)/shard_map/ppermute | solution.py:17
  67.5 18.6 %collective-permute-start.22 = (bf16[256,1152]{1,0:T(8,128)(2,1)S(1)}, bf16[256,1152]{1,0:T(8,128)(2,1)S(1)}, u32[]{:S(2)}, u32[]{:S(2)}) collective-permute-start(bf16[256,1152]{1,0:T(8,128)(2,1)S(1)} %broadcast_select_fusion), channel_id=1, source_target_pairs={{4,8},{5,1},{6,10},{7,3},{8,4},{9,13},{10,6},{11,15},{20,24},{21,1... | collective-permute-start | bytes 1769480 | tf_op jit(solution)/shard_map/ppermute | solution.py:33
  75.0 5.6 %collective-permute-start.15 = (bf16[48,256]{1,0:T(8,128)(2,1)S(1)}, bf16[48,256]{1,0:T(8,128)(2,1)S(1)}, u32[]{:S(2)}, u32[]{:S(2)}) collective-permute-start(bf16[48,256]{1,0:T(8,128)(2,1)S(1)} %get-tuple-element.34), channel_id=1, source_target_pairs={{0,8},{2,10},{4,12},{6,14},{8,0},{10,2},{12,4},{14,6},{1,9},{3,11}... | collective-permute-start | bytes 73736 | tf_op jit(solution)/shard_map/ppermute | solution.py:17
  77.8 5.6 %collective-permute-start.16 = (bf16[48,256]{1,0:T(8,128)(2,1)S(1)}, bf16[48,256]{1,0:T(8,128)(2,1)S(1)}, u32[]{:S(2)}, u32[]{:S(2)}) collective-permute-start(bf16[48,256]{1,0:T(8,128)(2,1)S(1)} %get-tuple-element.35), channel_id=1, source_target_pairs={{0,12},{2,14},{4,8},{6,10},{8,4},{10,6},{12,0},{14,2},{1,13},{3,15... | collective-permute-start | bytes 73736 | tf_op jit(solution)/shard_map/ppermute | solution.py:17
  83.5 5.6 %collective-permute-start.23 = (bf16[48,1024]{1,0:T(8,128)(2,1)S(1)}, bf16[48,1024]{1,0:T(8,128)(2,1)S(1)}, u32[]{:S(2)}, u32[]{:S(2)}) collective-permute-start(bf16[48,1024]{1,0:T(8,128)(2,1)S(1)} %pad_maximum_fusion.refs_1_), channel_id=1, source_target_pairs={{0,18},{2,16},{4,22},{6,20},{8,26},{10,24},{12,30},{14,28},{16,2},... | collective-permute-start | bytes 294920 | tf_op jit(solution)/shard_map/ppermute | solution.py:44
  86.0 6.1 %collective-permute-start.24 = (bf16[256,1152]{1,0:T(8,128)(2,1)S(1)}, bf16[256,1152]{1,0:T(8,128)(2,1)S(1)}, u32[]{:S(2)}, u32[]{:S(2)}) collective-permute-start(bf16[256,1152]{1,0:T(8,128)(2,1)S(1)} %collective-permute-done.21.refs_6_), channel_id=1, source_target_pairs={{0,1},{1,0},{2,3},{3,2},{4,5},{5,4},{6,7},{7,6},{8,9},{9,8},{10,11... | collective-permute-start | bytes 1769480 | tf_op jit(solution)/shard_map/ppermute | solution.py:22
  89.1 7.6 %collective-permute-start.25 = (bf16[256,1152]{1,0:T(8,128)(2,1)S(1)}, bf16[256,1152]{1,0:T(8,128)(2,1)S(1)}, u32[]{:S(2)}, u32[]{:S(2)}) collective-permute-start(bf16[256,1152]{1,0:T(8,128)(2,1)S(1)} %collective-permute-done.22.refs_6_), channel_id=1, source_target_pairs={{0,1},{1,0},{2,3},{3,2},{4,5},{5,4},{6,7},{7,6},{8,9},{9,8},{10,11... | collective-permute-start | bytes 1769480 | tf_op jit(solution)/shard_map/ppermute | solution.py:22
  89.1 5.2 %collective-permute-start.17 = (bf16[48,1024]{1,0:T(8,128)(2,1)S(1)}, bf16[48,1024]{1,0:T(8,128)(2,1)S(1)}, u32[]{:S(2)}, u32[]{:S(2)}) collective-permute-start(bf16[48,1024]{1,0:T(8,128)(2,1)S(1)} %pad_maximum_fusion.refs_1_), channel_id=1, source_target_pairs={{0,2},{2,0},{4,6},{6,4},{8,10},{10,8},{12,14},{14,12},{16,18},{18,... | collective-permute-start | bytes 294920 | tf_op jit(solution)/shard_map/ppermute | solution.py:44
  90.6 4.9 %collective-permute-start.18 = (bf16[48,1024]{1,0:T(8,128)(2,1)S(1)}, bf16[48,1024]{1,0:T(8,128)(2,1)S(1)}, u32[]{:S(2)}, u32[]{:S(2)}) collective-permute-start(bf16[48,1024]{1,0:T(8,128)(2,1)S(1)} %pad_maximum_fusion.refs_1_), channel_id=1, source_target_pairs={{0,16},{2,18},{4,20},{6,22},{8,24},{10,26},{12,28},{14,30},{16,0},... | collective-permute-start | bytes 294920 | tf_op jit(solution)/shard_map/ppermute | solution.py:44
  97.5 5.8 %collective-permute-start.26 = (bf16[48,1152]{1,0:T(8,128)(2,1)S(1)}, bf16[48,1152]{1,0:T(8,128)(2,1)S(1)}, u32[]{:S(2)}, u32[]{:S(2)}) collective-permute-start(bf16[48,1152]{1,0:T(8,128)(2,1)S(1)} %get-tuple-element.40), channel_id=1, source_target_pairs={{0,2},{2,0},{4,6},{6,4},{8,10},{10,8},{12,14},{14,12},{16,18},{18,... | collective-permute-start | bytes 331784 | tf_op jit(solution)/shard_map/ppermute | solution.py:44
  98.1 5.6 %collective-permute-start.27 = (bf16[48,1152]{1,0:T(8,128)(2,1)S(1)}, bf16[48,1152]{1,0:T(8,128)(2,1)S(1)}, u32[]{:S(2)}, u32[]{:S(2)}) collective-permute-start(bf16[48,1152]{1,0:T(8,128)(2,1)S(1)} %get-tuple-element.41), channel_id=1, source_target_pairs={{0,16},{2,18},{4,20},{6,22},{8,24},{10,26},{12,28},{14,30},{16,0},... | collective-permute-start | bytes 331784 | tf_op jit(solution)/shard_map/ppermute | solution.py:44
  99.6 5.9 %collective-permute-start.28 = (bf16[48,1152]{1,0:T(8,128)(2,1)S(1)}, bf16[48,1152]{1,0:T(8,128)(2,1)S(1)}, u32[]{:S(2)}, u32[]{:S(2)}) collective-permute-start(bf16[48,1152]{1,0:T(8,128)(2,1)S(1)} %get-tuple-element.42), channel_id=1, source_target_pairs={{0,18},{2,16},{4,22},{6,20},{8,26},{10,24},{12,30},{14,28},{16,2},... | collective-permute-start | bytes 331784 | tf_op jit(solution)/shard_map/ppermute | solution.py:44
  (12 other events, 226.9 us)
